TPU v7x, 32 devices: a whole 2x2x4 slice. The times are simulated.
32 devices in a mesh: dp: 16 (over z, x, core), tensor: 2 (over y).
Axes of the slice: x: 2, y: 2, z: 4, core: 2. Of those that a mesh axis runs over, the one named last changes fastest.
Arguments:
- tokens: bfloat16 [16384, 1024], P(('dp', 'tensor')), may hold values from -6 to 6
- norm_gain1: float32 [1024], replicated, may hold values from 0.5 to 1.5
- w_query: bfloat16 [1024, 1024], P('dp', 'tensor'), may hold values from -0.1875 to 0.1875
- w_key: bfloat16 [1024, 1024], P('dp', 'tensor'), may hold values from -0.1875 to 0.1875
- w_value: bfloat16 [1024, 2048], P('dp', 'tensor'), may hold values from -0.1875 to 0.1875
- w_gate: bfloat16 [1024, 2048], P('dp', 'tensor'), may hold values from -0.1875 to 0.1875
- w_decay: bfloat16 [1024, 8], P('dp', 'tensor'), may hold values from -0.375 to 0.375
- w_write: bfloat16 [1024, 8], P('dp', 'tensor'), may hold values from -0.375 to 0.375
- conv_query: float32 [4, 1024], P(None, 'tensor'), may hold values from -3 to 3
- conv_key: float32 [4, 1024], P(None, 'tensor'), may hold values from -3 to 3
- conv_value: float32 [4, 2048], P(None, 'tensor'), may hold values from -3 to 3
- a_log: float32 [8], P('tensor'), may hold values from -3 to 1
- dt_bias: float32 [8], P('tensor'), may hold values from -4 to -1
- out_gain: float32 [256], replicated, may hold values from 0.5 to 1.5
- w_out: bfloat16 [2048, 1024], P('tensor', 'dp'), may hold values from -0.25 to 0.25
- norm_gain2: float32 [1024], replicated, may hold values from 0.5 to 1.5
- w_ffgate: bfloat16 [1024, 2816], P('dp', 'tensor'), may hold values from -0.1875 to 0.1875
- w_ffup: bfloat16 [1024, 2816], P('dp', 'tensor'), may hold values from -0.1875 to 0.1875
- w_ffdown: bfloat16 [2816, 1024], P('tensor', 'dp'), may hold values from -0.109375 to 0.109375
- cotangent: bfloat16 [16384, 1024], P(('dp', 'tensor')), may hold values from -11 to 11, as said below
Outputs:
- result: bfloat16 [16384, 1024], P(('dp', 'tensor'))
- grad_tokens: float32 [16384, 1024], P(('dp', 'tensor'))
- grad_norm_gain1: float32 [1024], replicated
- grad_query: float32 [1024, 1024], P('dp', 'tensor')
- grad_key: float32 [1024, 1024], P('dp', 'tensor')
- grad_value: float32 [1024, 2048], P('dp', 'tensor')
- grad_gate: float32 [1024, 2048], P('dp', 'tensor')
- grad_decay: float32 [1024, 8], P('dp', 'tensor')
- grad_write: float32 [1024, 8], P('dp', 'tensor')
- grad_conv_query: float32 [4, 1024], P(None, 'tensor')
- grad_conv_key: float32 [4, 1024], P(None, 'tensor')
- grad_conv_value: float32 [4, 2048], P(None, 'tensor')
- grad_a_log: float32 [8], P('tensor')
- grad_dt_bias: float32 [8], P('tensor')
- grad_out_gain: float32 [256], replicated
- grad_out: float32 [2048, 1024], P('tensor', 'dp')
- grad_norm_gain2: float32 [1024], replicated
- grad_ffgate: float32 [1024, 2816], P('dp', 'tensor')
- grad_ffup: float32 [1024, 2816], P('dp', 'tensor')
- grad_ffdown: float32 [2816, 1024], P('tensor', 'dp')
Inputs may be any that keep to these rules, and one draw needn't show every extreme that they name: `cotangent`: gradient of the loss, of order one in every row.
All inputs are finite; a program needn't handle non-finite values.
Results may differ from a plain program's by a relative error of at most 0.012.
Values may be sent and summed in bfloat16 or wider, within the bound.
No kernel may reach another device: no remote copies, remote signals or barrier semaphores. Data moves between devices by JAX's collectives and lax.ppermute only.
A program may use at most 256 MiB of HBM per device.

v0:
```python
import math

import jax
import jax.numpy as jnp
from jax import lax
from jax.sharding import PartitionSpec as P

SPAN = 64
LEN = 512


def row_norm(values, gain):
    factor = lax.rsqrt(jnp.mean(values * values, axis=-1, keepdims=True) + 1e-05)
    return values * factor * gain


def unit_norm(vectors):
    return vectors * lax.rsqrt(jnp.sum(vectors * vectors, axis=-1, keepdims=True) + 1e-06)


def causal_conv(values, kernel):
    taps_count = kernel.shape[0]
    seq_len = values.shape[1]
    padded = jnp.pad(values, ((0, 0), (taps_count - 1, 0), (0, 0)))
    summed = padded[:, 0:seq_len, :] * kernel[0]
    for offset in range(1, taps_count):
        summed = summed + padded[:, offset : offset + seq_len, :] * kernel[offset]
    return summed


def to_blocks(tensor, seq_count, nblocks):
    heads_n = tensor.shape[2]
    return jnp.transpose(tensor.reshape(seq_count, nblocks, SPAN, heads_n, -1), (0, 3, 1, 2, 4))


def delta_rule(queries, keys_in, values_in, decay, write_rate):
    highest = lax.Precision.HIGHEST
    seq_count, seq_len, heads_n, key_dim = queries.shape
    val_dim = values_in.shape[-1]
    nblocks = seq_len // SPAN
    q_blk = to_blocks(queries, seq_count, nblocks)
    k_blk = to_blocks(keys_in, seq_count, nblocks)
    v_blk = to_blocks(values_in, seq_count, nblocks)
    g_blk = to_blocks(decay[..., None], seq_count, nblocks)[..., 0]
    b_blk = to_blocks(write_rate[..., None], seq_count, nblocks)[..., 0]
    cumul = jnp.cumsum(g_blk, axis=-1)
    positions = jnp.arange(SPAN)
    strict = positions[:, None] > positions[None, :]
    inclusive = positions[:, None] >= positions[None, :]
    cum_gaps = cumul[..., :, None] - cumul[..., None, :]
    strict_decay = jnp.where(strict, jnp.exp(jnp.where(strict, cum_gaps, 0.0)), 0.0)
    incl_decay = jnp.where(inclusive, jnp.exp(jnp.where(inclusive, cum_gaps, 0.0)), 0.0)
    key_inner = jnp.einsum("shnik,shnjk->shnij", k_blk, k_blk, precision=highest)
    system = jnp.eye(SPAN, dtype=jnp.float32) + b_blk[..., :, None] * key_inner * strict_decay
    right_side = jnp.concatenate(
        [b_blk[..., None] * v_blk, (b_blk * jnp.exp(cumul))[..., None] * k_blk], axis=-1
    )
    solved = jax.scipy.linalg.solve_triangular(system, right_side, lower=True, unit_diagonal=True)
    solved_v = solved[..., :val_dim]
    solved_k = solved[..., val_dim:]
    query_key = jnp.einsum("shnik,shnjk->shnij", q_blk, k_blk, precision=highest) * incl_decay
    query_dec = q_blk * jnp.exp(cumul)[..., None]
    key_dec = k_blk * jnp.exp(cumul[..., -1:] - cumul)[..., None]
    last_dec = jnp.exp(cumul[..., -1])

    def advance(carried, pieces):
        part_v, part_k, part_qk, part_q, part_kd, part_last = pieces
        update = part_v - jnp.einsum("shck,shkv->shcv", part_k, carried, precision=highest)
        output = jnp.einsum("shck,shkv->shcv", part_q, carried, precision=highest)
        output = output + jnp.einsum("shcj,shjv->shcv", part_qk, update, precision=highest)
        carried = part_last[..., None, None] * carried + jnp.einsum(
            "shck,shcv->shkv", part_kd, update, precision=highest
        )
        return (carried, output)

    inputs = tuple(
        (
            jnp.moveaxis(member, 2, 0)
            for member in (solved_v, solved_k, query_key, query_dec, key_dec, last_dec)
        )
    )
    initial = jnp.zeros((seq_count, heads_n, key_dim, val_dim), jnp.float32)
    unused, outputs = lax.scan(jax.checkpoint(advance), initial, inputs)
    return jnp.transpose(outputs, (1, 0, 3, 2, 4)).reshape(seq_count, seq_len, heads_n, val_dim)


def mix_heads(
    proj_q,
    proj_k,
    proj_v,
    proj_gate,
    proj_decay,
    proj_write,
    conv_q,
    conv_k,
    conv_v,
    a_log,
    dt_bias,
    out_gain,
):
    row_count = proj_q.shape[0]
    seq_count = row_count // LEN
    heads_n = proj_decay.shape[1]

    def conv_act(projected, kernel):
        convolved = causal_conv(projected.reshape(seq_count, LEN, -1), kernel)
        return jax.nn.silu(convolved).reshape(seq_count, LEN, heads_n, -1)

    queries = unit_norm(conv_act(proj_q, conv_q))
    queries = queries * (1.0 / math.sqrt(queries.shape[-1]))
    keys_in = unit_norm(conv_act(proj_k, conv_k))
    values_in = conv_act(proj_v, conv_v)
    write_rate = jax.nn.sigmoid(proj_write).reshape(seq_count, LEN, heads_n)
    decay = (-jnp.exp(a_log) * jax.nn.softplus(proj_decay + dt_bias)).reshape(
        seq_count, LEN, heads_n
    )
    mixed = delta_rule(queries, keys_in, values_in, decay, write_rate)
    normed = row_norm(mixed, out_gain)
    gated = normed * jax.nn.silu(proj_gate.reshape(seq_count, LEN, heads_n, -1))
    return gated.reshape(row_count, -1)


def swiglu(gate_val, up_val):
    return jax.nn.silu(gate_val) * up_val


def matmul(left, right):
    return jnp.dot(left, right, preferred_element_type=jnp.float32)


def rows_inner(left, right):
    return jnp.einsum("rd,rc->dc", left, right, preferred_element_type=jnp.float32)


def against_rows(left, right):
    return jnp.einsum("rc,dc->rd", left, right, preferred_element_type=jnp.float32)


def gather_mix(w_query, w_key, w_value, w_gate, w_decay, w_write, w_out):
    return (
        lax.all_gather(w_query, "dp", axis=0, tiled=True),
        lax.all_gather(w_key, "dp", axis=0, tiled=True),
        lax.all_gather(w_value, "dp", axis=0, tiled=True),
        lax.all_gather(w_gate, "dp", axis=0, tiled=True),
        lax.all_gather(w_decay, "dp", axis=0, tiled=True),
        lax.all_gather(w_write, "dp", axis=0, tiled=True),
        lax.all_gather(w_out, "dp", axis=1, tiled=True),
    )


def gather_ffn(w_ffgate, w_ffup, w_ffdown):
    return (
        lax.all_gather(w_ffgate, "dp", axis=0, tiled=True),
        lax.all_gather(w_ffup, "dp", axis=0, tiled=True),
        lax.all_gather(w_ffdown, "dp", axis=1, tiled=True),
    )


def local(
    tokens,
    norm_gain1,
    w_query,
    w_key,
    w_value,
    w_gate,
    w_decay,
    w_write,
    conv_query,
    conv_key,
    conv_value,
    a_log,
    dt_bias,
    out_gain,
    w_out,
    norm_gain2,
    w_ffgate,
    w_ffup,
    w_ffdown,
    cotangent,
):
    mix_full = gather_mix(w_query, w_key, w_value, w_gate, w_decay, w_write, w_out)
    tokens32 = tokens.astype(jnp.float32)
    norm1_out, norm1_back = jax.vjp(row_norm, tokens32, norm_gain1)
    normed1 = lax.all_gather(norm1_out.astype(jnp.bfloat16), "tensor", axis=0, tiled=True)
    projections = tuple((matmul(normed1, weight) for weight in mix_full[:6]))
    gated, mix_back = jax.vjp(
        mix_heads, *projections, conv_query, conv_key, conv_value, a_log, dt_bias, out_gain
    )
    gated_low = gated.astype(jnp.bfloat16)
    mix_part = matmul(gated_low, mix_full[6])
    resid1 = tokens32 + lax.psum_scatter(mix_part, "tensor", scatter_dimension=0, tiled=True)
    norm2_out, norm2_back = jax.vjp(row_norm, resid1, norm_gain2)
    normed2 = lax.all_gather(norm2_out.astype(jnp.bfloat16), "tensor", axis=0, tiled=True)
    ffn_full = gather_ffn(w_ffgate, w_ffup, w_ffdown)
    gate_val = matmul(normed2, ffn_full[0])
    up_val = matmul(normed2, ffn_full[1])
    hidden32, swiglu_back = jax.vjp(swiglu, gate_val, up_val)
    hidden = hidden32.astype(jnp.bfloat16)
    ffn_part = matmul(hidden, ffn_full[2])
    result = resid1 + lax.psum_scatter(
        ffn_part.astype(jnp.bfloat16), "tensor", scatter_dimension=0, tiled=True
    ).astype(jnp.float32)
    cot_full = lax.all_gather(cotangent, "tensor", axis=0, tiled=True)
    ffn_full = gather_ffn(w_ffgate, w_ffup, w_ffdown)
    grad_ffdown = rows_inner(hidden, cot_full)
    grad_hidden = against_rows(cot_full, ffn_full[2])
    grad_gate32, grad_up32 = swiglu_back(grad_hidden)
    grad_gate_low = grad_gate32.astype(jnp.bfloat16)
    grad_up_low = grad_up32.astype(jnp.bfloat16)
    grad_ffgate = rows_inner(normed2, grad_gate_low)
    grad_ffup = rows_inner(normed2, grad_up_low)
    grad_normed2 = against_rows(grad_gate_low, ffn_full[0]) + against_rows(grad_up_low, ffn_full[1])
    ffn_grads = (
        lax.psum_scatter(grad_ffgate, "dp", scatter_dimension=0, tiled=True),
        lax.psum_scatter(grad_ffup, "dp", scatter_dimension=0, tiled=True),
        lax.psum_scatter(grad_ffdown, "dp", scatter_dimension=1, tiled=True),
    )
    grad_rows2 = lax.psum_scatter(grad_normed2, "tensor", scatter_dimension=0, tiled=True)
    grad_resid_norm, grad_gain2 = norm2_back(grad_rows2)
    grad_resid = cotangent.astype(jnp.float32) + grad_resid_norm
    resid_full = lax.all_gather(grad_resid.astype(jnp.bfloat16), "tensor", axis=0, tiled=True)
    mix_full = gather_mix(w_query, w_key, w_value, w_gate, w_decay, w_write, w_out)
    grad_out = rows_inner(gated_low, resid_full)
    grad_gated = against_rows(resid_full, mix_full[6])
    mix_grads = mix_back(grad_gated)
    proj_grads = tuple((member.astype(jnp.bfloat16) for member in mix_grads[:6]))
    weight_grads = tuple((rows_inner(normed1, member) for member in proj_grads))
    grad_normed1 = against_rows(proj_grads[0], mix_full[0])
    for index_at in range(1, 6):
        grad_normed1 = grad_normed1 + against_rows(proj_grads[index_at], mix_full[index_at])
    mix_sums = (
        lax.psum_scatter(weight_grads[0], "dp", scatter_dimension=0, tiled=True),
        lax.psum_scatter(weight_grads[1], "dp", scatter_dimension=0, tiled=True),
        lax.psum_scatter(weight_grads[2], "dp", scatter_dimension=0, tiled=True),
        lax.psum_scatter(weight_grads[3], "dp", scatter_dimension=0, tiled=True),
        lax.psum_scatter(weight_grads[4], "dp", scatter_dimension=0, tiled=True),
        lax.psum_scatter(weight_grads[5], "dp", scatter_dimension=0, tiled=True),
        lax.psum_scatter(grad_out, "dp", scatter_dimension=1, tiled=True),
    )
    grad_rows1 = lax.psum_scatter(
        grad_normed1.astype(jnp.bfloat16), "tensor", scatter_dimension=0, tiled=True
    ).astype(jnp.float32)
    grad_tokens_norm, grad_gain1 = norm1_back(grad_rows1)
    grad_tokens = grad_resid + grad_tokens_norm
    small_sums = lax.psum(
        (mix_grads[6], mix_grads[7], mix_grads[8], mix_grads[9], mix_grads[10]), "dp"
    )
    gain_sums = lax.psum((grad_gain1, grad_gain2, mix_grads[11]), ("dp", "tensor"))
    return (
        result.astype(jnp.bfloat16),
        grad_tokens,
        gain_sums[0],
        mix_sums[0],
        mix_sums[1],
        mix_sums[2],
        mix_sums[3],
        mix_sums[4],
        mix_sums[5],
        small_sums[0],
        small_sums[1],
        small_sums[2],
        small_sums[3],
        small_sums[4],
        gain_sums[2],
        mix_sums[6],
        gain_sums[1],
        ffn_grads[0],
        ffn_grads[1],
        ffn_grads[2],
    )


def solution(mesh):
    placed = (
        P(("dp", "tensor"), None),
        P(),
        P("dp", "tensor"),
        P("dp", "tensor"),
        P("dp", "tensor"),
        P("dp", "tensor"),
        P("dp", "tensor"),
        P("dp", "tensor"),
        P(None, "tensor"),
        P(None, "tensor"),
        P(None, "tensor"),
        P("tensor"),
        P("tensor"),
        P(),
        P("tensor", "dp"),
        P(),
        P("dp", "tensor"),
        P("dp", "tensor"),
        P("tensor", "dp"),
        P(("dp", "tensor"), None),
    )
    return jax.shard_map(
        local,
        mesh=mesh,
        in_specs=placed,
        out_specs=(
            P(("dp", "tensor"), None),
            P(("dp", "tensor"), None),
            P(),
            P("dp", "tensor"),
            P("dp", "tensor"),
            P("dp", "tensor"),
            P("dp", "tensor"),
            P("dp", "tensor"),
            P("dp", "tensor"),
            P(None, "tensor"),
            P(None, "tensor"),
            P(None, "tensor"),
            P("tensor"),
            P("tensor"),
            P(),
            P("tensor", "dp"),
            P(),
            P("dp", "tensor"),
            P("dp", "tensor"),
            P("tensor", "dp"),
        ),
        check_vma=False,
    )
```

profile of v0, /device:TPU:0, one launch (start us, length us, event | category | flops | bytes accessed | tf_op | source)
XLA Modules:
  0.0 2138.1 jit_solution(9729380152259318161)
XLA Ops:
  15.9 23.1 %all-gather = bf16[16,64,4]{1,2,0:T(4,128)(2,1)S(1)} all-gather(bf16[1,64,4]{1,2,0:T(4,128)(2,1)S(1)} %bitcast.525), channel_id=1, replica_groups=mesh['dp'=16,'tensor'=2] {'dp'}, dimensions={0}, use_global_device_ids=true | all-gather | bytes 8704 | tf_op jit(solution)/shard_map/all_gather | solution.py:145
  39.2 17.5 all-gather.1
  57.1 28.0 %all-gather.15.cloned.1.call-done = bf16[1024,1024]{1,0:T(8,128)(2,1)} async-done(((bf16[512,1024]{1,0:T(8,128)(2,1)}), bf16[1024,1024]{1,0:T(8,128)(2,1)}) %all-gather.15.cloned.1.call-update) | async-done | bytes 2097168 | tf_op jit(solution)/shard_map/all_gather | solution.py:184
  104.5 20.7 all-gather.21.cloned.1.call-done
  151.3 316.0 %custom-call.10 = f32[2,4,8,1,64,64]{4,5,3,2,1,0:T(8,128)} custom-call(f32[2,4,8,1,64,64]{5,4,3,2,1,0:T(8,128)} %fusion.64), custom_call_target="InvertDiagBlocksLowerTriangular" | custom-call | tf_op jit(solution)/shard_map/jvp(jit(_solve_triangular))/vmap(vmap(vmap()))/triangular_solve | solution.py:58
  521.2 73.4 %while.42 = (s32[]{:T(128)}, f32[2,4,128,256]{3,2,1,0:T(8,128)S(1)}, f32[8,2,4,64,256]{4,3,2,1,0:T(8,128)}, f32[8,2,4,128,256]{4,3,2,1,0:T(8,128)}, f32[8,2,4]{2...) while((s32[]{:T(128)}, ...), condition=%wide.region_5.6_spmd.clone, body=%wide.region_4.5_spmd.clone.sunk | while | flops 706478080 | bytes 11013862 | solution.py:83
  608.8 9.5 multiply_convert_fusion.2
  625.7 52.7 %reduce-scatter.19.cloned.1.call-done = f32[512,1024]{1,0:T(8,128)} async-done(((f32[1024,1024]{1,0:T(8,128)}), f32[512,1024]{1,0:T(8,128)}) %reduce-scatter.19.cloned.1.call-update) | async-done | bytes 2097168 | tf_op jit(solution)/shard_map/reduce_scatter | solution.py:191
  684.0 40.7 %all-gather.29.cloned.1.call-done = bf16[1024,1408]{1,0:T(8,128)(2,1)} async-done(((bf16[64,1408]{1,0:T(8,128)(2,1)}), bf16[1024,1408]{1,0:T(8,128)(2,1)}) %all-gather.29.cloned.1.call-update) | async-done | bytes 2883600 | tf_op jit(solution)/shard_map/all_gather | solution.py:153
  724.7 33.9 %all-gather.27.cloned.1.call-done = bf16[1024,1024]{1,0:T(8,128)(2,1)} async-done(((bf16[512,1024]{1,0:T(8,128)(2,1)}), bf16[1024,1024]{1,0:T(8,128)(2,1)}) %all-gather.27.cloned.1.call-update) | async-done | bytes 2097168 | tf_op jit(solution)/shard_map/all_gather | solution.py:193
  766.8 37.8 %all-gather.31.cloned.1.call-done = bf16[1024,1408]{1,0:T(8,128)(2,1)} async-done(((bf16[64,1408]{1,0:T(8,128)(2,1)}), bf16[1024,1408]{1,0:T(8,128)(2,1)}) %all-gather.31.cloned.1.call-update) | async-done | bytes 2883600 | tf_op jit(solution)/shard_map/all_gather | solution.py:154
  813.0 24.9 %all-gather.35.cloned.1.call-done = bf16[1024,1024]{1,0:T(8,128)(2,1)} async-done(((bf16[512,1024]{1,0:T(8,128)(2,1)}), bf16[1024,1024]{1,0:T(8,128)(2,1)}) %all-gather.35.cloned.1.call-update) | async-done | bytes 2097168 | tf_op jit(solution)/shard_map/all_gather | solution.py:203
  838.0 46.1 %all-gather.33.cloned.1.call-done = bf16[1408,1024]{0,1:T(8,128)(2,1)} async-done(((bf16[1408,64]{0,1:T(8,128)(2,1)}), bf16[1408,1024]{0,1:T(8,128)(2,1)}) %all-gather.33.cloned.1.call-update) | async-done | bytes 2883600 | tf_op jit(solution)/shard_map/all_gather | solution.py:155
  884.1 11.2 multiply_convert_fusion
  904.3 53.1 %reduce-scatter.23.cloned.1.call-done = f32[512,1024]{1,0:T(8,128)} async-done(((f32[1024,1024]{1,0:T(8,128)}), f32[512,1024]{1,0:T(8,128)}) %reduce-scatter.23.cloned.1.call-update) | async-done | bytes 2097168 | tf_op jit(solution)/shard_map/reduce_scatter | solution.py:218
  972.4 22.8 %all-gather.37.cloned.1.call-done = bf16[1024,1024]{1,0:T(8,128)(2,1)} async-done(((bf16[512,1024]{1,0:T(8,128)(2,1)}), bf16[1024,1024]{1,0:T(8,128)(2,1)}) %all-gather.37.cloned.1.call-update) | async-done | bytes 2097168 | tf_op jit(solution)/shard_map/all_gather | solution.py:221
  995.2 10.1 fusion.48
  1030.0 157.9 %while.43 = (s32[]{:T(128)}, f32[2,4,128,256]{3,2,1,0:T(8,128)S(1)}, f32[8,2,4,64,256]{4,3,2,1,0:T(8,128)}, f32[8,2,4,64,128]{4,3,2,1,0:T(8,128)}, f32[8,2,4,64,...) while((s32[]{:T(128)}, ...), condition=%wide.region_15.16_spmd.clone, body=%wide.region_13.15_spmd.clone.sunk | while | flops 1612709888 | bytes 32115144 | solution.py:83
  1187.8 8.4 fusion.37
  1196.4 13.1 fusion.35
  1371.5 8.4 fusion.190
  1380.0 8.4 fusion.191
  1423.2 61.7 %all-reduce.32 = (f32[4,512]{1,0:T(4,128)}, f32[4,512]{1,0:T(4,128)}, f32[4,1024]{1,0:T(4,128)}, f32[4]{0:T(128)}, f32[4]{0:T(128)}) all-reduce(f32[4,512]{1,0:T(4,128)S(1)} %pad_add_fusion.12, f32[4,512]{1,0:T(4,128)S(1)} %pad_add_fusion.11, f32[4,1024]{1,0:T(4,128)S(1)} %pad_add_fusion.10, ...), channel_id=1, replica_groups=mesh['dp'=16,'tensor'=2] {'dp'}, use_global_device_ids=true, to_apply=%region_41.42 | all-reduce | flops 8200 | bytes 65600 | tf_op jit(solution)/shard_map/psum | solution.py:245
  1489.9 37.8 %all-reduce.31 = (f32[1024]{0:T(1024)}, f32[256]{0:T(256)}, f32[1024]{0:T(1024)}) all-reduce(f32[1024]{0:T(1024)S(1)} %get-tuple-element.596, f32[256]{0:T(256)S(1)} %copy-done.129, f32[1024]{0:T(1024)S(1)} %copy-done.123), channel_id=1, replica_groups=mesh['dp'=16,'tensor'=2] {'dp','tensor'}, use_global_device_ids=true, to_apply=%region_30.31 | all-reduce | flops 2304 | bytes 18432 | tf_op jit(solution)/shard_map/psum | solution.py:248
  1532.5 69.8 %reduce-scatter.37.cloned.1.call-done = f32[64,1408]{1,0:T(8,128)} async-done(((f32[1024,1408]{1,0:T(8,128)}), f32[64,1408]{1,0:T(8,128)}) %reduce-scatter.37.cloned.1.call-update) | async-done | bytes 360464 | tf_op jit(solution)/shard_map/reduce_scatter | solution.py:214
  1602.3 85.0 %reduce-scatter.39.cloned.1.call-done = f32[64,1408]{1,0:T(8,128)} async-done(((f32[1024,1408]{1,0:T(8,128)}), f32[64,1408]{1,0:T(8,128)}) %reduce-scatter.39.cloned.1.call-update) | async-done | bytes 360464 | tf_op jit(solution)/shard_map/reduce_scatter | solution.py:215
  1687.2 85.1 %reduce-scatter.41.cloned.1.call-done = f32[1408,64]{0,1:T(8,128)} async-done(((f32[1408,1024]{0,1:T(8,128)}), f32[1408,64]{0,1:T(8,128)}) %reduce-scatter.41.cloned.1.call-update) | async-done | bytes 360464 | tf_op jit(solution)/shard_map/reduce_scatter | solution.py:216
  1772.4 65.4 %reduce-scatter.29.cloned.1.call-done = f32[64,512]{1,0:T(8,128)} async-done(((f32[1024,512]{1,0:T(8,128)}), f32[64,512]{1,0:T(8,128)}) %reduce-scatter.29.cloned.1.call-update) | async-done | bytes 131088 | tf_op jit(solution)/shard_map/reduce_scatter | solution.py:233
  1837.7 65.1 %reduce-scatter.27.cloned.1.call-done = f32[64,512]{1,0:T(8,128)} async-done(((f32[1024,512]{1,0:T(8,128)}), f32[64,512]{1,0:T(8,128)}) %reduce-scatter.27.cloned.1.call-update) | async-done | bytes 131088 | tf_op jit(solution)/shard_map/reduce_scatter | solution.py:232
  1902.8 76.0 %reduce-scatter.35.cloned.1.call-done = f32[1024,64]{0,1:T(8,128)} async-done(((f32[1024,1024]{0,1:T(8,128)}), f32[1024,64]{0,1:T(8,128)}) %reduce-scatter.35.cloned.1.call-update) | async-done | bytes 262160 | tf_op jit(solution)/shard_map/reduce_scatter | solution.py:238
  1978.8 76.4 %reduce-scatter.31.cloned.1.call-done = f32[64,1024]{1,0:T(8,128)} async-done(((f32[1024,1024]{1,0:T(8,128)}), f32[64,1024]{1,0:T(8,128)}) %reduce-scatter.31.cloned.1.call-update) | async-done | bytes 262160 | tf_op jit(solution)/shard_map/reduce_scatter | solution.py:234
  2055.3 76.1 %reduce-scatter.33.cloned.1.call-done = f32[64,1024]{1,0:T(8,128)} async-done(((f32[1024,1024]{1,0:T(8,128)}), f32[64,1024]{1,0:T(8,128)}) %reduce-scatter.33.cloned.1.call-update) | async-done | bytes 262160 | tf_op jit(solution)/shard_map/reduce_scatter | solution.py:235
  (762 shorter events, 635.6 us)
Async XLA Ops:
  7.2 49.9 %all-gather.17.cloned.1.call-start = ((), (), s32[]{:S(2)}) async-start(), calls=%async_computation.15 | async-start | bytes 1114112 | tf_op jit(solution)/shard_map/all_gather | solution.py:142
  7.9 77.1 %all-gather.15.cloned.1.call-start = ((), (), s32[]{:S(2)}) async-start(), calls=%async_computation.14 | async-start | bytes 3145728 | tf_op jit(solution)/shard_map/all_gather | solution.py:184
  13.2 111.9 %all-gather.21.cloned.1.call-start = ((), (), s32[]{:S(2)}) async-start(), calls=%async_computation.17 | async-start | bytes 1114112 | tf_op jit(solution)/shard_map/all_gather | solution.py:141
  14.0 474.1 %all-gather.19.cloned.1.call-start = ((), (), s32[]{:S(2)}) async-start(), calls=%async_computation.16 | async-start | bytes 2228224 | tf_op jit(solution)/shard_map/all_gather | solution.py:143
  14.6 594.2 %all-gather.23.cloned.1.call-start = ((), (), s32[]{:S(2)}) async-start(), calls=%async_computation.18 | async-start | bytes 2228224 | tf_op jit(solution)/shard_map/all_gather | solution.py:144
  15.1 603.1 %all-gather.25.cloned.1.call-start = ((), (), s32[]{:S(2)}) async-start(), calls=%async_computation.19 | async-start | bytes 2228224 | tf_op jit(solution)/shard_map/all_gather | solution.py:147
  15.7 662.6 %reduce-scatter.19.cloned.1.call-start = ((), (), s32[]{:S(2)}) async-start(), calls=%async_computation.20 | async-start | bytes 6291456 | tf_op jit(solution)/shard_map/reduce_scatter | solution.py:191
  15.8 464.9 %copy-start.73 = (pred[64,64]{1,0:T(8,128)(4,1)}, pred[64,64]{1,0:T(8,128)(4,1)S(1)}, u32[]{:S(2)}) copy-start(pred[64,64]{1,0:T(8,128)(4,1)S(1)} %iota_compare_fusion) | copy-start | bytes 12292
  56.9 435.8 %copy-start.89 = (f32[1,1024]{1,0:T(1,128)}, f32[1,1024]{1,0:T(1,128)S(1)}, u32[]{:S(2)}) copy-start(f32[1,1024]{1,0:T(1,128)S(1)} %get-tuple-element.709) | copy-start | bytes 12292
  56.9 435.8 %copy-start.91 = (f32[1,1024]{1,0:T(1,128)}, f32[1,1024]{1,0:T(1,128)S(1)}, u32[]{:S(2)}) copy-start(f32[1,1024]{1,0:T(1,128)S(1)} %get-tuple-element.710) | copy-start | bytes 12292
  56.9 435.8 %copy-start.93 = (f32[1,1024]{1,0:T(1,128)}, f32[1,1024]{1,0:T(1,128)S(1)}, u32[]{:S(2)}) copy-start(f32[1,1024]{1,0:T(1,128)S(1)} %get-tuple-element.711) | copy-start | bytes 12292
  56.9 435.8 %copy-start.95 = (f32[1,1024]{1,0:T(1,128)}, f32[1,1024]{1,0:T(1,128)S(1)}, u32[]{:S(2)}) copy-start(f32[1,1024]{1,0:T(1,128)S(1)} %get-tuple-element.712) | copy-start | bytes 12292
  102.5 400.5 %copy-start.67 = (f32[2,8,64,4,1]{2,1,3,0,4:T(8,128)}, f32[2,8,64,4,1]{2,1,3,0,4:T(8,128)S(1)}, u32[]{:S(2)}) copy-start(f32[2,8,64,4,1]{2,1,3,0,4:T(8,128)S(1)} %copy.347) | copy-start | bytes 49156
  624.8 99.8 %all-gather.29.cloned.1.call-start = ((), (), s32[]{:S(2)}) async-start(), calls=%async_computation.22 | async-start | bytes 3063808 | tf_op jit(solution)/shard_map/all_gather | solution.py:153
  625.6 132.9 %all-gather.27.cloned.1.call-start = ((), (), s32[]{:S(2)}) async-start(), calls=%async_computation.21 | async-start | bytes 3145728 | tf_op jit(solution)/shard_map/all_gather | solution.py:193
  681.8 122.8 %all-gather.31.cloned.1.call-start = ((), (), s32[]{:S(2)}) async-start(), calls=%async_computation.23 | async-start | bytes 3063808 | tf_op jit(solution)/shard_map/all_gather | solution.py:154
  682.4 155.6 %all-gather.35.cloned.1.call-start = ((), (), s32[]{:S(2)}) async-start(), calls=%async_computation.26 | async-start | bytes 3145728 | tf_op jit(solution)/shard_map/all_gather | solution.py:203
  683.1 201.0 %all-gather.33.cloned.1.call-start = ((), (), s32[]{:S(2)}) async-start(), calls=%async_computation.24 | async-start | bytes 3063808 | tf_op jit(solution)/shard_map/all_gather | solution.py:155
  683.7 273.7 %reduce-scatter.23.cloned.1.call-start = ((), (), s32[]{:S(2)}) async-start(), calls=%async_computation.27 | async-start | bytes 6291456 | tf_op jit(solution)/shard_map/reduce_scatter | solution.py:218
  904.3 90.9 %all-gather.37.cloned.1.call-start = ((), (), s32[]{:S(2)}) async-start(), calls=%async_computation.28 | async-start | bytes 3145728 | tf_op jit(solution)/shard_map/all_gather | solution.py:221
  962.0 523.0 %reduce-scatter.45.cloned.1.call-start = ((), (), s32[]{:S(2)}) async-start(), calls=%async_computation.39 | async-start | bytes 557056
  1333.3 153.1 %reduce-scatter.43.cloned.1.call-start = ((), (), s32[]{:S(2)}) async-start(), calls=%async_computation.38 | async-start | bytes 557056
  1334.9 152.8 %reduce-scatter.25.cloned.1.call-start = ((), (), s32[]{:S(2)}) async-start(), calls=%async_computation.29 | async-start | bytes 3145728 | tf_op jit(solution)/shard_map/reduce_scatter | solution.py:240
  1363.7 164.1 %reduce-scatter.21.cloned.1.call-start = ((), (), s32[]{:S(2)}) async-start(), calls=%async_computation.25 | async-start | bytes 3145728 | tf_op jit(solution)/shard_map/reduce_scatter | solution.py:200
  1371.5 230.8 %reduce-scatter.37.cloned.1.call-start = ((), (), s32[]{:S(2)}) async-start(), calls=%async_computation.35 | async-start | bytes 6127616 | tf_op jit(solution)/shard_map/reduce_scatter | solution.py:214
  1380.0 307.3 %reduce-scatter.39.cloned.1.call-start = ((), (), s32[]{:S(2)}) async-start(), calls=%async_computation.36 | async-start | bytes 6127616 | tf_op jit(solution)/shard_map/reduce_scatter | solution.py:215
  1388.4 383.9 %reduce-scatter.41.cloned.1.call-start = ((), (), s32[]{:S(2)}) async-start(), calls=%async_computation.37 | async-start | bytes 6127616 | tf_op jit(solution)/shard_map/reduce_scatter | solution.py:216
  1396.9 440.9 %reduce-scatter.29.cloned.1.call-start = ((), (), s32[]{:S(2)}) async-start(), calls=%async_computation.31 | async-start | bytes 2228224 | tf_op jit(solution)/shard_map/reduce_scatter | solution.py:233
  1401.0 501.8 %reduce-scatter.27.cloned.1.call-start = ((), (), s32[]{:S(2)}) async-start(), calls=%async_computation.30 | async-start | bytes 2228224 | tf_op jit(solution)/shard_map/reduce_scatter | solution.py:232
  1403.7 575.2 %reduce-scatter.35.cloned.1.call-start = ((), (), s32[]{:S(2)}) async-start(), calls=%async_computation.34 | async-start | bytes 4456448 | tf_op jit(solution)/shard_map/reduce_scatter | solution.py:238
  1410.4 644.9 %reduce-scatter.31.cloned.1.call-start = ((), (), s32[]{:S(2)}) async-start(), calls=%async_computation.32 | async-start | bytes 4456448 | tf_op jit(solution)/shard_map/reduce_scatter | solution.py:234
  1416.5 714.9 %reduce-scatter.33.cloned.1.call-start = ((), (), s32[]{:S(2)}) async-start(), calls=%async_computation.33 | async-start | bytes 4456448 | tf_op jit(solution)/shard_map/reduce_scatter | solution.py:235
  (161 other events, 5189.0 us)
Sparse Core Ops, SparseCore 0:
  10.2 40.5 all-gather.16
  52.9 32.1 all-gather.14
  87.2 37.8 all-gather.20
  127.1 40.3 all-gather.18
  169.5 41.3 all-gather.22
  212.9 40.9 all-gather.24
  625.0 53.3 reduce-scatter.18
  680.7 43.9 all-gather.28
  726.8 31.7 all-gather.26
  760.7 43.9 all-gather.30
  806.2 31.7 all-gather.34
  840.1 43.9 all-gather.32
  904.4 52.9 reduce-scatter.22
  962.1 33.0 all-gather.36
  1333.4 56.1 reduce-scatter.44
  1393.0 55.1 reduce-scatter.42
  1450.9 30.9 reduce-scatter.24
  1484.0 32.5 reduce-scatter.20
  1521.1 81.1 reduce-scatter.36
  1606.6 80.6 reduce-scatter.38
  1691.7 80.6 reduce-scatter.40
  1776.7 61.0 reduce-scatter.28
  1842.1 60.7 reduce-scatter.26
  1907.1 71.6 reduce-scatter.34
  1983.3 71.9 reduce-scatter.30
  2059.6 71.7 reduce-scatter.32
where the time goes:
time: 2150 us; the launch traced here: 2140 us
  waiting for transfers between devices  965 us (45%)
  other arithmetic  446 us (21%)
  matrix products  387 us (18%)
  local copies, waits for them, and re-layouts  179 us (8%)
  blocking collectives  140 us (7%)
    another operation x5, other arithmetic, delta_rule(): jax.scipy.linalg.solve_triangular(system, right_side, lower=True, unit_di...  318 us
    reduce_scatter x1, waiting for transfers between devices, local(): lax.psum_scatter(grad_ffdown, 'dp', scatter_dimension=1, tiled=True)  85.1 us
    reduce_scatter x1, waiting for transfers between devices, local(): lax.psum_scatter(grad_ffup, 'dp', scatter_dimension=0, tiled=True)  85 us
    reduce_scatter x1, waiting for transfers between devices, local(): lax.psum_scatter(weight_grads[2], 'dp', scatter_dimension=0, tiled=True)  76.4 us
    reduce_scatter x1, waiting for transfers between devices, local(): lax.psum_scatter(weight_grads[3], 'dp', scatter_dimension=0, tiled=True)  76.1 us
    reduce_scatter x1, waiting for transfers between devices, local(): lax.psum_scatter(grad_out, 'dp', scatter_dimension=1, tiled=True)  76 us
    reduce_scatter x1, waiting for transfers between devices, local(): lax.psum_scatter(grad_ffgate, 'dp', scatter_dimension=0, tiled=True)  69.8 us
    reduce_scatter x1, waiting for transfers between devices, local(): lax.psum_scatter(weight_grads[1], 'dp', scatter_dimension=0, tiled=True)  65.4 us
  transfers between devices with their start and end apart: 26, of which 18 were waited for; matrix products, arithmetic and copies ran while one was open for 30% of the time, Pallas kernels for 0%

commit v1 on v0

v1 whole, which is shorter than its diff:
```python
import math, functools
import jax, jax.numpy as jnp
from jax import lax
from jax.experimental import pallas as pl
from jax.experimental.pallas import tpu as pltpu
from jax.sharding import PartitionSpec as P

F32 = jnp.float32
BF16 = jnp.bfloat16
LEN = 512
DK = 128
DV = 256
CHUNK = 128
PARTS = LEN // CHUNK


def dot_nn(a, b):
    return lax.dot_general(a, b, (((1,), (0,)), ((), ())), preferred_element_type=F32)


def dot_nt(a, b):
    return lax.dot_general(a, b, (((1,), (1,)), ((), ())), preferred_element_type=F32)


def dot_tn(a, b):
    return lax.dot_general(a, b, (((0,), (0,)), ((), ())), preferred_element_type=F32)


def sigmoid(x):
    return 1.0 / (1.0 + jnp.exp(-x))


def softplus(x):
    return jnp.maximum(x, 0.0) + jnp.log1p(jnp.exp(-jnp.abs(x)))


def split3(x):
    first = x.astype(BF16)
    rest = x - first.astype(F32)
    second = rest.astype(BF16)
    third = (rest - second.astype(F32)).astype(BF16)
    return first, second, third


def exact_sum(ones, x, pieces):
    parts = split3(x)[:pieces]
    total = dot_nn(ones, parts[0])
    for part in parts[1:]:
        total = total + dot_nn(ones, part)
    return total


def iota2(rows, cols, axis):
    return lax.broadcasted_iota(jnp.int32, (rows, cols), axis)


def same_group(size):
    shift = size.bit_length() - 1
    return (iota2(CHUNK, CHUNK, 0) >> shift) == (iota2(CHUNK, CHUNK, 1) >> shift)


def invert_all(lowers):
    row, col = iota2(CHUNK, CHUNK, 0), iota2(CHUNK, CHUNK, 1)
    eye = jnp.where(row == col, 1.0, 0.0)
    in8 = same_group(8)
    base = [jnp.where(in8, lower, 0.0) for lower in lowers]
    base_low = [member.astype(BF16) for member in base]
    second = [dot_nn(member, member) for member in base_low]
    second_low = [member.astype(BF16) for member in second]
    third = [dot_nn(a, b) for a, b in zip(base_low, second_low)]
    fourth = [dot_nn(member, member).astype(BF16) for member in second_low]
    start = [eye - a + b - c for a, b, c in zip(base, second, third)]
    inverse = [a + dot_nn(a.astype(BF16), b) for a, b in zip(start, fourth)]
    size = 8
    while size < CHUNK:
        ring = same_group(2 * size) & jnp.logical_not(same_group(size))
        between = [jnp.where(ring, lower, 0.0).astype(BF16) for lower in lowers]
        low = [member.astype(BF16) for member in inverse]
        inner = [dot_nn(a, b).astype(BF16) for a, b in zip(between, low)]
        inverse = [a - dot_nn(b, c) for a, b, c in zip(inverse, low, inner)]
        size *= 2
    return [member.astype(BF16) for member in inverse]


def window(ref, part, halo=8):
    body = ref[pl.ds(part * CHUNK, CHUNK), :].astype(F32)
    if part == 0:
        head = jnp.zeros((halo, body.shape[1]), F32)
    else:
        head = ref[pl.ds(part * CHUNK - halo, halo), :].astype(F32)
    return jnp.concatenate([head, body], axis=0)


def shifted(rows, tap):
    return rows[5 + tap : 5 + tap + CHUNK, :]


def convolve(rows, taps):
    total = shifted(rows, 0) * taps[0:1, :]
    for tap in range(1, 4):
        total = total + shifted(rows, tap) * taps[tap : tap + 1, :]
    return total


def pick(rows, lane):
    cols = lax.broadcasted_iota(jnp.int32, rows.shape, 1)
    return jnp.sum(jnp.where(cols == lane, rows, 0.0), axis=1, keepdims=True)


def chunk_rates(ab_ref, heads_ref, part, head, heads_n):
    rows = ab_ref[pl.ds(part * CHUNK, CHUNK), :].astype(F32)
    decay_in = pick(rows, head) + pick(heads_ref[1:2, :], head)
    write = sigmoid(pick(rows, heads_n + head))
    rate = -jnp.exp(pick(heads_ref[0:1, :], head))
    soft = softplus(decay_in)
    decay = jnp.broadcast_to(rate * soft, (CHUNK, CHUNK))
    lower = (iota2(CHUNK, CHUNK, 0) >= iota2(CHUNK, CHUNK, 1)).astype(F32).astype(BF16)
    total = exact_sum(lower, decay, 3)
    return write, total, decay_in, rate, soft


def chunk_core(q_ref, k_ref, v_ref, ab_ref, heads_ref, cq, ck, cv, part, head, heads_n):
    row, col = iota2(CHUNK, CHUNK, 0), iota2(CHUNK, CHUNK, 1)
    strict, inclusive = row > col, row >= col
    out = {}
    write, total, decay_in, rate, soft = chunk_rates(ab_ref, heads_ref, part, head, heads_n)
    out.update(write=write, decay_in=decay_in, rate=rate, soft=soft)
    rows_q, rows_k, rows_v = window(q_ref, part), window(k_ref, part), window(v_ref, part)
    xq, xk, xv = convolve(rows_q, cq), convolve(rows_k, ck), convolve(rows_v, cv)
    gq, gk, gv = sigmoid(xq), sigmoid(xk), sigmoid(xv)
    sq, sk, values = xq * gq, xk * gk, xv * gv
    rq = lax.rsqrt(jnp.sum(sq * sq, axis=1, keepdims=True) + 1e-06)
    rk = lax.rsqrt(jnp.sum(sk * sk, axis=1, keepdims=True) + 1e-06)
    queries = sq * rq * (1.0 / math.sqrt(DK))
    keys = sk * rk
    q_low, k_low = queries.astype(BF16), keys.astype(BF16)
    gaps = jnp.minimum(total - total.T, 0.0)
    fade = jnp.where(inclusive, jnp.exp(gaps), 0.0)
    fade_strict = jnp.where(strict, fade, 0.0)
    key_inner = dot_nt(k_low, k_low)
    scores = dot_nt(q_low, k_low) * fade
    from_start = jnp.exp(total)
    to_end = jnp.exp(total[CHUNK - 1 : CHUNK, :] - total)
    last = jnp.exp(total[CHUNK - 1 : CHUNK, 0:1])
    lower = write * key_inner * fade_strict
    out.update(rows_q=rows_q, rows_k=rows_k, rows_v=rows_v, xq=xq, xk=xk, xv=xv, gq=gq, gk=gk, gv=gv)
    out.update(rq=rq, rk=rk, queries=queries, keys=keys, values=values, q_low=q_low, k_low=k_low)
    out.update(fade=fade, fade_strict=fade_strict, key_inner=key_inner, scores=scores, lower=lower)
    out.update(from_start=from_start, to_end=to_end, last=last)
    out.update(key_start=(write * from_start) * keys, q_start=queries * from_start, key_end=keys * to_end)
    return out


def forward_kernel(heads_n, q_ref, k_ref, v_ref, g_ref, ab_ref, cq_ref, ck_ref, cv_ref, heads_ref, gain_ref,
                   gated_ref, mixed_ref, delta_ref, solve_ref, state_ref):
    head = pl.program_id(1)
    cq, ck, cv, gain = cq_ref[...], ck_ref[...], cv_ref[...], gain_ref[0:1, :]
    cores = [
        chunk_core(q_ref, k_ref, v_ref, ab_ref, heads_ref, cq, ck, cv, part, head, heads_n)
        for part in range(PARTS)
    ]
    solves = invert_all([core["lower"] for core in cores])
    for part in range(PARTS):
        solve_ref[0, 0, part] = solves[part]
    value_parts = [dot_nn(t, (c["write"] * c["values"]).astype(BF16)) for t, c in zip(solves, cores)]
    key_parts = [dot_nn(t, c["key_start"].astype(BF16)).astype(BF16) for t, c in zip(solves, cores)]
    state = jnp.zeros((DK, DV), F32)
    for part in range(PARTS):
        core = cores[part]
        state_low = state.astype(BF16)
        state_ref[0, 0, part] = state_low
        update = value_parts[part] - dot_nn(key_parts[part], state_low)
        update_low = update.astype(BF16)
        mixed = dot_nn(core["q_start"].astype(BF16), state_low) + dot_nn(core["scores"].astype(BF16), update_low)
        if part < PARTS - 1:
            state = core["last"] * state + dot_tn(core["key_end"].astype(BF16), update_low)
        span = pl.ds(part * CHUNK, CHUNK)
        delta_ref[span, :] = update_low
        mixed_ref[span, :] = mixed.astype(BF16)
        factor = lax.rsqrt(jnp.mean(mixed * mixed, axis=1, keepdims=True) + 1e-05)
        gate_in = g_ref[span, :].astype(F32)
        gated_ref[span, :] = (mixed * factor * gain * (gate_in * sigmoid(gate_in))).astype(BF16)


def backward_kernel(heads_n, q_ref, k_ref, v_ref, g_ref, ab_ref, cq_ref, ck_ref, cv_ref, heads_ref, gain_ref,
                    grad_ref, mixed_ref, delta_ref, solve_ref, state_ref, dp_ref, small_ref, ab_acc):
    head = pl.program_id(1)
    row, col = iota2(CHUNK, CHUNK, 0), iota2(CHUNK, CHUNK, 1)
    strict = row > col
    upper_ones = (row <= col).astype(F32).astype(BF16)
    cq, ck, cv, gain = cq_ref[...], ck_ref[...], cv_ref[...], gain_ref[0:1, :]
    width_k, width_v = heads_n * DK, heads_n * DV
    scale = 1.0 / math.sqrt(DK)

    def fold(x):
        return jnp.sum(x.reshape(CHUNK // 8, 8, x.shape[1]), axis=0)

    state_grad = jnp.zeros((DK, DV), F32)
    gain_sum = jnp.zeros((8, DV), F32)
    taps_sum = {name: [jnp.zeros((8, size), F32) for _ in range(4)] for name, size in (("q", DK), ("k", DK), ("v", DV))}
    heads_next = {"q": jnp.zeros((8, DK), F32), "k": jnp.zeros((8, DK), F32), "v": jnp.zeros((8, DV), F32)}
    rate_sum = jnp.zeros((8, CHUNK), F32)
    bias_sum = jnp.zeros((8, CHUNK), F32)
    for part in reversed(range(PARTS)):
        core = chunk_core(q_ref, k_ref, v_ref, ab_ref, heads_ref, cq, ck, cv, part, head, heads_n)
        span = pl.ds(part * CHUNK, CHUNK)
        write, keys, queries, values = core["write"], core["keys"], core["queries"], core["values"]
        k_low, q_low, fade = core["k_low"], core["q_low"], core["fade"]
        solve, state_low, delta = solve_ref[0, 0, part], state_ref[0, 0, part], delta_ref[span, :]
        mixed = mixed_ref[span, :].astype(F32)
        factor = lax.rsqrt(jnp.mean(mixed * mixed, axis=1, keepdims=True) + 1e-05)
        normed = mixed * factor
        gate_in = g_ref[span, :].astype(F32)
        gate_sig = sigmoid(gate_in)
        gate = gate_in * gate_sig
        grad = grad_ref[span, :].astype(F32)
        plain = grad * normed
        gain_sum = gain_sum + fold(plain * gate)
        dp_ref[span, pl.ds(pl.multiple_of(2 * width_k + width_v + head * DV, DV), DV)] = (
            plain * gain * (gate_sig + gate * (1.0 - gate_sig))
        ).astype(BF16)
        normed_grad = grad * gate * gain
        mixed_grad = factor * (normed_grad - normed * jnp.mean(normed_grad * normed, axis=1, keepdims=True))
        mixed_low = mixed_grad.astype(BF16)
        key_part = dot_nn(solve, core["key_start"].astype(BF16)).astype(BF16)
        grad_low = state_grad.astype(BF16)
        update_grad = dot_tn(core["scores"].astype(BF16), mixed_low) + dot_nn(core["key_end"].astype(BF16), grad_low)
        update_low = update_grad.astype(BF16)
        key_end_grad = dot_nt(delta, grad_low)
        last_grad = jnp.sum(state_low.astype(F32) * state_grad)
        if part > 0:
            state_grad = (
                core["last"] * state_grad
                + dot_tn(core["q_start"].astype(BF16), mixed_low)
                - dot_tn(key_part, update_low)
            )
        q_start_grad = dot_nt(mixed_low, state_low)
        scores_grad = dot_nt(mixed_low, delta)
        right_grad = dot_tn(solve, update_low)
        right_low = right_grad.astype(BF16)
        lower_grad = jnp.where(strict, -dot_nt(right_low, delta), 0.0)
        key_start_grad = -dot_nt(right_low, state_low)
        inner_low = (scores_grad * fade).astype(BF16)
        queries_grad = q_start_grad * core["from_start"] + dot_nn(inner_low, k_low)
        faded_lower = lower_grad * core["fade_strict"]
        key_inner_grad = write * faded_lower
        both = (key_inner_grad + key_inner_grad.T).astype(BF16)
        keys_grad = (
            key_end_grad * core["to_end"]
            + key_start_grad * (write * core["from_start"])
            + dot_tn(inner_low, q_low)
            + dot_nn(both, k_low)
        )
        values_grad = write * right_grad
        start_keys = key_start_grad * core["from_start"] * keys
        write_grad = (
            jnp.sum(right_grad * values, axis=1, keepdims=True)
            + jnp.sum(start_keys + faded_lower * core["key_inner"], axis=1, keepdims=True)
        )
        ends = key_end_grad * core["key_end"]
        gaps_grad = scores_grad * core["scores"] + lower_grad * core["lower"]
        total_grad = jnp.sum(
            q_start_grad * core["q_start"] + write * start_keys - ends + gaps_grad - gaps_grad.T, axis=1, keepdims=True
        )
        at_end = jnp.sum(ends) + last_grad * core["last"]
        decay_grad = exact_sum(upper_ones, jnp.broadcast_to(total_grad, (CHUNK, CHUNK)), 2) + at_end
        rate_sum = rate_sum + fold(decay_grad * (core["rate"] * core["soft"]))
        decay_in_grad = decay_grad * (core["rate"] * sigmoid(core["decay_in"]))
        bias_sum = bias_sum + fold(decay_in_grad)
        write_in_grad = write_grad * (write * (1.0 - write))
        entry = jnp.where(col == head, decay_in_grad, 0.0) + jnp.where(col == heads_n + head, write_in_grad, 0.0)

        @pl.when(head == 0)
        def _():
            ab_acc[span, :] = entry

        @pl.when(head > 0)
        def _():
            ab_acc[span, :] = ab_acc[span, :] + entry

        unit_grad = queries_grad * scale
        unit = queries * (1.0 / scale)
        sq_grad = core["rq"] * (unit_grad - unit * jnp.sum(unit_grad * unit, axis=1, keepdims=True))
        sk_grad = core["rk"] * (keys_grad - keys * jnp.sum(keys_grad * keys, axis=1, keepdims=True))
        for name, grad_in, x, sig, rows, taps, start, size in (
            ("q", sq_grad, core["xq"], core["gq"], core["rows_q"], cq, 0, DK),
            ("k", sk_grad, core["xk"], core["gk"], core["rows_k"], ck, width_k, DK),
            ("v", values_grad, core["xv"], core["gv"], core["rows_v"], cv, 2 * width_k, DV),
        ):
            x_grad = grad_in * (sig + x * sig * (1.0 - sig))
            for tap in range(4):
                taps_sum[name][tap] = taps_sum[name][tap] + fold(shifted(rows, tap) * x_grad)
            longer = jnp.concatenate([x_grad, heads_next[name]], axis=0)
            heads_next[name] = x_grad[0:8, :]
            proj = x_grad * taps[3:4, :]
            for tap in range(3):
                proj = proj + longer[3 - tap : 3 - tap + CHUNK, :] * taps[tap : tap + 1, :]
            dp_ref[span, pl.ds(pl.multiple_of(start + head * size, size), size)] = proj.astype(BF16)

    @pl.when(head == heads_n - 1)
    def _():
        dp_ref[:, pl.ds(2 * width_k + 2 * width_v, 128)] = ab_acc[...].astype(BF16)

    def row(x):
        return jnp.sum(x, axis=0, keepdims=True)

    lane = iota2(1, DV, 1)
    rates = jnp.sum(rate_sum[:, 0:1], axis=0, keepdims=True)
    biases = jnp.sum(bias_sum[:, 0:1], axis=0, keepdims=True)
    small = [row(taps_sum["v"][tap]) for tap in range(4)]
    small += [jnp.concatenate([row(taps_sum["q"][tap]), row(taps_sum["k"][tap])], axis=1) for tap in range(4)]
    small += [row(gain_sum), jnp.where(lane == 0, rates, 0.0) + jnp.where(lane == 1, biases, 0.0)]
    small += [jnp.zeros((6, DV), F32)]
    small_ref[0, 0] = jnp.concatenate(small, axis=0)


def specs(heads_n):
    col_v = 2 * heads_n * DK // DV
    return [
        pl.BlockSpec((LEN, DK), lambda s, h: (s, h)),
        pl.BlockSpec((LEN, DK), lambda s, h: (s, heads_n + h)),
        pl.BlockSpec((LEN, DV), lambda s, h: (s, col_v + h)),
        pl.BlockSpec((LEN, DV), lambda s, h: (s, col_v + heads_n + h)),
        pl.BlockSpec((LEN, 128), lambda s, h: (s, 2 * heads_n + 4 * heads_n)),
        pl.BlockSpec((4, DK), lambda s, h: (0, h)),
        pl.BlockSpec((4, DK), lambda s, h: (0, h)),
        pl.BlockSpec((4, DV), lambda s, h: (0, h)),
        pl.BlockSpec((8, 128), lambda s, h: (0, 0)),
        pl.BlockSpec((1, DV), lambda s, h: (0, 0)),
    ]


def saved_specs(heads_n):
    return [
        pl.BlockSpec((LEN, DV), lambda s, h: (s, h)),
        pl.BlockSpec((LEN, DV), lambda s, h: (s, h)),
        pl.BlockSpec((1, 1, PARTS, CHUNK, CHUNK), lambda s, h: (s, h, 0, 0, 0)),
        pl.BlockSpec((1, 1, PARTS, DK, DV), lambda s, h: (s, h, 0, 0, 0)),
    ]


def mix_forward(proj, cq, ck, cv, heads_in, gain):
    rows = proj.shape[0]
    seqs, heads_n = rows // LEN, cq.shape[1] // DK
    wide = jax.ShapeDtypeStruct((rows, heads_n * DV), BF16)
    return pl.pallas_call(
        functools.partial(forward_kernel, heads_n),
        grid=(seqs, heads_n),
        in_specs=specs(heads_n),
        out_specs=[pl.BlockSpec((LEN, DV), lambda s, h: (s, h))] + saved_specs(heads_n),
        out_shape=[
            wide, wide, wide,
            jax.ShapeDtypeStruct((seqs, heads_n, PARTS, CHUNK, CHUNK), BF16),
            jax.ShapeDtypeStruct((seqs, heads_n, PARTS, DK, DV), BF16),
        ],
        cost_estimate=pl.CostEstimate(flops=2 * 10**9, bytes_accessed=25 * 10**6, transcendentals=10**6),
        name="mix_forward",
    )(proj, proj, proj, proj, proj, cq, ck, cv, heads_in, gain)


def mix_backward(proj, cq, ck, cv, heads_in, gain, grad, saved):
    rows, cols = proj.shape
    seqs, heads_n = rows // LEN, cq.shape[1] // DK
    return pl.pallas_call(
        functools.partial(backward_kernel, heads_n),
        grid=(seqs, heads_n),
        in_specs=specs(heads_n) + [pl.BlockSpec((LEN, DV), lambda s, h: (s, h))] + saved_specs(heads_n),
        out_specs=[
            pl.BlockSpec((LEN, cols), lambda s, h: (s, 0)),
            pl.BlockSpec((1, 1, 16, DV), lambda s, h: (s, h, 0, 0)),
        ],
        out_shape=[
            jax.ShapeDtypeStruct((rows, cols), BF16),
            jax.ShapeDtypeStruct((seqs, heads_n, 16, DV), F32),
        ],
        scratch_shapes=[pltpu.VMEM((LEN, 128), F32)],
        cost_estimate=pl.CostEstimate(flops=5 * 10**9, bytes_accessed=40 * 10**6, transcendentals=10**6),
        name="mix_backward",
    )(proj, proj, proj, proj, proj, cq, ck, cv, heads_in, gain, grad, *saved)


def matmul(left, right):
    return jnp.dot(left, right, preferred_element_type=F32)


def rows_inner(left, right):
    return lax.dot_general(left, right, (((0,), (0,)), ((), ())), preferred_element_type=F32)


def against_rows(left, right):
    return lax.dot_general(left, right, (((1,), (1,)), ((), ())), preferred_element_type=F32)


def row_factor(values):
    return lax.rsqrt(jnp.mean(values * values, axis=-1, keepdims=True) + 1e-05)


def norm_backward(values, factor, gain, grad):
    normed = values * factor
    inner = grad * gain
    spread = jnp.mean(inner * normed, axis=-1, keepdims=True)
    return factor * (inner - normed * spread), jnp.sum(grad * normed, axis=0)


SWAP = [(0, 1), (1, 0)]


def swap(value, axis):
    return lax.ppermute(value, axis, SWAP)


def gather_rows(shard):
    mine = lax.all_gather(shard, "chip", axis=0, tiled=True)
    other = swap(mine, "core")
    first = lax.axis_index("core") == 0
    count = shard.shape[0]
    even = jnp.where(first, mine, other).reshape(-1, 1, count, shard.shape[1])
    odd = jnp.where(first, other, mine).reshape(-1, 1, count, shard.shape[1])
    return jnp.concatenate([even, odd], axis=1).reshape(-1, shard.shape[1])


def core_columns(values, chips):
    core = lax.axis_index("core")
    split = values.reshape(values.shape[0], chips, 2, -1)
    mine = lax.dynamic_index_in_dim(split, core, 2, keepdims=False)
    other = lax.dynamic_index_in_dim(split, 1 - core, 2, keepdims=False)
    return mine.reshape(values.shape[0], -1), other.reshape(values.shape[0], -1)


def weight_grad(columns, grads):
    mine, other = columns
    sent = jnp.concatenate([rows_inner(other, grad).astype(BF16) for grad in grads], axis=1)
    came = swap(sent, "core")
    kept, at = [], 0
    for grad in grads:
        kept.append((rows_inner(mine, grad) + came[:, at : at + grad.shape[1]].astype(F32)).astype(BF16))
        at += grad.shape[1]
    return jnp.concatenate(kept, axis=1)


def all_sum(value, axis, size):
    step = 1
    while step < size:
        value = value + lax.ppermute(value, axis, [(at, at ^ step) for at in range(size)])
        step *= 2
    return value


def local(chips, tokens, norm_gain1, w_query, w_key, w_value, w_gate, w_decay, w_write, conv_query, conv_key,
          conv_value, a_log, dt_bias, out_gain, w_out, norm_gain2, w_ffgate, w_ffup, w_ffdown, cotangent):
    heads_n = a_log.shape[0]
    half = tokens.shape[0]
    pad = jnp.zeros((w_query.shape[0], 128 - 2 * heads_n), BF16)
    mix_shard = jnp.concatenate([w_query, w_key, w_value, w_gate, w_decay, w_write, pad], axis=1)
    late_shard = jnp.concatenate([w_out.T, w_ffgate, w_ffup, w_ffdown.T], axis=1)
    ff = w_ffgate.shape[1]
    wide = w_out.shape[0]
    tokens_other = swap(tokens, "tensor")
    cot = jnp.concatenate([cotangent, swap(cotangent, "tensor")], axis=0)
    w_mix = gather_rows(mix_shard)
    w_late = gather_rows(late_shard)
    w_out_t, w_gu, w_down_t = w_late[:, :wide], w_late[:, wide : wide + 2 * ff], w_late[:, wide + 2 * ff :]

    tokens32 = jnp.concatenate([tokens, tokens_other], axis=0).astype(F32)
    factor1 = row_factor(tokens32)
    normed1 = (tokens32 * factor1 * norm_gain1).astype(BF16)
    proj = matmul(normed1, w_mix)
    heads_in = jnp.pad(jnp.stack([a_log, dt_bias]), ((0, 6), (0, 128 - heads_n)))
    gain = out_gain.reshape(1, -1)
    gated, *saved = mix_forward(proj, conv_query, conv_key, conv_value, heads_in, gain)
    mix_part = against_rows(gated, w_out_t)
    resid1 = tokens32[:half] + mix_part[:half] + swap(mix_part[half:].astype(BF16), "tensor").astype(F32)
    factor2 = row_factor(resid1)
    normed2_own = (resid1 * factor2 * norm_gain2).astype(BF16)
    normed2 = jnp.concatenate([normed2_own, swap(normed2_own, "tensor")], axis=0)

    gate_up = matmul(normed2, w_gu)
    gate_val, up_val = gate_up[:, :ff], gate_up[:, ff:]
    gate_sig = jax.nn.sigmoid(gate_val)
    act = gate_val * gate_sig
    hidden = (act * up_val).astype(BF16)
    ffn_part = against_rows(hidden, w_down_t)
    result = resid1 + ffn_part[:half] + swap(ffn_part[half:].astype(BF16), "tensor").astype(F32)

    grad_hidden = matmul(cot, w_down_t)
    grad_gate = (grad_hidden * up_val * (gate_sig + act * (1.0 - gate_sig))).astype(BF16)
    grad_up = (grad_hidden * act).astype(BF16)
    grad_normed2 = against_rows(grad_gate, w_gu[:, :ff]) + against_rows(grad_up, w_gu[:, ff:])
    grad_rows2 = grad_normed2[:half] + swap(grad_normed2[half:].astype(BF16), "tensor").astype(F32)
    grad_norm, grad_gain2 = norm_backward(resid1, factor2, norm_gain2, grad_rows2)
    grad_resid = cotangent.astype(F32) + grad_norm
    resid_own = grad_resid.astype(BF16)
    resid_full = jnp.concatenate([resid_own, swap(resid_own, "tensor")], axis=0)
    grad_gated = matmul(resid_full, w_out_t)

    ffn_sum = jnp.concatenate(
        [weight_grad(core_columns(normed2, chips), (grad_gate, grad_up)), weight_grad(core_columns(cot, chips), (hidden,)),
         weight_grad(core_columns(resid_full, chips), (gated,))], axis=1)
    ffn_sum = lax.psum_scatter(ffn_sum, "chip", scatter_dimension=0, tiled=True).astype(F32)

    grad_proj, small = mix_backward(proj, conv_query, conv_key, conv_value, heads_in, gain, grad_gated, saved)
    small = jnp.sum(small, axis=0)
    small = all_sum(all_sum(small.reshape(-1, DV), "core", 2), "chip", chips).reshape(heads_n, 16, DV)
    mix_sum = weight_grad(core_columns(normed1, chips), (grad_proj,))
    mix_sum = lax.psum_scatter(mix_sum, "chip", scatter_dimension=0, tiled=True).astype(F32)
    grad_normed1 = against_rows(grad_proj, w_mix)
    grad_rows1 = grad_normed1[:half] + swap(grad_normed1[half:].astype(BF16), "tensor").astype(F32)
    grad_norm1, grad_gain1 = norm_backward(tokens32[:half], factor1[:half], norm_gain1, grad_rows1)
    grad_tokens = grad_resid + grad_norm1
    gain_rows = jnp.concatenate([grad_gain1.reshape(-1, 128), grad_gain2.reshape(-1, 128)], axis=0)
    gain_rows = all_sum(all_sum(all_sum(gain_rows, "core", 2), "tensor", 2), "chip", chips)
    out_gain_sum = all_sum(jnp.sum(small[:, 8], axis=0, keepdims=True), "tensor", 2)

    key_w, val_w = heads_n * DK, heads_n * DV

    def taps(rows):
        return jnp.transpose(rows, (1, 0, 2)).reshape(4, -1)

    decay_at = 2 * key_w + 2 * val_w
    return (
        result.astype(BF16),
        grad_tokens,
        gain_rows[: gain_rows.shape[0] // 2].reshape(-1),
        mix_sum[:, :key_w],
        mix_sum[:, key_w : 2 * key_w],
        mix_sum[:, 2 * key_w : 2 * key_w + val_w],
        mix_sum[:, 2 * key_w + val_w : decay_at],
        mix_sum[:, decay_at : decay_at + heads_n],
        mix_sum[:, decay_at + heads_n : decay_at + 2 * heads_n],
        taps(small[:, 4:8, :DK]),
        taps(small[:, 4:8, DK:]),
        taps(small[:, :4]),
        small[:, 9, 0],
        small[:, 9, 1],
        out_gain_sum.reshape(-1),
        ffn_sum[:, 3 * ff :].T,
        gain_rows[gain_rows.shape[0] // 2 :].reshape(-1),
        ffn_sum[:, :ff],
        ffn_sum[:, ff : 2 * ff],
        ffn_sum[:, 2 * ff : 3 * ff].T,
    )


def solution(mesh):
    chips = mesh.shape["dp"] // 2
    inner = jax.sharding.Mesh(mesh.devices.reshape(chips, 2, -1), ("chip", "core", "tensor"))
    dp, rows, every = ("chip", "core"), P(("chip", "core", "tensor"), None), P()
    down, across, taps, head = P(dp, "tensor"), P("tensor", dp), P(None, "tensor"), P("tensor")
    return jax.shard_map(
        functools.partial(local, chips),
        mesh=inner,
        in_specs=(rows, every, down, down, down, down, down, down, taps, taps, taps, head, head, every, across, every,
                  down, down, across, rows),
        out_specs=(rows, rows, every, down, down, down, down, down, down, taps, taps, taps, head, head, every, across,
                   every, down, down, across),
        check_vma=False,
    )
```

time: 2150 us -> 710 us (0.33)
  waiting for transfers between devices: 965 us -> 392 us
  other arithmetic: 446 us -> 50.1 us
  matrix products: 387 us -> 98.6 us
  local copies, waits for them, and re-layouts: 179 us -> 38.8 us
  blocking collectives: 140 us -> 0 us
  Pallas kernels: 0 us -> 94.3 us
    reduce_scatter x12 -> x2, waiting for transfers between devices: 705 us -> 85.3 us  [the longest x1 85.3 us: local(): lax.psum_scatter(ffn_sum, 'chip', scatter_dimension=0, tiled=True)]
    another operation x19 -> x1, other arithmetic: 337 us -> 0.6 us  [local(): jnp.stack([a_log, dt_bias])]
    dot_general x139 -> x19, matrix products: 361 us -> 98.6 us  [the longest x4 41.4 us: matmul(): return jnp.dot(left, right, preferred_element_type=F32)]
    ppermute x0 -> x24, waiting for transfers between devices: none -> 156 us  [the longest x14 129 us: swap(): return lax.ppermute(value, axis, SWAP)]
    all_gather x12 -> x2, waiting for transfers between devices: 255 us -> 151 us  [gather_rows(): mine = lax.all_gather(shard, 'chip', axis=0, tiled=True)]
    psum x2 -> x0, blocking collectives: 99.5 us -> none  [the longest x1 61.7 us: local(): lax.psum((mix_grads[6], mix_grads[7], mix_grads[8], mix_grads[9], mix_gra...]
    pallas_call x0 -> x2, Pallas kernels: none -> 94.3 us  [the longest x1 58.9 us: mix_backward(): pl.pallas_call(functools.partial(backward_kernel, heads_n), grid=(seqs, h...]
    reduce_sum x26 -> x6, other arithmetic: 49.6 us -> 4.62 us  [the longest x2 3.69 us: norm_backward(): return (factor * (inner - normed * spread), jnp.sum(grad * normed, axis=0))]
  transfers between devices with their start and end apart: 26 -> 28, of which waited for: 18 -> 21; matrix products, arithmetic and copies ran while one was open for 30% -> 16% of each run, Pallas kernels for 0% -> 5%
where the time goes in v1:
time: 710 us; the launch traced here: 706 us
  waiting for transfers between devices  392 us (55%)
  matrix products  98.6 us (14%)
  Pallas kernels  94.3 us (13%)
  other arithmetic  50.1 us (7%)
  local copies, waits for them, and re-layouts  38.8 us (5%)
  starting transfers between devices  17.8 us (3%)
  between operations  14.6 us (2%)
    all_gather x2, waiting for transfers between devices, gather_rows(): mine = lax.all_gather(shard, 'chip', axis=0, tiled=True)  151 us
    ppermute x14, waiting for transfers between devices, swap(): return lax.ppermute(value, axis, SWAP)  129 us
    reduce_scatter x1, waiting for transfers between devices, local(): lax.psum_scatter(ffn_sum, 'chip', scatter_dimension=0, tiled=True)  85.3 us
    pallas_call x1, Pallas kernels, mix_backward(): pl.pallas_call(functools.partial(backward_kernel, heads_n), grid=(seqs, h...  58.9 us
    dot_general x4, matrix products, matmul(): return jnp.dot(left, right, preferred_element_type=F32)  41.4 us
    pallas_call x1, Pallas kernels, mix_forward(): pl.pallas_call(functools.partial(forward_kernel, heads_n), grid=(seqs, he...  35.4 us
    dot_general x10, matrix products, rows_inner(): lax.dot_general(left, right, (((0,), (0,)), ((), ())), preferred_element_...  29.3 us
    dot_general x5, matrix products, against_rows(): lax.dot_general(left, right, (((1,), (1,)), ((), ())), preferred_element_...  27.8 us
  transfers between devices with their start and end apart: 28, of which 21 were waited for; matrix products, arithmetic and copies ran while one was open for 16% of the time, Pallas kernels for 5%

profile of v1, /device:TPU:0, one launch (start us, length us, event | category | flops | bytes accessed | tf_op | source)
XLA Modules:
  0.0 706.4 jit_solution(5804449108989252838)
XLA Ops:
  13.0 62.1 %all-gather.3.cloned.1.call-done = bf16[512,3200]{1,0:T(8,128)(2,1)} async-done(((bf16[64,3200]{1,0:T(8,128)(2,1)}), bf16[512,3200]{1,0:T(8,128)(2,1)}) %all-gather.3.cloned.1.call-update) | async-done | bytes 3276816 | tf_op jit(solution)/shard_map/all_gather | solution.py:413
  75.2 89.0 %all-gather.5.cloned.1.call-done = bf16[512,5248]{1,0:T(8,128)(2,1)} async-done(((bf16[64,5248]{1,0:T(8,128)(2,1)}), bf16[512,5248]{1,0:T(8,128)(2,1)}) %all-gather.5.cloned.1.call-update) | async-done | bytes 5373968 | tf_op jit(solution)/shard_map/all_gather | solution.py:413
  166.2 23.5 %collective-permute-done = bf16[512,1024]{1,0:T(8,128)(2,1)S(1)} collective-permute-done((bf16[512,1024]{1,0:T(8,128)(2,1)S(1)}, bf16[512,1024]{1,0:T(8,128)(2,1)S(1)}, u32[]{:S(2)}, u32[]{:S(2)}) %collective-permute-start) | collective-permute-done | bytes 1048608 | tf_op jit(solution)/shard_map/ppermute | solution.py:409
  194.4 11.9 %fusion.10.q_ref.k_ref.v_ref.g_ref.ab_ref = f32[1024,3200]{1,0:T(8,128)} fusion(bf16[1024,3200]{1,0:T(8,128)(2,1)S(1)} %bitcast.93, f32[1024]{0:T(1024)S(1)} %copy-done.19, f32[1024]{0:T(1024)S(1)} %add_rsqrt_fusion, bf16[512,1024]{1,0:T(8,128)(2,1)S(1)} %collective-permute-done, bf16[512,1024]{1,0:T(8,128)(2,1)S(1)} %copy-done.3), kind=kOutput, calls=%fused_computation.34 | convolution fusion | flops 6718226432 | bytes 21766144 | tf_op jit(solution)/shard_map/dot_general | solution.py:383
  206.3 35.4 %mix_forward.1 = (bf16[1024,1024]{1,0:T(8,128)(2,1)}, bf16[1024,1024]{1,0:T(8,128)(2,1)}, bf16[1024,1024]{1,0:T(8,128)(2,1)}, bf16[2,4,4,128,128]{4,3,2,1,0:T(8,128)(2,1)}, bf16[2,4,4,128,256]{4,3,2,1,0:T(8,128)(2,1)}) custom-call(f32[1024,3200]{1,0:T(8,128)} %fusion.10.q_ref.k_ref.v_ref.g_ref.ab_ref, f32[1024,3200]{1,0:T(8,128)} %fusion.10.q_ref.k_ref.v_ref.g_ref.ab_ref, ...), custom_call_target="tpu_custom_call" | custom-call | flops 2000000000 | bytes 25000000 | tf_op jit(solution)/shard_map/mix_forward/pallas_call | solution.py:346
  241.7 9.0 %broadcast_select_fusion.1 = (bf16[512,5248]{1,0:T(8,128)(2,1)}, bf16[512,5248]{1,0:T(8,128)(2,1)}) fusion(bf16[512,5248]{1,0:T(8,128)(2,1)} %all-gather.5.cloned.1.call-done, bf16[512,5248]{1,0:T(8,128)(2,1)} %collective-permute-done.2, pred[]{:T(512)S(6)} %eq.4), kind=kLoop, calls=%fused_computation.13 | loop fusion | flops 5373952 | bytes 21495808 | tf_op jit(solution)/shard_map/jit(_where)/select_n | solution.py:417
  250.7 5.9 pad_maximum_fusion
  262.7 22.8 %collective-permute-done.3 = bf16[512,1024]{1,0:T(8,128)(2,1)S(1)} collective-permute-done((bf16[512,1024]{1,0:T(8,128)(2,1)S(1)}, bf16[512,1024]{1,0:T(8,128)(2,1)S(1)}, u32[]{:S(2)}, u32[]{:S(2)}) %collective-permute-start.3) | collective-permute-done | bytes 1048608 | tf_op jit(solution)/shard_map/ppermute | solution.py:409
  291.5 22.0 %collective-permute-done.4 = bf16[512,1024]{1,0:T(8,128)(2,1)} collective-permute-done((bf16[512,1024]{1,0:T(8,128)(2,1)}, bf16[512,1024]{1,0:T(8,128)(2,1)}, u32[]{:S(2)}, u32[]{:S(2)}) %collective-permute-start.4) | collective-permute-done | bytes 1048608 | tf_op jit(solution)/shard_map/ppermute | solution.py:409
  313.5 12.1 %fusion = f32[1024,2816]{1,0:T(8,128)} fusion(bf16[1024,5248]{1,0:T(8,128)(2,1)} %bitcast.82, bf16[512,1024]{1,0:T(8,128)(2,1)} %collective-permute-done.4, bf16[512,1024]{1,0:T(8,128)(2,1)} %multiply_convert_fusion.6), kind=kOutput, calls=%fused_computation.4 | convolution fusion | flops 5909774336 | bytes 19398656 | tf_op jit(solution)/shard_map/dot_general | solution.py:383
  325.7 8.0 %collective-permute-done.6 = bf16[512,1024]{0,1:T(8,128)(2,1)S(1)} collective-permute-done((bf16[512,1024]{0,1:T(8,128)(2,1)}, bf16[512,1024]{0,1:T(8,128)(2,1)S(1)}, u32[]{:S(2)}, u32[]{:S(2)}) %collective-permute-start.6) | collective-permute-done | bytes 1048608 | tf_op jit(solution)/shard_map/ppermute | solution.py:409
  333.7 10.8 %multiply_convert_fusion.1 = (bf16[1024,1408]{1,0:T(8,128)(2,1)S(1)}, bf16[1024,1408]{1,0:T(8,128)(2,1)S(1)}, bf16[1024,1408]{1,0:T(8,128)(2,1)}) fusion(f32[1024,2816]{1,0:T(8,128)} %fusion, bf16[1024,5248]{1,0:T(8,128)(2,1)} %bitcast.83, bf16[512,1024]{0,1:T(8,128)(2,1)S(1)} %collective-permute-done.6, bf16[512,1024]{0,1:T(8,128)(2,1)S(1)} %copy-done.9), kind=kOutput, calls=%fused_computation.7 | convolution fusion | flops 2977169408 | bytes 25165824 | tf_op jit(solution)/shard_map/dot_general | solution.py:383
  344.6 5.0 fusion.2
  349.6 5.4 fusion.16
  361.0 20.3 %collective-permute-done.7 = bf16[512,1024]{1,0:T(8,128)(2,1)S(1)} collective-permute-done((bf16[512,1024]{1,0:T(8,128)(2,1)S(1)}, bf16[512,1024]{1,0:T(8,128)(2,1)S(1)}, u32[]{:S(2)}, u32[]{:S(2)}) %collective-permute-start.7) | collective-permute-done | bytes 1048608 | tf_op jit(solution)/shard_map/ppermute | solution.py:409
  382.1 18.7 %collective-permute-done.5 = bf16[512,1024]{1,0:T(8,128)(2,1)S(1)} collective-permute-done((bf16[512,1024]{1,0:T(8,128)(2,1)S(1)}, bf16[512,1024]{1,0:T(8,128)(2,1)S(1)}, u32[]{:S(2)}, u32[]{:S(2)}) %collective-permute-start.5) | collective-permute-done | bytes 1048608 | tf_op jit(solution)/shard_map/ppermute | solution.py:409
  413.0 4.3 copy.63
  420.8 5.5 collective-permute-done.8
  426.3 6.5 fusion.19.grad_ref
  432.8 58.9 %mix_backward.1 = (bf16[1024,3200]{1,0:T(8,128)(2,1)}, f32[2,4,16,256]{3,2,1,0:T(8,128)}) custom-call(f32[1024,3200]{1,0:T(8,128)} %fusion.10.q_ref.k_ref.v_ref.g_ref.ab_ref, f32[1024,3200]{1,0:T(8,128)} %fusion.10.q_ref.k_ref.v_ref.g_ref.ab_ref, f32[1024,3200]{1,0:T(8,128)} %fusion.10.q_ref.k_ref.v_ref.g_ref.ab_ref, ...), custom_call_target="tpu_custom_call" | custom-call | flops 5000000000 | bytes 40000000 | tf_op jit(solution)/shard_map/mix_backward/pallas_call | solution.py:364
  491.7 6.9 convolution_convert_fusion
  498.7 5.8 collective-permute-done.15
  504.6 5.2 add_convert_fusion
  511.0 3.8 convolution_convert_fusion.3
  522.5 4.0 copy.64
  534.8 3.8 add_convert_fusion.3
  541.7 3.7 pad_maximum_fusion.2
  545.4 11.6 %fusion.31 = f32[1024,1024]{1,0:T(8,128)S(1)} fusion(bf16[1024,3200]{1,0:T(8,128)(2,1)} %get-tuple-element.32, bf16[1024,3200]{1,0:T(8,128)(2,1)} %bitcast.94), kind=kOutput, calls=%fused_computation.102 | convolution fusion | flops 6710886400 | bytes 17301504 | tf_op jit(solution)/shard_map/dot_general | solution.py:391
  561.8 3.6 collective-permute-done.17
  566.1 6.2 collective-permute-done.18
  572.4 9.1 %collective-permute-done.19 = f32[64,256]{1,0:T(8,128)S(1)} collective-permute-done((f32[64,256]{1,0:T(8,128)S(1)}, f32[64,256]{1,0:T(8,128)S(1)}, u32[]{:S(2)}, u32[]{:S(2)}) %collective-permute-start.19) | collective-permute-done | bytes 65568 | tf_op jit(solution)/shard_map/ppermute | solution.py:444
  610.7 85.3 %reduce-scatter.5.cloned.1.call-done = bf16[64,5248]{1,0:T(8,128)(2,1)} async-done(((bf16[512,5248]{1,0:T(8,128)(2,1)}), bf16[64,5248]{1,0:T(8,128)(2,1)}) %reduce-scatter.5.cloned.1.call-update) | async-done | bytes 671760 | tf_op jit(solution)/shard_map/reduce_scatter | solution.py:499
  (187 shorter events, 105.6 us)
Async XLA Ops:
  7.2 157.0 %copy-start.3 = (bf16[512,1024]{1,0:T(8,128)(2,1)S(1)}, bf16[512,1024]{1,0:T(8,128)(2,1)}, u32[]{:S(2)}) copy-start(bf16[512,1024]{1,0:T(8,128)(2,1)} %param.20) | copy-start | bytes 3145732
  7.2 158.4 %copy-start.21 = (f32[4]{0:T(128)S(1)}, f32[4]{0:T(128)}, u32[]{:S(2)}) copy-start(f32[4]{0:T(128)} %param.31) | copy-start | bytes 52
  7.2 158.4 %copy-start.20 = (f32[4]{0:T(128)S(1)}, f32[4]{0:T(128)}, u32[]{:S(2)}) copy-start(f32[4]{0:T(128)} %param.32) | copy-start | bytes 52
  7.2 67.9 %all-gather.3.cloned.1.call-start = ((), (), s32[]{:S(2)}) async-start(), calls=%async_computation.2 | async-start | bytes 3686400 | tf_op jit(solution)/shard_map/all_gather | solution.py:413
  10.8 153.3 %all-gather.5.cloned.1.call-start = ((), (), s32[]{:S(2)}) async-start(), calls=%async_computation.3 | async-start | bytes 6045696 | tf_op jit(solution)/shard_map/all_gather | solution.py:413
  13.0 592.1 %reduce-scatter.3.cloned.1.call-start = ((), (), s32[]{:S(2)}) async-start(), calls=%async_computation.4 | async-start | bytes 3686400 | tf_op jit(solution)/shard_map/reduce_scatter | solution.py:505
  75.2 115.1 %collective-permute-start.1 = (bf16[512,3200]{1,0:T(8,128)(2,1)}, bf16[512,3200]{1,0:T(8,128)(2,1)}, u32[]{:S(2)}, u32[]{:S(2)}) collective-permute-start(bf16[512,3200]{1,0:T(8,128)(2,1)} %all-gather.3.cloned.1.call-done), channel_id=1, source_target_pairs={{0,2},{2,0},{1,3},{3,1},{4,6},{6,4},{5,7},{7,5},{8,10},{10,8},{9,1... | collective-permute-start | bytes 9830408 | tf_op jit(solution)/shard_map/ppermute | solution.py:409
  164.1 77.6 %collective-permute-start.2 = (bf16[512,5248]{1,0:T(8,128)(2,1)}, bf16[512,5248]{1,0:T(8,128)(2,1)}, u32[]{:S(2)}, u32[]{:S(2)}) collective-permute-start(bf16[512,5248]{1,0:T(8,128)(2,1)} %all-gather.5.cloned.1.call-done), channel_id=1, source_target_pairs={{0,2},{2,0},{1,3},{3,1},{4,6},{6,4},{5,7},{7,5},{8,10},{10,8},{9,1... | collective-permute-start | bytes 16121864 | tf_op jit(solution)/shard_map/ppermute | solution.py:409
  164.1 25.6 %collective-permute-start = (bf16[512,1024]{1,0:T(8,128)(2,1)S(1)}, bf16[512,1024]{1,0:T(8,128)(2,1)S(1)}, u32[]{:S(2)}, u32[]{:S(2)}) collective-permute-start(bf16[512,1024]{1,0:T(8,128)(2,1)S(1)} %copy-done.3), channel_id=1, source_target_pairs={{0,1},{1,0},{2,3},{3,2},{4,5},{5,4},{6,7},{7,6},{8,9},{9,8},{10,11... | collective-permute-start | bytes 3145736 | tf_op jit(solution)/shard_map/ppermute | solution.py:409
  189.7 72.5 %copy-start.4 = (bf16[512,1024]{1,0:T(8,128)(2,1)}, bf16[512,1024]{1,0:T(8,128)(2,1)S(1)}, u32[]{:S(2)}) copy-start(bf16[512,1024]{1,0:T(8,128)(2,1)S(1)} %collective-permute-done) | copy-start | bytes 3145732
  260.7 24.8 %collective-permute-start.3 = (bf16[512,1024]{1,0:T(8,128)(2,1)S(1)}, bf16[512,1024]{1,0:T(8,128)(2,1)S(1)}, u32[]{:S(2)}, u32[]{:S(2)}) collective-permute-start(bf16[512,1024]{1,0:T(8,128)(2,1)S(1)} %slice.272), channel_id=1, source_target_pairs={{0,1},{1,0},{2,3},{3,2},{4,5},{5,4},{6,7},{7,6},{8,9},{9,8},{10,11... | collective-permute-start | bytes 3145736 | tf_op jit(solution)/shard_map/ppermute | solution.py:409
  287.2 26.3 %collective-permute-start.4 = (bf16[512,1024]{1,0:T(8,128)(2,1)}, bf16[512,1024]{1,0:T(8,128)(2,1)}, u32[]{:S(2)}, u32[]{:S(2)}) collective-permute-start(bf16[512,1024]{1,0:T(8,128)(2,1)} %multiply_convert_fusion.6), channel_id=1, source_target_pairs={{0,1},{1,0},{2,3},{3,2},{4,5},{5,4},{6,7},{7,6},{8,9},{9,8},{10,11... | collective-permute-start | bytes 3145736 | tf_op jit(solution)/shard_map/ppermute | solution.py:409
  290.9 42.8 %collective-permute-start.6 = (bf16[512,1024]{0,1:T(8,128)(2,1)}, bf16[512,1024]{0,1:T(8,128)(2,1)S(1)}, u32[]{:S(2)}, u32[]{:S(2)}) collective-permute-start(bf16[512,1024]{0,1:T(8,128)(2,1)} %copy.60), channel_id=1, source_target_pairs={{0,1},{1,0},{2,3},{3,2},{4,5},{5,4},{6,7},{7,6},{8,9},{9,8},{10,11... | collective-permute-start | bytes 3145736 | tf_op jit(solution)/shard_map/ppermute | solution.py:409
  355.2 26.1 %collective-permute-start.7 = (bf16[512,1024]{1,0:T(8,128)(2,1)S(1)}, bf16[512,1024]{1,0:T(8,128)(2,1)S(1)}, u32[]{:S(2)}, u32[]{:S(2)}) collective-permute-start(bf16[512,1024]{1,0:T(8,128)(2,1)S(1)} %slice.270), channel_id=1, source_target_pairs={{0,1},{1,0},{2,3},{3,2},{4,5},{5,4},{6,7},{7,6},{8,9},{9,8},{10,11... | collective-permute-start | bytes 3145736 | tf_op jit(solution)/shard_map/ppermute | solution.py:409
  360.4 40.4 %collective-permute-start.5 = (bf16[512,1024]{1,0:T(8,128)(2,1)S(1)}, bf16[512,1024]{1,0:T(8,128)(2,1)S(1)}, u32[]{:S(2)}, u32[]{:S(2)}) collective-permute-start(bf16[512,1024]{1,0:T(8,128)(2,1)S(1)} %slice.271), channel_id=1, source_target_pairs={{0,1},{1,0},{2,3},{3,2},{4,5},{5,4},{6,7},{7,6},{8,9},{9,8},{10,11... | collective-permute-start | bytes 3145736 | tf_op jit(solution)/shard_map/ppermute | solution.py:409
  403.9 22.4 %collective-permute-start.8 = (bf16[512,1024]{1,0:T(8,128)(2,1)}, bf16[512,1024]{1,0:T(8,128)(2,1)}, u32[]{:S(2)}, u32[]{:S(2)}) collective-permute-start(bf16[512,1024]{1,0:T(8,128)(2,1)} %get-tuple-element.100), channel_id=1, source_target_pairs={{0,1},{1,0},{2,3},{3,2},{4,5},{5,4},{6,7},{7,6},{8,9},{9,8},{10,11... | collective-permute-start | bytes 3145736 | tf_op jit(solution)/shard_map/ppermute | solution.py:409
  498.7 5.9 collective-permute-start.15
  509.8 186.2 %reduce-scatter.5.cloned.1.call-start = ((), (), s32[]{:S(2)}) async-start(), calls=%async_computation.5 | async-start | bytes 6045696 | tf_op jit(solution)/shard_map/reduce_scatter | solution.py:499
  518.4 16.3 %collective-permute-start.21 = (bf16[512,2816]{1,0:T(8,128)(2,1)}, bf16[512,2816]{1,0:T(8,128)(2,1)}, u32[]{:S(2)}, u32[]{:S(2)}) collective-permute-start(bf16[512,2816]{1,0:T(8,128)(2,1)} %pad_maximum_fusion.3), channel_id=1, source_target_pairs={{0,2},{2,0},{1,3},{3,1},{4,6},{6,4},{5,7},{7,5},{8,10},{10,8},{9,1... | collective-permute-start | bytes 8650760 | tf_op jit(solution)/shard_map/ppermute | solution.py:409
  530.7 9.1 %collective-permute-start.22 = (bf16[512,1408]{1,0:T(8,128)(2,1)S(1)}, bf16[512,1408]{1,0:T(8,128)(2,1)S(1)}, u32[]{:S(2)}, u32[]{:S(2)}) collective-permute-start(bf16[512,1408]{1,0:T(8,128)(2,1)S(1)} %convolution_convert_fusion.1), channel_id=1, source_target_pairs={{0,2},{2,0},{1,3},{3,1},{4,6},{6,4},{5,7},{7,5},{8,10},{10,8},{9,1... | collective-permute-start | bytes 4325384 | tf_op jit(solution)/shard_map/ppermute | solution.py:409
  532.2 6.4 collective-permute-start.23
  558.3 25.5 %collective-permute-start.9 = (bf16[512,1024]{1,0:T(8,128)(2,1)}, bf16[512,1024]{1,0:T(8,128)(2,1)S(1)}, u32[]{:S(2)}, u32[]{:S(2)}) collective-permute-start(bf16[512,1024]{1,0:T(8,128)(2,1)} %slice.269), channel_id=1, source_target_pairs={{0,1},{1,0},{2,3},{3,2},{4,5},{5,4},{6,7},{7,6},{8,9},{9,8},{10,11... | collective-permute-start | bytes 3145736 | tf_op jit(solution)/shard_map/ppermute | solution.py:409
  559.8 1.3 collective-permute-start.16
  561.1 4.3 collective-permute-start.17
  565.5 6.9 collective-permute-start.18
  572.3 9.2 %collective-permute-start.19 = (f32[64,256]{1,0:T(8,128)S(1)}, f32[64,256]{1,0:T(8,128)S(1)}, u32[]{:S(2)}, u32[]{:S(2)}) collective-permute-start(f32[64,256]{1,0:T(8,128)S(1)} %add.150), channel_id=1, source_target_pairs={{0,16},{4,20},{8,24},{12,28},{16,0},{20,4},{24,8},{28,12},{1,17},{... | collective-permute-start | bytes 196616 | tf_op jit(solution)/shard_map/ppermute | solution.py:444
  586.7 1.2 collective-permute-start.10
  588.0 3.7 collective-permute-start.11
  589.5 4.0 collective-permute-start.20
  591.6 3.7 collective-permute-start.12
  595.3 3.7 collective-permute-start.13
  598.9 5.5 collective-permute-start.14
  (31 other events, 459.3 us)
Sparse Core Ops, SparseCore 0:
  10.9 64.1 all-gather.2
  77.9 86.1 all-gather.4
  509.9 77.1 reduce-scatter.2
  590.6 105.3 reduce-scatter.4

commit v2 on v1

v2 whole, which is shorter than its diff:
```python
import functools
import math

import jax
import jax.numpy as jnp
from jax import lax
from jax.experimental import pallas as pl
from jax.experimental.pallas import tpu as pltpu
from jax.sharding import PartitionSpec as P


F32 = jnp.float32
BF16 = jnp.bfloat16
LEN = 512
DK = 128
DV = 256
CHUNK = 128
FF_HALF = 768
PARTS = LEN // CHUNK


def dot_nn(a, b):
    return lax.dot_general(a, b, (((1,), (0,)), ((), ())), preferred_element_type=F32)


def dot_nt(a, b):
    return lax.dot_general(a, b, (((1,), (1,)), ((), ())), preferred_element_type=F32)


def dot_tn(a, b):
    return lax.dot_general(a, b, (((0,), (0,)), ((), ())), preferred_element_type=F32)


def sigmoid(x):
    return 1.0 / (1.0 + jnp.exp(-x))


def softplus(x):
    return jnp.maximum(x, 0.0) + jnp.log1p(jnp.exp(-jnp.abs(x)))


def exact_rows(rows, ones):
    first = rows.astype(BF16)
    rest = rows - first.astype(F32)
    second = rest.astype(BF16)
    third = (rest - second.astype(F32)).astype(BF16)
    return dot_nn(first, ones) + dot_nn(second, ones) + dot_nn(third, ones)


def iota2(rows, cols, axis):
    return lax.broadcasted_iota(jnp.int32, (rows, cols), axis)


def same_group(size):
    shift = size.bit_length() - 1
    return (iota2(CHUNK, CHUNK, 0) >> shift) == (iota2(CHUNK, CHUNK, 1) >> shift)


def tri(upper):
    row, col = iota2(CHUNK, CHUNK, 0), iota2(CHUNK, CHUNK, 1)
    keep = row <= col if upper else row >= col
    return keep.astype(F32).astype(BF16)


def spread(row):
    return jnp.broadcast_to(row, (CHUNK, CHUNK)).T


def twice(x):
    return jnp.concatenate([x, x], axis=1)


def odd_blocks(x, size):
    return jnp.concatenate([x[at : at + size] for at in range(size, CHUNK, 2 * size)], axis=0)


def weave(even, odd, size):
    parts = []
    for at in range(0, CHUNK // 2, size):
        parts += [even[at : at + size], odd[at : at + size]]
    return jnp.concatenate(parts, axis=0)


def invert_all(lowers):
    in8 = same_group(8)
    lane = iota2(8, CHUNK, 1) & 7
    place = iota2(8, CHUNK, 0)
    small = [jnp.sum(jnp.where(in8, lower, 0.0).reshape(CHUNK // 8, 8, CHUNK), axis=0) for lower in lowers]
    masked = [jnp.where(lane == at, member, 0.0) for member in small for at in range(7)]
    columns = dot_nn(jnp.concatenate(masked, axis=0).astype(BF16), in8.astype(F32).astype(BF16))
    inverse = []
    for which in range(len(lowers)):
        solved = jnp.where(lane == place, 1.0, 0.0)
        for at in range(7):
            start = (which * 7 + at) * 8
            solved = solved - columns[start : start + 8] * jnp.broadcast_to(solved[at : at + 1], (8, CHUNK))
        inverse.append(jnp.where(in8, jnp.concatenate([solved] * (CHUNK // 8), axis=0), 0.0))
    size = 8
    while size < CHUNK:
        ring = jnp.logical_and(same_group(2 * size), jnp.logical_not(same_group(size)))
        between = [odd_blocks(jnp.where(ring, lower, 0.0), size).astype(BF16) for lower in lowers]
        low = [member.astype(BF16) for member in inverse]
        inner = [dot_nn(a, b) for a, b in zip(between, low)]
        padded = [weave(jnp.zeros_like(member), member, size).astype(BF16) for member in inner]
        odd = [odd_blocks(member, size) for member in inverse]
        new_odd = [a - dot_nn(a.astype(BF16), b) for a, b in zip(odd, padded)]
        even = [
            jnp.concatenate([member[at : at + size] for at in range(0, CHUNK, 2 * size)], axis=0) for member in inverse
        ]
        inverse = [weave(a, b, size) for a, b in zip(even, new_odd)]
        size *= 2
    return [member.astype(BF16) for member in inverse]


def head_value(heads_ref, row, head):
    values = heads_ref[row : row + 1, :]
    lane = lax.broadcasted_iota(jnp.int32, values.shape, 1)
    return jnp.sum(jnp.where(lane == head, values, 0.0), axis=1, keepdims=True)


def head_rates(ab_ref, heads_ref, head, heads_n):
    decay_in = ab_ref[pl.ds(head, 1), :] + head_value(heads_ref, 1, head)
    write = sigmoid(ab_ref[pl.ds(heads_n + head, 1), :])
    rate = -jnp.exp(head_value(heads_ref, 0, head))
    soft = softplus(decay_in)
    decay = rate * soft
    rows = [decay[:, at * CHUNK : (at + 1) * CHUNK] for at in range(PARTS)]
    stacked = jnp.concatenate(rows + [jnp.zeros((8 - PARTS, CHUNK), F32)], axis=0)
    return write, decay_in, rate, soft, exact_rows(stacked, tri(True))


def convolve(ref, part, taps):
    body = ref[pl.ds(part * CHUNK, CHUNK), :]
    if part == 0:
        head = jnp.zeros((8, body.shape[1]), F32)
    else:
        head = ref[pl.ds(part * CHUNK - 8, 8), :]
    rows = jnp.concatenate([head, body], axis=0)
    total = body * taps[3:4, :]
    for tap in range(3):
        total = total + rows[5 + tap : 5 + tap + CHUNK, :] * taps[tap : tap + 1, :]
    return total


def chunk_core(xq, xk, xv, write_row, total_row):
    row, col = iota2(CHUNK, CHUNK, 0), iota2(CHUNK, CHUNK, 1)
    gq, gk, gv = sigmoid(xq), sigmoid(xk), sigmoid(xv)
    sq, sk, values = xq * gq, xk * gk, xv * gv
    rq = lax.rsqrt(jnp.sum(sq * sq, axis=1, keepdims=True) + 1e-06)
    rk = lax.rsqrt(jnp.sum(sk * sk, axis=1, keepdims=True) + 1e-06)
    queries = sq * (rq * (1.0 / math.sqrt(DK)))
    keys = sk * rk
    q_low, k_low = queries.astype(BF16), keys.astype(BF16)
    write, total = spread(write_row), spread(total_row)
    fade = jnp.where(row >= col, jnp.exp(jnp.minimum(total - total_row, 0.0)), 0.0)
    fade_strict = jnp.where(row > col, fade, 0.0)
    key_inner = dot_nt(k_low, k_low)
    last_row = total_row[:, CHUNK - 1 : CHUNK]
    from_start = jnp.exp(total)
    to_end = jnp.exp(last_row - total)
    return dict(
        gq=gq, gk=gk, gv=gv, rq=rq, rk=rk, queries=queries, keys=keys, values=values, q_low=q_low, k_low=k_low,
        write=write, fade=fade, fade_strict=fade_strict, key_inner=key_inner, scores=dot_nt(q_low, k_low) * fade,
        lower=write * key_inner * fade_strict, from_start=from_start, to_end=to_end, last=jnp.exp(last_row),
        key_start=(write * from_start) * keys, q_start=queries * from_start, key_end=keys * to_end,
    )


def forward_kernel(heads_n, x_ref, wq_ref, wk_ref, wv_ref, wg_ref, wab_ref, cq_ref, ck_ref, cv_ref, heads_ref,
                   gain_ref, gated_ref, mixed_ref, delta_ref, solve_ref, state_ref, pq_ref, pk_ref, pv_ref, pg_ref,
                   xq_ref, xk_ref, xv_ref, ab_ref, turned):
    head = pl.program_id(0)

    @pl.when(head == 0)
    def _():
        turned[...] = dot_nn(x_ref[...], wab_ref[...]).T
        ab_ref[...] = turned[0:8, :]

    pq_ref[...] = dot_nn(x_ref[...], wq_ref[...])
    pk_ref[...] = dot_nn(x_ref[...], wk_ref[...])
    pv_ref[...] = dot_nn(x_ref[...], wv_ref[...])
    pg_ref[...] = dot_nn(x_ref[...], wg_ref[...])
    gain = gain_ref[0:1, :]
    write, _, _, _, totals = head_rates(turned, heads_ref, head, heads_n)
    cores = []
    for part in range(PARTS):
        span = pl.ds(part * CHUNK, CHUNK)
        xs = [convolve(ref, part, taps[...]) for ref, taps in ((pq_ref, cq_ref), (pk_ref, ck_ref), (pv_ref, cv_ref))]
        for ref, value in zip((xq_ref, xk_ref, xv_ref), xs):
            ref[span, :] = value
        cores.append(chunk_core(*xs, write[:, part * CHUNK : (part + 1) * CHUNK], totals[part : part + 1, :]))
    solves = invert_all([core["lower"] for core in cores])
    for part in range(PARTS):
        solve_ref[0, 0, part] = solves[part]
    value_parts = [dot_nn(t, (twice(c["write"]) * c["values"]).astype(BF16)) for t, c in zip(solves, cores)]
    key_parts = [dot_nn(t, c["key_start"].astype(BF16)).astype(BF16) for t, c in zip(solves, cores)]
    state = jnp.zeros((DK, DV), F32)
    for part in range(PARTS):
        core = cores[part]
        state_low = state.astype(BF16)
        state_ref[0, 0, part] = state_low
        update = value_parts[part] - dot_nn(key_parts[part], state_low)
        update_low = update.astype(BF16)
        mixed = dot_nn(core["q_start"].astype(BF16), state_low) + dot_nn(core["scores"].astype(BF16), update_low)
        if part < PARTS - 1:
            state = core["last"] * state + dot_tn(core["key_end"].astype(BF16), update_low)
        span = pl.ds(part * CHUNK, CHUNK)
        delta_ref[span, :] = update_low
        mixed_ref[span, :] = mixed.astype(BF16)
        factor = lax.rsqrt(jnp.mean(mixed * mixed, axis=1, keepdims=True) + 1e-05)
        gate_in = pg_ref[span, :]
        gated_ref[span, :] = (mixed * factor * gain * (gate_in * sigmoid(gate_in))).astype(BF16)


def backward_kernel(heads_n, resid_ref, wo_ref, cq_ref, ck_ref, cv_ref, heads_ref, gain_ref, mixed_ref, delta_ref,
                    solve_ref, state_ref, pq_ref, pk_ref, pv_ref, pg_ref, xq_ref, xk_ref, xv_ref, ab_ref, *refs):
    dp_ref, small_ref, grad_ref, turned = refs[-4:]
    head = pl.program_id(0)
    row, col = iota2(CHUNK, CHUNK, 0), iota2(CHUNK, CHUNK, 1)
    gain = gain_ref[0:1, :]
    width_k, width_v = heads_n * DK, heads_n * DV
    scale = 1.0 / math.sqrt(DK)

    def fold(x):
        return jnp.sum(x.reshape(CHUNK // 8, 8, x.shape[1]), axis=0)

    def down(x):
        return jnp.sum(x, axis=0, keepdims=True)

    @pl.when(head == 0)
    def _():
        turned[...] = jnp.zeros_like(turned)

    grad_ref[...] = dot_nn(resid_ref[...], wo_ref[...])
    write_row, decay_in, rate, soft, totals = head_rates(ab_ref, heads_ref, head, heads_n)
    state_grad = jnp.zeros((DK, DV), F32)
    gain_sum = jnp.zeros((8, DV), F32)
    taps_sum = {name: [jnp.zeros((8, size), F32) for _ in range(4)] for name, size in (("q", DK), ("k", DK), ("v", DV))}
    following = {"q": jnp.zeros((8, DK), F32), "k": jnp.zeros((8, DK), F32), "v": jnp.zeros((8, DV), F32)}
    rate_sum = jnp.zeros((1, CHUNK), F32)
    bias_sum = jnp.zeros((1, CHUNK), F32)
    suffix, which = tri(False), iota2(8, CHUNK, 0)
    for part in reversed(range(PARTS)):
        span = pl.ds(part * CHUNK, CHUNK)
        piece = slice(part * CHUNK, (part + 1) * CHUNK)
        xq, xk, xv = xq_ref[span, :], xk_ref[span, :], xv_ref[span, :]
        core = chunk_core(xq, xk, xv, write_row[:, piece], totals[part : part + 1, :])
        write, keys, queries, values = core["write"], core["keys"], core["queries"], core["values"]
        k_low, q_low, fade = core["k_low"], core["q_low"], core["fade"]
        solve, state_low, delta = solve_ref[0, 0, part], state_ref[0, 0, part], delta_ref[span, :]
        mixed = mixed_ref[span, :].astype(F32)
        factor = lax.rsqrt(jnp.mean(mixed * mixed, axis=1, keepdims=True) + 1e-05)
        normed = mixed * factor
        gate_in = pg_ref[span, :]
        gate_sig = sigmoid(gate_in)
        gate = gate_in * gate_sig
        grad = grad_ref[span, :]
        plain = grad * normed
        gain_sum = gain_sum + fold(plain * gate)
        dp_ref[span, pl.ds(pl.multiple_of(2 * width_k + width_v + head * DV, DV), DV)] = (
            plain * gain * (gate_sig + gate * (1.0 - gate_sig))
        ).astype(BF16)
        normed_grad = grad * gate * gain
        mixed_grad = factor * (normed_grad - normed * jnp.mean(normed_grad * normed, axis=1, keepdims=True))
        mixed_low = mixed_grad.astype(BF16)
        key_part = dot_nn(solve, core["key_start"].astype(BF16)).astype(BF16)
        grad_low = state_grad.astype(BF16)
        update_grad = dot_tn(core["scores"].astype(BF16), mixed_low) + dot_nn(core["key_end"].astype(BF16), grad_low)
        update_low = update_grad.astype(BF16)
        key_end_grad = dot_nt(delta, grad_low)
        last_grad = jnp.sum(state_low.astype(F32) * state_grad)
        if part > 0:
            state_grad = (
                core["last"] * state_grad
                + dot_tn(core["q_start"].astype(BF16), mixed_low)
                - dot_tn(key_part, update_low)
            )
        q_start_grad = dot_nt(mixed_low, state_low)
        scores_grad = dot_nt(mixed_low, delta)
        right_grad = dot_tn(solve, update_low)
        right_low = right_grad.astype(BF16)
        lower_grad = jnp.where(row > col, -dot_nt(right_low, delta), 0.0)
        key_start_grad = -dot_nt(right_low, state_low)
        inner_low = (scores_grad * fade).astype(BF16)
        queries_grad = q_start_grad * core["from_start"] + dot_nn(inner_low, k_low)
        faded_lower = lower_grad * core["fade_strict"]
        key_inner_grad = write * faded_lower
        both = (key_inner_grad + key_inner_grad.T).astype(BF16)
        keys_grad = (
            key_end_grad * core["to_end"]
            + key_start_grad * (write * core["from_start"])
            + dot_tn(inner_low, q_low)
            + dot_nn(both, k_low)
        )
        values_grad = twice(write) * right_grad
        start_keys = key_start_grad * core["from_start"] * keys
        value_terms = right_grad * values
        write_grad = down(
            (start_keys + faded_lower * core["key_inner"] + value_terms[:, :CHUNK] + value_terms[:, CHUNK:]).T
        )
        ends = key_end_grad * core["key_end"]
        gaps_grad = scores_grad * core["scores"] + lower_grad * core["lower"]
        total_grad = down((q_start_grad * core["q_start"] + write * start_keys - ends + gaps_grad).T) - down(gaps_grad)
        at_end = jnp.sum(ends) + last_grad * core["last"]
        decay_grad = exact_rows(jnp.broadcast_to(total_grad, (8, CHUNK)), suffix)[0:1, :] + at_end
        rate_sum = rate_sum + decay_grad * (rate * soft[:, piece])
        decay_in_grad = decay_grad * (rate * sigmoid(decay_in[:, piece]))
        bias_sum = bias_sum + decay_in_grad
        write_in_grad = write_grad * (write_row[:, piece] * (1.0 - write_row[:, piece]))
        held = jnp.where(which == head, decay_in_grad, turned[0:8, span])
        turned[0:8, span] = jnp.where(which == heads_n + head, write_in_grad, held)
        unit = queries * (1.0 / scale)
        sq_grad = (core["rq"] * scale) * (
            queries_grad - unit * jnp.sum(queries_grad * unit, axis=1, keepdims=True)
        )
        sk_grad = core["rk"] * (keys_grad - keys * jnp.sum(keys_grad * keys, axis=1, keepdims=True))
        for name, grad_in, x, sig, p_ref, taps_ref, start, size in (
            ("q", sq_grad, xq, core["gq"], pq_ref, cq_ref, 0, DK),
            ("k", sk_grad, xk, core["gk"], pk_ref, ck_ref, width_k, DK),
            ("v", values_grad, xv, core["gv"], pv_ref, cv_ref, 2 * width_k, DV),
        ):
            taps, rows = taps_ref[...], p_ref[span, :]
            x_grad = grad_in * (sig + x * sig * (1.0 - sig))
            longer = jnp.concatenate([x_grad, following[name]], axis=0)
            following[name] = x_grad[0:8, :]
            taps_sum[name][3] = taps_sum[name][3] + fold(rows * x_grad)
            proj = x_grad * taps[3:4, :]
            for tap in range(3):
                moved = longer[3 - tap : 3 - tap + CHUNK, :]
                taps_sum[name][tap] = taps_sum[name][tap] + fold(rows * moved)
                proj = proj + moved * taps[tap : tap + 1, :]
            dp_ref[span, pl.ds(pl.multiple_of(start + head * size, size), size)] = proj.astype(BF16)

    @pl.when(head == heads_n - 1)
    def _():
        dp_ref[:, pl.ds(2 * width_k + 2 * width_v, 128)] = turned[...].T.astype(BF16)

    lane = iota2(1, DV, 1)
    rates, biases = jnp.sum(rate_sum, axis=1, keepdims=True), jnp.sum(bias_sum, axis=1, keepdims=True)
    small = [down(taps_sum["v"][tap]) for tap in range(4)]
    small += [jnp.concatenate([down(taps_sum["q"][tap]), down(taps_sum["k"][tap])], axis=1) for tap in range(4)]
    small += [down(gain_sum), jnp.where(lane == 0, rates, 0.0) + jnp.where(lane == 1, biases, 0.0)]
    small += [jnp.zeros((6, DV), F32)]
    small_ref[0, 0] = jnp.concatenate(small, axis=0)


def param_specs():
    return [
        pl.BlockSpec((4, DK), lambda h: (0, h)),
        pl.BlockSpec((4, DK), lambda h: (0, h)),
        pl.BlockSpec((4, DV), lambda h: (0, h)),
        pl.BlockSpec((8, 128), lambda h: (0, 0)),
        pl.BlockSpec((1, DV), lambda h: (0, 0)),
    ]


def saved_specs():
    narrow, wide = pl.BlockSpec((LEN, DK), lambda h: (0, h)), pl.BlockSpec((LEN, DV), lambda h: (0, h))
    return [
        wide, wide,
        pl.BlockSpec((1, 1, PARTS, CHUNK, CHUNK), lambda h: (0, h, 0, 0, 0)),
        pl.BlockSpec((1, 1, PARTS, DK, DV), lambda h: (0, h, 0, 0, 0)),
        narrow, narrow, wide, wide, narrow, narrow, wide,
        pl.BlockSpec((8, LEN), lambda h: (0, 0)),
    ]


def mix_forward(normed, weights, seq, params):
    width, heads_n = normed.shape[1], params[0].shape[1] // DK
    col_q, col_v = heads_n * DV // DK, heads_n + 2 * heads_n * DK // DV

    def shape(*dims, kind=F32):
        return jax.ShapeDtypeStruct(dims, kind)

    low = shape(LEN, heads_n * DV, kind=BF16)
    narrow, wide = shape(LEN, heads_n * DK), shape(LEN, heads_n * DV)
    return pl.pallas_call(
        functools.partial(forward_kernel, heads_n),
        grid=(heads_n,),
        in_specs=[
            pl.BlockSpec((LEN, width), lambda h: (seq, 0)),
            pl.BlockSpec((width, DK), lambda h: (0, col_q + h)),
            pl.BlockSpec((width, DK), lambda h: (0, col_q + heads_n + h)),
            pl.BlockSpec((width, DV), lambda h: (0, col_v + h)),
            pl.BlockSpec((width, DV), lambda h: (0, col_v + heads_n + h)),
            pl.BlockSpec((width, 128), lambda h: (0, col_q + 6 * heads_n)),
        ] + param_specs(),
        out_specs=[pl.BlockSpec((LEN, DV), lambda h: (0, h))] + saved_specs(),
        out_shape=[
            low, low, low,
            shape(1, heads_n, PARTS, CHUNK, CHUNK, kind=BF16),
            shape(1, heads_n, PARTS, DK, DV, kind=BF16),
            narrow, narrow, wide, wide, narrow, narrow, wide,
            shape(8, LEN),
        ],
        scratch_shapes=[pltpu.VMEM((128, LEN), F32)],
        cost_estimate=pl.CostEstimate(flops=3 * 10**9 * heads_n, bytes_accessed=5 * 10**6 * heads_n, transcendentals=10**6),
        name="mix_forward",
    )(normed, *[weights] * 5, *params)


def mix_backward(resid, w_out, seq, params, saved, cols, earlier=None):
    heads_n, width = params[0].shape[1] // DK, resid.shape[1]
    held = [earlier] if earlier is not None else []
    return pl.pallas_call(
        functools.partial(backward_kernel, heads_n),
        grid=(heads_n,),
        in_specs=[pl.BlockSpec((LEN, width), lambda h: (0, 0)), pl.BlockSpec((width, DV), lambda h: (0, h))]
        + param_specs() + saved_specs() + [pl.BlockSpec(memory_space=pl.ANY)] * len(held),
        out_specs=[
            pl.BlockSpec((LEN, cols), lambda h: (seq, 0)),
            pl.BlockSpec((1, 1, 16, DV), lambda h: (0, h, 0, 0)),
        ],
        out_shape=[
            jax.ShapeDtypeStruct((2 * LEN, cols), BF16),
            jax.ShapeDtypeStruct((1, heads_n, 16, DV), F32),
        ],
        scratch_shapes=[pltpu.VMEM((LEN, DV), F32), pltpu.VMEM((128, LEN), F32)],
        input_output_aliases={19: 0} if held else {},
        cost_estimate=pl.CostEstimate(flops=5 * 10**9 * heads_n, bytes_accessed=6 * 10**6 * heads_n, transcendentals=10**6),
        name="mix_backward",
    )(resid, w_out, *params, *saved, *held)


def ffn_kernel(held, x_ref, cot_ref, mine_ref, other_ref, *refs):
    outs, (w_ref, part_sum, back_sum, sems) = refs[held : held + 8], refs[held + 8 :]
    part_ref, back_ref = outs[6], outs[7]
    units = w_ref.shape[2]
    copies = []
    for half, source in enumerate((mine_ref, other_ref)):
        for at in range(3):
            slot = 3 * half + at
            copies.append(
                pltpu.make_async_copy(source.at[:, pl.ds(at * units, units)], w_ref.at[slot], sems.at[slot])
            )
    for copy in copies:
        copy.start()
    for half in range(2):
        at = 3 * half
        copies[at].wait()
        gate = dot_nn(x_ref[...], w_ref[at])
        copies[at + 1].wait()
        up = dot_nn(x_ref[...], w_ref[at + 1])
        copies[at + 2].wait()
        grad = dot_nn(cot_ref[...], w_ref[at + 2])
        sig = sigmoid(gate)
        act = gate * sig
        outs[at][...] = (act * up).astype(BF16)
        outs[at + 1][...] = (grad * up * (sig + act * (1.0 - sig))).astype(BF16)
        outs[at + 2][...] = (grad * act).astype(BF16)
        part = dot_nt(outs[at][...], w_ref[at + 2])
        back = dot_nt(outs[at + 1][...], w_ref[at]) + dot_nt(outs[at + 2][...], w_ref[at + 1])
        if half == 0:
            part_sum[...] = part
            back_sum[...] = back
        else:
            part_ref[...] = (part_sum[...] + part).astype(part_ref.dtype)
            back_ref[...] = (back_sum[...] + back).astype(back_ref.dtype)


def ffn_both(x, cot, mine, other, seq, total, kind, earlier=None):
    rows, width = x.shape
    units = FF_HALF
    whole = pl.BlockSpec((rows, width), lambda i: (0, 0))
    anywhere = pl.BlockSpec(memory_space=pl.ANY)
    tiles = pl.BlockSpec((rows, units), lambda i: (seq, 0))
    held = list(earlier) if earlier else []
    return pl.pallas_call(
        functools.partial(ffn_kernel, len(held)),
        grid=(1,),
        in_specs=[whole, whole, anywhere, anywhere] + [anywhere] * len(held),
        out_specs=[tiles] * 6 + [whole, whole],
        out_shape=[jax.ShapeDtypeStruct((total, units), BF16)] * 6 + [jax.ShapeDtypeStruct((rows, width), kind)] * 2,
        input_output_aliases={4 + at: at for at in range(len(held))},
        scratch_shapes=[pltpu.VMEM((6, width, units), BF16)] + [pltpu.VMEM((rows, width), F32)] * 2
        + [pltpu.SemaphoreType.DMA((6,))],
        cost_estimate=pl.CostEstimate(flops=24 * rows * width * units, bytes_accessed=25 * 10**6, transcendentals=rows * units * 2),
        name="ffn_both",
    )(x, cot, mine, other, *held)


def late_kernel(plan, held, *refs):
    lefts, rights = refs[: plan[0]], refs[plan[0] : plan[0] + len(plan[1])]
    out_ref, turned = refs[-2], refs[-1]
    step = pl.program_id(0)
    for at, (right, (source, fresh)) in enumerate(zip(rights, plan[1])):

        @pl.when(step == at)
        def _(right=right, source=source, fresh=fresh):
            if fresh:
                turned[:, :LEN] = lefts[2 * source][...].T
                turned[:, LEN:] = lefts[2 * source + 1][...].T
            total = dot_nn(turned[...], right[...])
            if held:
                total = total + refs[plan[0] + len(plan[1])][...].astype(F32)
            out_ref[...] = total.astype(BF16)


def late_grads(normed, cot, units, came=None):
    hidden, grad_gate, grad_up = units
    rows, tile = hidden.shape
    width = cot[0].shape[1]
    lefts, rights = [*normed, *cot], [grad_gate, grad_up, hidden]
    plan = (4, ((0, True), (0, False), (1, True)))
    across = pl.BlockSpec((width, tile), lambda i: (0, i))
    held = [came] if came is not None else []
    return pl.pallas_call(
        functools.partial(late_kernel, plan, len(held)),
        grid=(3,),
        in_specs=[pl.BlockSpec((LEN, width), lambda i: (0, 0))] * 4 + [pl.BlockSpec((rows, tile), lambda i: (0, 0))] * 3
        + [across] * len(held),
        out_specs=across,
        out_shape=jax.ShapeDtypeStruct((width, 3 * tile), BF16),
        scratch_shapes=[pltpu.VMEM((width, rows), BF16)],
        cost_estimate=pl.CostEstimate(flops=6 * rows * width * tile, bytes_accessed=16 * 10**6, transcendentals=0),
        name="late_grads",
    )(*lefts, *rights, *held)


def mix_kernel(held, resid_s, resid_o, normed_ref, gated_s, gated_o, grad_ref, *refs):
    out_ref, split = refs[-1], gated_s.shape[1]
    first = dot_nn(resid_s[...].T, gated_s[...]) + dot_nn(resid_o[...].T, gated_o[...])
    second = dot_nn(normed_ref[...].T, grad_ref[...])
    if held:
        first = first + refs[0][:, :split].astype(F32)
        second = second + refs[0][:, split:].astype(F32)
    out_ref[:, :split] = first.astype(BF16)
    out_ref[:, split:] = second.astype(BF16)


def mix_grads(resid, gated, normed, grads, came=None):
    (rows, width), tile = normed.shape, 256
    cols = gated[0].shape[1] + grads.shape[1]
    down = pl.BlockSpec((tile, cols), lambda i: (i, 0))
    held = [came] if came is not None else []
    whole = [pl.BlockSpec(value.shape, lambda i: (0, 0)) for value in (*gated, grads)]
    return pl.pallas_call(
        functools.partial(mix_kernel, len(held)),
        grid=(width // tile,),
        in_specs=[pl.BlockSpec((LEN, tile), lambda i: (0, i))] * 2 + [pl.BlockSpec((rows, tile), lambda i: (0, i))]
        + whole + [down] * len(held),
        out_specs=down,
        out_shape=jax.ShapeDtypeStruct((width, cols), BF16),
        cost_estimate=pl.CostEstimate(flops=2 * rows * width * cols, bytes_accessed=14 * 10**6, transcendentals=0),
        name="mix_grads",
    )(*resid, normed, *gated, grads, *held)


def back_kernel(skip, mine_ref, other_ref, w0_ref, w1_ref, unit_ref, out_ref, low_ref, gain_ref):
    total = dot_nt(mine_ref[...], w0_ref[:, skip:]) + dot_nt(other_ref[...], w1_ref[:, skip:])
    out_ref[...] = total
    low_ref[...] = total.astype(BF16)
    gain_ref[...] = jnp.sum(total * unit_ref[...], axis=0, keepdims=True)


def back_rows(grads, weights, unit, seq):
    (width, all_cols), cols, tile = weights[0].shape, grads[0].shape[1], 256
    rows = pl.BlockSpec((LEN, cols), lambda i: (seq, 0))
    rights = pl.BlockSpec((tile, all_cols), lambda i: (i, 0))
    outs = pl.BlockSpec((LEN, tile), lambda i: (0, i))
    return pl.pallas_call(
        functools.partial(back_kernel, all_cols - cols),
        grid=(width // tile,),
        in_specs=[rows, rows, rights, rights, pl.BlockSpec((LEN, tile), lambda i: (seq, i))],
        out_specs=[outs, outs, pl.BlockSpec((1, tile), lambda i: (0, i))],
        out_shape=[
            jax.ShapeDtypeStruct((LEN, width), F32),
            jax.ShapeDtypeStruct((LEN, width), BF16),
            jax.ShapeDtypeStruct((1, width), F32),
        ],
        cost_estimate=pl.CostEstimate(flops=4 * LEN * width * cols, bytes_accessed=17 * 10**6, transcendentals=0),
        name="back_rows",
    )(*grads, *weights, unit)


def against_rows(left, right):
    return lax.dot_general(left, right, (((1,), (1,)), ((), ())), preferred_element_type=F32)


def row_factor(values):
    return lax.rsqrt(jnp.mean(values * values, axis=-1, keepdims=True) + 1e-05)


def norm_backward(normed, factor, gain, grad):
    inner = grad * gain
    return factor * (inner - normed * jnp.mean(inner * normed, axis=-1, keepdims=True))


SWAP = [(0, 1), (1, 0)]


def swap(value, axis):
    return lax.ppermute(value, axis, SWAP)


def after(value, other):
    return lax.optimization_barrier((value, other))[0]


def by_core(mine, other):
    first = lax.axis_index("core") == 0
    return jnp.where(first, mine, other), jnp.where(first, other, mine)


def own_half(parts):
    return by_core(parts[0], parts[1])


def halves(value):
    size = value.shape[-1] // 2
    return value[..., :size], value[..., size:]


def chip_rows(parts):
    mine, other = own_half(parts)
    return jnp.concatenate(by_core(mine, swap(other, "core")), axis=0)


def wide_halves(value, size):
    return tuple(jnp.pad(part, ((0, 0), (0, size - part.shape[1]))) for part in halves(value))


class Ring:
    def __init__(self, chips):
        self.chips = chips
        order = list(range(0, chips, 2)) + list(range(chips - 1, 0, -2))
        after = order[1:] + order[:1]
        self.ahead, self.back = list(zip(order, after)), list(zip(after, order))
        me = lax.axis_index("chip")
        self.place = jnp.where(me % 2 == 0, me // 2, chips - 1 - me // 2)

    def chip_at(self, offset):
        place = (self.place + offset + self.chips) % self.chips
        return jnp.where(place < self.chips // 2, 2 * place, 2 * (self.chips - 1 - place) + 1)

    def gather(self, piece, joined):
        rows = piece.shape[0]
        pieces, offsets = [piece], [0]
        up = down = piece
        steps = (self.chips - 1) // 2
        for step in range(1, steps + 1):
            up, down = lax.ppermute(up, "chip", self.ahead), lax.ppermute(down, "chip", self.back)
            up, down = lax.optimization_barrier((up, down))
            pieces += [up, down]
            offsets += [-step, step]
        far = self.chips // 2
        top = lax.ppermute(up[: rows // 2], "chip", self.ahead)
        bottom = lax.ppermute(down[rows // 2 :], "chip", self.back)
        pieces += lax.optimization_barrier((top, bottom))
        return joined(pieces, [self.chip_at(offset) for offset in offsets + [far]])

    def by_slices(self, pieces, places):
        rows, cols = pieces[0].shape
        full = jnp.zeros((self.chips, rows, cols), pieces[0].dtype)
        starts = [0] * (len(pieces) - 1) + [rows // 2]
        for value, place, start in zip(pieces, places + places[-1:], starts):
            full = lax.dynamic_update_slice(full, value[None], (place, start, 0))
        return full.reshape(-1, cols)

    def by_copies(self, pieces, places):
        rows, cols = pieces[0].shape
        count = len(pieces)

        def kernel(places_ref, *refs):
            out_ref, held, into, out = refs[count:]
            firsts = [at * rows for at in range(count - 1)] + [(count - 2) * rows + rows // 2]
            stages, results = [], []
            for at, ref in enumerate(refs[:count]):
                start = pl.multiple_of(places_ref[min(at, count - 2)] * rows, rows)
                if at == count - 1:
                    start = pl.multiple_of(start + rows // 2, rows // 2)
                slot = held.at[pl.ds(firsts[at], ref.shape[0]), :]
                stages.append(pltpu.make_async_copy(ref, slot, into.at[at]))
                results.append(pltpu.make_async_copy(slot, out_ref.at[pl.ds(start, ref.shape[0]), :], out.at[at]))
                stages[-1].start()
            for stage, result in zip(stages, results):
                stage.wait()
                result.start()
            for result in results:
                result.wait()

        return pl.pallas_call(
            kernel,
            grid_spec=pltpu.PrefetchScalarGridSpec(
                num_scalar_prefetch=1,
                grid=(1,),
                in_specs=[pl.BlockSpec(memory_space=pl.ANY)] * count,
                out_specs=pl.BlockSpec(memory_space=pl.ANY),
                scratch_shapes=[pltpu.VMEM((self.chips * rows, cols), pieces[0].dtype)]
                + [pltpu.SemaphoreType.DMA((count,))] * 2,
            ),
            out_shape=jax.ShapeDtypeStruct((self.chips * rows, cols), pieces[0].dtype),
            cost_estimate=pl.CostEstimate(flops=0, bytes_accessed=4 * self.chips * rows * cols, transcendentals=0),
            name="lay_out",
        )(jnp.stack(places), *pieces)

    def scatter_sum(self, values):
        split = [value.reshape(self.chips, -1, value.shape[1]) for value in values]

        def join(offset, came=None):
            parts = [lax.dynamic_index_in_dim(value, self.chip_at(offset), 0, keepdims=False) for value in split]
            total = sum(part.astype(F32) for part in parts)
            return total if came is None else total + came.astype(F32)

        far = self.chips // 2
        up, down = join(far).astype(BF16), join(1 - far).astype(BF16)
        sent = []
        for step in range(far - 1, 0, -1):
            up, down = lax.ppermute(up, "chip", self.ahead), lax.ppermute(down, "chip", self.back)
            up, down = lax.optimization_barrier((up, down))
            up = join(step, up).astype(BF16)
            if step > 1:
                down = join(1 - step, down).astype(BF16)
            sent.append(up)
        last = lax.ppermute(up, "chip", self.ahead)
        return (lambda ready: join(0, after(down, ready)) + after(last, ready).astype(F32)), sent


def owner_rows(value):
    value = value.astype(F32)
    rows = value.shape[0] // 2
    mine, other = own_half((value[:rows], value[rows:]))
    return by_core(mine, swap(other, "core"))


def all_sum(value, axis, size):
    step = size // 2
    while step:
        came = lax.ppermute(value, axis, [(at, at ^ step) for at in range(size)])
        value = value + came
        step = step // 2
    return value


def local(chips, *args):
    return layer(chips, *args)


def layer(chips, tokens, norm_gain1, w_query, w_key, w_value, w_gate, w_decay, w_write, conv_query, conv_key,
          conv_value, a_log, dt_bias, out_gain, w_out, norm_gain2, w_ffgate, w_ffup, w_ffdown, cotangent):
    ring = Ring(chips)
    heads_n = a_log.shape[0] // 2
    ff = w_ffgate.shape[1] // 2
    tokens_o = swap(tokens, "tensor")
    cot_o = swap(cotangent, "tensor")

    pad = jnp.zeros((w_query.shape[0], 128 - 2 * heads_n), BF16)
    mix_parts = [
        jnp.concatenate(list(parts) + [pad], axis=1)
        for parts in zip(*map(halves, (w_out.T, w_query, w_key, w_value, w_gate, w_decay, w_write)))
    ]
    ffn_rows = chip_rows([
        jnp.concatenate(parts, axis=1)
        for parts in zip(*(wide_halves(value, FF_HALF) for value in (w_ffgate, w_ffup, w_ffdown.T)))
    ])
    w_mix = [ring.gather(chip_rows(mix_parts), ring.by_slices)]
    w_mix.append(swap(w_mix[0], "core"))
    w_ffn = [ring.gather(after(ffn_rows, w_mix[0]), ring.by_copies)]
    w_ffn.append(swap(w_ffn[0], "core"))
    val_w = heads_n * DV

    tokens32 = jnp.concatenate([tokens, tokens_o], axis=0).astype(F32)
    factor1 = row_factor(tokens32)
    unit1 = tokens32 * factor1
    normed1 = (unit1 * norm_gain1).astype(BF16)
    gain = out_gain.reshape(1, -1)
    params = []
    sides = [own_half(halves(value)) for value in (conv_query, conv_key, conv_value, a_log, dt_bias)]
    for cq, ck, cv, rate, bias in zip(*sides):
        heads_in = jnp.pad(jnp.stack([rate, bias]), ((0, 6), (0, 128 - heads_n)))
        params.append((cq, ck, cv, heads_in, gain))

    mixed = {}

    def mix(normed, seq, side):
        mixed[seq, side] = mix_forward(normed, w_mix[side], seq, params[side])

    def out_part(seq):
        return against_rows(mixed[seq, 0][0], w_mix[0][:, :val_w]) + against_rows(mixed[seq, 1][0], w_mix[1][:, :val_w])

    mix(normed1, 1, 0)
    mix(after(normed1, mixed[1, 0][0]), 1, 1)
    part_o = out_part(1).astype(BF16)
    came_s = swap(part_o, "tensor")
    mix(after(normed1, part_o), 0, 0)
    mix(after(normed1, mixed[0, 0][0]), 0, 1)
    resid1 = tokens32[:LEN] + out_part(0) + came_s.astype(F32)
    factor2 = row_factor(resid1)
    unit2 = resid1 * factor2
    normed2_s = (unit2 * norm_gain2).astype(BF16)
    normed2_o = swap(normed2_s, "tensor")

    *units, part_s, back_s = ffn_both(normed2_s, cotangent, w_ffn[0], w_ffn[1], 0, 2 * LEN, F32)
    *units, part_low, back_low = ffn_both(normed2_o, cot_o, w_ffn[0], w_ffn[1], 1, 2 * LEN, BF16, units)
    grad_rows2 = back_s + swap(back_low, "tensor").astype(F32)
    normed2, cot = (normed2_s, after(normed2_o, back_low)), (cotangent, cot_o)
    late_sent = late_grads(normed2, cot, units[3:])
    late_came = swap(late_sent, "core")
    late_own = late_grads((normed2_s, after(normed2_o, late_sent)), cot, units[:3])
    grad_resid = cotangent.astype(F32) + norm_backward(unit2, factor2, norm_gain2, grad_rows2)
    resid_s = after(grad_resid.astype(BF16), late_own)
    resid_o = swap(resid_s, "tensor")
    resid_rows = (resid_s, resid_o)
    result = resid1 + part_s + swap(after(part_low, resid_o), "tensor").astype(F32)
    late_last, _ = ring.scatter_sum([late_own, late_came])

    cols = w_mix[0].shape[1] - val_w
    grad_proj, small = [None, None], [None, None]
    ready = late_own
    for step, (seq, side) in enumerate(((0, 1), (0, 0), (1, 1), (1, 0))):
        grad_proj[side], sums = mix_backward(
            after(resid_rows[seq], ready), w_mix[side], seq, params[side], mixed[seq, side][1:], cols,
            grad_proj[side]
        )
        ready = grad_proj[side]
        small[side] = sums if seq == 0 else small[side] + sums
        if step == 2:
            ready = mix_grads(resid_rows, (mixed[0, 1][0], mixed[1, 1][0]), normed1, grad_proj[1])
            mix_came = swap(ready, "core")
    mix_own = mix_grads(resid_rows, (mixed[0, 0][0], mixed[1, 0][0]), normed1, grad_proj[0], mix_came)
    mix_last, mix_sent = ring.scatter_sum([mix_own])
    late_sum = owner_rows(late_last(mix_own))
    grad_proj[0] = after(grad_proj[0], mix_own)

    _, back_sent, gain_o = back_rows(grad_proj, w_mix, unit1, 1)
    mix_sum = owner_rows(mix_last(back_sent))
    back_s, _, gain_s = back_rows(grad_proj, w_mix, unit1, 0)
    grad_gain1 = gain_o[0] + gain_s[0]
    came_back = swap(back_sent, "tensor")
    last_parts = (came_back, back_s, unit1[:LEN], factor1[:LEN])
    came_back, back_s, unit_s, factor_s, *_ = lax.optimization_barrier((*last_parts, *mix_sent[-1:]))
    grad_rows1 = back_s + came_back.astype(F32)
    grad_tokens = grad_resid + norm_backward(unit_s, factor_s, norm_gain1, grad_rows1)

    grad_gain2 = jnp.sum(grad_rows2 * unit2, axis=0)
    head_rows = jnp.concatenate(by_core(small[0][0], small[1][0]), axis=0)
    out_gain_row = jnp.sum(head_rows[:, 8], axis=0, keepdims=True)
    wide = jnp.concatenate(
        [grad_gain1.reshape(-1, DV), grad_gain2.reshape(-1, DV), out_gain_row, head_rows.reshape(-1, DV)], axis=0
    )
    wide = all_sum(all_sum(wide, "chip", chips), "core", 2)
    count = grad_gain1.shape[0] // DV
    gains = all_sum(wide[: 2 * count + 1], "tensor", 2)
    head_rows = wide[2 * count + 1 :].reshape(2 * heads_n, 16, DV)

    def taps(rows):
        return jnp.transpose(rows, (1, 0, 2)).reshape(4, -1)

    def columns(parts, start, size):
        return jnp.concatenate([part[:, start : start + size] for part in parts], axis=1)

    key_w = heads_n * DK
    at = [0, val_w, val_w + key_w, val_w + 2 * key_w, 2 * val_w + 2 * key_w, 3 * val_w + 2 * key_w]
    return (
        result.astype(BF16),
        grad_tokens,
        gains[:count].reshape(-1),
        columns(mix_sum, at[1], key_w),
        columns(mix_sum, at[2], key_w),
        columns(mix_sum, at[3], val_w),
        columns(mix_sum, at[4], val_w),
        columns(mix_sum, at[5], heads_n),
        columns(mix_sum, at[5] + heads_n, heads_n),
        taps(head_rows[:, 4:8, :DK]),
        taps(head_rows[:, 4:8, DK:]),
        taps(head_rows[:, :4]),
        head_rows[:, 9, 0],
        head_rows[:, 9, 1],
        gains[2 * count],
        columns(mix_sum, at[0], val_w).T,
        gains[count : 2 * count].reshape(-1),
        columns(late_sum, 0, ff),
        columns(late_sum, FF_HALF, ff),
        columns(late_sum, 2 * FF_HALF, ff).T,
    )


def solution(mesh):
    chips = mesh.shape["dp"] // 2
    inner = jax.sharding.Mesh(mesh.devices.reshape(chips, 2, -1), ("chip", "core", "tensor"))
    dp, rows, every = ("chip", "core"), P(("chip", "core", "tensor"), None), P()
    down, across, taps, head = P(dp, "tensor"), P("tensor", dp), P(None, "tensor"), P("tensor")
    return jax.shard_map(
        functools.partial(local, chips),
        mesh=inner,
        in_specs=(rows, every, down, down, down, down, down, down, taps, taps, taps, head, head, every, across, every,
                  down, down, across, rows),
        out_specs=(rows, rows, every, down, down, down, down, down, down, taps, taps, taps, head, head, every, across,
                   every, down, down, across),
        check_vma=False,
    )
```

time: 710 us -> 506 us (0.71)
  waiting for transfers between devices: 392 us -> 162 us
  Pallas kernels: 94.3 us -> 208 us
  matrix products: 98.6 us -> 12.4 us
  starting transfers between devices: 17.8 us -> 46.7 us
  local copies, waits for them, and re-layouts: 38.8 us -> 25.3 us
  between operations: 14.6 us -> 2.15 us
    all_gather x2 -> x0, waiting for transfers between devices: 151 us -> none  [gather_rows(): mine = lax.all_gather(shard, 'chip', axis=0, tiled=True)]
    ppermute x10 -> x35, waiting for transfers between devices: 26.9 us -> 151 us  [the longest x6 56.9 us: gather(): lax.ppermute(up, 'chip', self.ahead)]
    ppermute x14 -> x16, waiting for transfers between devices: 129 us -> 10.9 us  [swap(): return lax.ppermute(value, axis, SWAP)]
    pallas_call x2 -> x17, Pallas kernels: 94.3 us -> 208 us  [the longest x4 55.4 us: mix_backward(): pl.pallas_call(functools.partial(backward_kernel, heads_n), grid=(heads_n...]
    reduce_scatter x2 -> x0, waiting for transfers between devices: 85.3 us -> none  [the longest x1 85.3 us: local(): lax.psum_scatter(ffn_sum, 'chip', scatter_dimension=0, tiled=True)]
    dot_general x14 -> x0, matrix products: 70.8 us -> none  [the longest x4 41.4 us: matmul(): return jnp.dot(left, right, preferred_element_type=F32)]
    ppermute x10 -> x35, starting transfers between devices: 6.42 us -> 37.4 us  [the longest x6 8.01 us: gather(): lax.ppermute(up, 'chip', self.ahead)]
    dot_general x5 -> x4, matrix products: 27.8 us -> 12.4 us  [against_rows(): lax.dot_general(left, right, (((1,), (1,)), ((), ())), preferred_element_...]
  transfers between devices with their start and end apart: 28 -> 51, of which waited for: 21 -> 31; matrix products, arithmetic and copies ran while one was open for 16% -> 14% of each run, Pallas kernels for 5% -> 38%
where the time goes in v2:
time: 506 us; the launch traced here: 500 us
  Pallas kernels  208 us (41%)
  waiting for transfers between devices  162 us (32%)
  starting transfers between devices  46.7 us (9%)
  other arithmetic  43.4 us (9%)
  local copies, waits for them, and re-layouts  25.3 us (5%)
  matrix products  12.4 us (2%)
    ppermute x6, waiting for transfers between devices, gather(): lax.ppermute(up, 'chip', self.ahead)  56.9 us
    pallas_call x4, Pallas kernels, mix_backward(): pl.pallas_call(functools.partial(backward_kernel, heads_n), grid=(heads_n...  55.4 us
    pallas_call x4, Pallas kernels, mix_forward(): pl.pallas_call(functools.partial(forward_kernel, heads_n), grid=(heads_n,...  53 us
    ppermute x6, waiting for transfers between devices, scatter_sum(): lax.ppermute(up, 'chip', self.ahead)  41.4 us
    pallas_call x2, Pallas kernels, ffn_both(): pl.pallas_call(functools.partial(ffn_kernel, len(held)), grid=(1,), in_sp...  34.4 us
    ppermute x5, waiting for transfers between devices, all_sum(): came = lax.ppermute(value, axis, [(at, at ^ step) for at in range(size)])  24.6 us
    pallas_call x2, Pallas kernels, late_grads(): pl.pallas_call(functools.partial(late_kernel, plan, len(held)), grid=(3,)...  21.3 us
    pallas_call x2, Pallas kernels, mix_grads(): pl.pallas_call(functools.partial(mix_kernel, len(held)), grid=(width // t...  20.2 us
  transfers between devices with their start and end apart: 51, of which 31 were waited for; matrix products, arithmetic and copies ran while one was open for 14% of the time, Pallas kernels for 38%

profile of v2, /device:TPU:0, one launch (start us, length us, event | category | flops | bytes accessed | tf_op | source)
XLA Modules:
  0.0 500.1 jit_solution(10570967757812679322)
XLA Ops:
  14.4 9.0 %collective-permute-done.2 = bf16[128,2176]{1,0:T(8,128)(2,1)S(1)} collective-permute-done((bf16[128,2176]{1,0:T(8,128)(2,1)S(1)}, bf16[128,2176]{1,0:T(8,128)(2,1)S(1)}, u32[]{:S(2)}, u32[]{:S(2)}) %collective-permute-start.2) | collective-permute-done | bytes 557088 | tf_op jit(solution)/shard_map/ppermute | solution.py:642
  28.7 9.8 %collective-permute-done.4 = bf16[128,2176]{1,0:T(8,128)(2,1)S(1)} collective-permute-done((bf16[128,2176]{1,0:T(8,128)(2,1)S(1)}, bf16[128,2176]{1,0:T(8,128)(2,1)S(1)}, u32[]{:S(2)}, u32[]{:S(2)}) %collective-permute-start.4) | collective-permute-done | bytes 557088 | tf_op jit(solution)/shard_map/ppermute | solution.py:642
  43.5 8.7 %collective-permute-done.6 = bf16[128,2176]{1,0:T(8,128)(2,1)S(1)} collective-permute-done((bf16[128,2176]{1,0:T(8,128)(2,1)S(1)}, bf16[128,2176]{1,0:T(8,128)(2,1)S(1)}, u32[]{:S(2)}, u32[]{:S(2)}) %collective-permute-start.6) | collective-permute-done | bytes 557088 | tf_op jit(solution)/shard_map/ppermute | solution.py:642
  67.9 12.2 %collective-permute-done.13.refs_1_ = bf16[128,2304]{1,0:T(8,128)(2,1)S(1)} collective-permute-done((bf16[128,2304]{1,0:T(8,128)(2,1)S(1)}, bf16[128,2304]{1,0:T(8,128)(2,1)S(1)}, u32[]{:S(2)}, u32[]{:S(2)}) %collective-permute-start.13) | collective-permute-done | bytes 589856 | tf_op jit(solution)/shard_map/ppermute | solution.py:642
  84.7 10.5 %collective-permute-done.15.refs_3_ = bf16[128,2304]{1,0:T(8,128)(2,1)} collective-permute-done((bf16[128,2304]{1,0:T(8,128)(2,1)S(1)}, bf16[128,2304]{1,0:T(8,128)(2,1)}, u32[]{:S(2)}, u32[]{:S(2)}) %collective-permute-start.15) | collective-permute-done | bytes 589856 | tf_op jit(solution)/shard_map/ppermute | solution.py:642
  102.5 6.8 %collective-permute-done.17.refs_5_ = bf16[128,2304]{1,0:T(8,128)(2,1)S(1)} collective-permute-done((bf16[128,2304]{1,0:T(8,128)(2,1)}, bf16[128,2304]{1,0:T(8,128)(2,1)S(1)}, u32[]{:S(2)}, u32[]{:S(2)}) %collective-permute-start.17) | collective-permute-done | bytes 589856 | tf_op jit(solution)/shard_map/ppermute | solution.py:642
  118.9 4.7 lay_out.1.mine_ref
  126.9 13.6 %mix_forward.4 = (bf16[512,512]{1,0:T(8,128)(2,1)}, bf16[512,512]{1,0:T(8,128)(2,1)}, bf16[512,512]{1,0:T(8,128)(2,1)}, bf16[1,2,4,128,128]{4,3,2,1,0:T(8,128)(2...) custom-call(bf16[1024,1024]{1,0:T(8,128)(2,1)} %get-tuple-element.16, ...), custom_call_target="tpu_custom_call" | custom-call | flops 6000000000 | bytes 10000000 | tf_op jit(solution)/shard_map/mix_forward/pallas_call | solution.py:377
  142.6 13.1 %mix_forward.5 = (bf16[512,512]{1,0:T(8,128)(2,1)}, bf16[512,512]{1,0:T(8,128)(2,1)}, bf16[512,512]{1,0:T(8,128)(2,1)}, bf16[1,2,4,128,128]{4,3,2,1,0:T(8,128)(2...) custom-call(bf16[1024,1024]{1,0:T(8,128)(2,1)} %get-tuple-element.16, ...), custom_call_target="tpu_custom_call" | custom-call | flops 6000000000 | bytes 10000000 | tf_op jit(solution)/shard_map/mix_forward/pallas_call | solution.py:377
  160.4 13.1 %mix_forward.6 = (bf16[512,512]{1,0:T(8,128)(2,1)}, bf16[512,512]{1,0:T(8,128)(2,1)}, bf16[512,512]{1,0:T(8,128)(2,1)}, bf16[1,2,4,128,128]{4,3,2,1,0:T(8,128)(2...) custom-call(bf16[1024,1024]{1,0:T(8,128)(2,1)} %get-tuple-element.16, ...), custom_call_target="tpu_custom_call" | custom-call | flops 6000000000 | bytes 10000000 | tf_op jit(solution)/shard_map/mix_forward/pallas_call | solution.py:377
  176.9 13.3 %mix_forward.7 = (bf16[512,512]{1,0:T(8,128)(2,1)}, bf16[512,512]{1,0:T(8,128)(2,1)}, bf16[512,512]{1,0:T(8,128)(2,1)}, bf16[1,2,4,128,128]{4,3,2,1,0:T(8,128)(2...) custom-call(bf16[1024,1024]{1,0:T(8,128)(2,1)} %get-tuple-element.16, ...), custom_call_target="tpu_custom_call" | custom-call | flops 6000000000 | bytes 10000000 | tf_op jit(solution)/shard_map/mix_forward/pallas_call | solution.py:377
  190.2 3.6 multiply_reduce_fusion.4
  195.1 17.3 %ffn_both.2 = (bf16[1024,768]{1,0:T(8,128)(2,1)}, bf16[1024,768]{1,0:T(8,128)(2,1)}, bf16[1024,768]{1,0:T(8,128)(2,1)}, bf16[1024,768]{1,0:T(8,128)(2,1)}, bf16[...) custom-call(bf16[512,1024]{1,0:T(8,128)(2,1)} %copy-done.10, ...), custom_call_target="tpu_custom_call" | custom-call | flops 9663676416 | bytes 25000000 | tf_op jit(solution)/shard_map/ffn_both/pallas_call | solution.py:468
  212.4 7.2 %collective-permute-done.22.x_ref.refs_1_ = bf16[512,1024]{1,0:T(8,128)(2,1)} collective-permute-done((bf16[512,1024]{1,0:T(8,128)(2,1)S(1)}, bf16[512,1024]{1,0:T(8,128)(2,1)}, u32[]{:S(2)}, u32[]{:S(2)}) %collective-permute-start.22) | collective-permute-done | bytes 1048608 | tf_op jit(solution)/shard_map/ppermute | solution.py:593
  219.6 17.1 %ffn_both.3 = (bf16[1024,768]{1,0:T(8,128)(2,1)}, bf16[1024,768]{1,0:T(8,128)(2,1)}, bf16[1024,768]{1,0:T(8,128)(2,1)}, bf16[1024,768]{1,0:T(8,128)(2,1)}, bf16[...) custom-call(bf16[512,1024]{1,0:T(8,128)(2,1)} %collective-permute-do, ...), custom_call_target="tpu_custom_call", output_to_operand_aliasing={{0}: (4, {}), {1}: (5, {}), {2}: (6, {}), {3}: (7, {}), {4}... | custom-call | flops 9663676416 | bytes 25000000 | tf_op jit(solution)/shard_map/ffn_both/pallas_call | solution.py:468
  237.3 10.9 %late_grads.2 = bf16[1024,2304]{1,0:T(8,128)(2,1)} custom-call(bf16[512,1024]{1,0:T(8,128)(2,1)} %copy-done.10, bf16[512,1024]{1,0:T(8,128)(2,1)} %collective-permute-done.22.x_ref.refs_1_, bf16[512,1024]{1,0:T(8,128)(2,1)} %refs_2_.3, bf16[512,1024]{1,0:T(8,128)(2,1)} %collective-permute-done.23.cot_ref.refs_3_, ...), custom_call_target="tpu_custom_call" | custom-call | flops 4831838208 | bytes 16000000 | tf_op jit(solution)/shard_map/late_grads/pallas_call | solution.py:507
  248.2 10.4 %late_grads.3 = bf16[1024,2304]{1,0:T(8,128)(2,1)} custom-call(bf16[512,1024]{1,0:T(8,128)(2,1)} %copy-done.10, bf16[512,1024]{1,0:T(8,128)(2,1)} %collective-permute-done.22.x_ref.refs_1_, bf16[512,1024]{1,0:T(8,128)(2,1)} %refs_2_.3, bf16[512,1024]{1,0:T(8,128)(2,1)} %collective-permute-done.23.cot_ref.refs_3_, ...), custom_call_target="tpu_custom_call" | custom-call | flops 4831838208 | bytes 16000000 | tf_op jit(solution)/shard_map/late_grads/pallas_call | solution.py:507
  264.1 3.7 fusion.34
  268.8 13.9 %mix_backward.4 = (bf16[1024,1664]{1,0:T(8,128)(2,1)}, f32[1,2,16,256]{3,2,1,0:T(8,128)}) custom-call(bf16[512,1024]{1,0:T(8,128)(2,1)} %copy-done.5, bf16[1024,2176]{1,0:T(8,128)(2,1)} %collective-permute-done.10.wq_ref.wk_ref.wv_ref.wg_ref.wab_ref.wo_ref.w1_ref, f32[4,256]{1,0:T(4,128)} %get-tuple-element.446.cq_ref, f32[4,256]{1,0:T(4,128)} %get-tuple-element.424.ck_ref, ...), custom_call_target="tpu_custom_call" | custom-call | flops 10000000000 | bytes 12000000 | tf_op jit(solution)/shard_map/mix_backward/pallas_call | solution.py:405
  282.7 13.7 %mix_backward.5 = (bf16[1024,1664]{1,0:T(8,128)(2,1)}, f32[1,2,16,256]{3,2,1,0:T(8,128)}) custom-call(bf16[512,1024]{1,0:T(8,128)(2,1)} %copy-done.5, bf16[1024,2176]{1,0:T(8,128)(2,1)} %bitcast.10.wq_ref.wk_ref.wv_ref.wg_ref.wab_ref.wo_ref.w0_ref, f32[4,256]{1,0:T(4,128)} %get-tuple-element.445.cq_ref, f32[4,256]{1,0:T(4,128)} %get-tuple-element.425.ck_ref, ...), custom_call_target="tpu_custom_call" | custom-call | flops 10000000000 | bytes 12000000 | tf_op jit(solution)/shard_map/mix_backward/pallas_call | solution.py:405
  296.3 14.0 %mix_backward.6 = (bf16[1024,1664]{1,0:T(8,128)(2,1)}, f32[1,2,16,256]{3,2,1,0:T(8,128)}) custom-call(bf16[512,1024]{1,0:T(8,128)(2,1)} %collective-permute-done.25.resid_ref.resid_o, bf16[1024,2176]{1,0:T(8,128)(2,1)} %collective-permute-done.10.wq_ref.wk_ref.wv_ref.wg_ref.wab_ref.wo_ref.w1_ref, ...), custom_call_target="tpu_custom_call", output_to_operand_aliasing={{0}: (19, {})} | custom-call | flops 10000000000 | bytes 12000000 | tf_op jit(solution)/shard_map/mix_backward/pallas_call | solution.py:405
  310.3 9.7 %mix_grads.2 = bf16[1024,2176]{1,0:T(8,128)(2,1)} custom-call(bf16[512,1024]{1,0:T(8,128)(2,1)} %copy-done.5, bf16[512,1024]{1,0:T(8,128)(2,1)} %collective-permute-done.25.resid_ref.resid_o, bf16[1024,1024]{1,0:T(8,128)(2,1)} %get-tuple-element.162.x_ref.normed_ref, bf16[512,512]{1,0:T(8,128)(2,1)} %get-tuple-element.163.gated_s, ...), custom_call_target="tpu_custom_call" | custom-call | flops 4563402752 | bytes 14000000 | tf_op jit(solution)/shard_map/mix_grads/pallas_call | solution.py:537
  329.2 9.7 %collective-permute-done.43 = bf16[128,2304]{1,0:T(8,128)(2,1)} collective-permute-done((bf16[128,2304]{1,0:T(8,128)(2,1)}, bf16[128,2304]{1,0:T(8,128)(2,1)}, u32[]{:S(2)}, u32[]{:S(2)}) %collective-permute-start.43) | collective-permute-done | bytes 589856 | tf_op jit(solution)/shard_map/ppermute | solution.py:709
  344.9 13.9 %mix_backward.7 = (bf16[1024,1664]{1,0:T(8,128)(2,1)}, f32[1,2,16,256]{3,2,1,0:T(8,128)}) custom-call(bf16[512,1024]{1,0:T(8,128)(2,1)} %collective-permute-done.25.resid_ref.resid_o, bf16[1024,2176]{1,0:T(8,128)(2,1)} %bitcast.10.wq_ref.wk_ref.wv_ref.wg_ref.wab_ref.wo_ref.w0_ref, ...), custom_call_target="tpu_custom_call", output_to_operand_aliasing={{0}: (19, {})} | custom-call | flops 10000000000 | bytes 12000000 | tf_op jit(solution)/shard_map/mix_backward/pallas_call | solution.py:405
  359.7 10.5 %mix_grads.3 = bf16[1024,2176]{1,0:T(8,128)(2,1)} custom-call(bf16[512,1024]{1,0:T(8,128)(2,1)} %copy-done.5, bf16[512,1024]{1,0:T(8,128)(2,1)} %collective-permute-done.25.resid_ref.resid_o, bf16[1024,1024]{1,0:T(8,128)(2,1)} %get-tuple-element.162.x_ref.normed_ref, bf16[512,512]{1,0:T(8,128)(2,1)} %get-tuple-element.161.gated_s, ...), custom_call_target="tpu_custom_call" | custom-call | flops 4563402752 | bytes 14000000 | tf_op jit(solution)/shard_map/mix_grads/pallas_call | solution.py:537
  370.2 9.7 %back_rows.2 = (f32[512,1024]{1,0:T(8,128)}, bf16[512,1024]{1,0:T(8,128)(2,1)}, f32[1,1024]{1,0:T(1,128)}) custom-call(bf16[1024,1664]{1,0:T(8,128)(2,1)} %get-tuple-element.249.grad_ref.mine_ref, bf16[1024,1664]{1,0:T(8,128)(2,1)} %get-tuple-element.234.grad_ref.other_ref, bf16[1024,2176]{1,0:T(8,128)(2,1)} %bitcast.10.wq_ref.wk_ref.wv_ref.wg_ref.wab_ref.wo_ref.w0_ref, ...), custom_call_target="tpu_custom_call" | custom-call | flops 3489660928 | bytes 17000000 | tf_op jit(solution)/shard_map/back_rows/pallas_call | solution.py:561
  379.9 9.7 %back_rows.3 = (f32[512,1024]{1,0:T(8,128)}, bf16[512,1024]{1,0:T(8,128)(2,1)}, f32[1,1024]{1,0:T(1,128)}) custom-call(bf16[1024,1664]{1,0:T(8,128)(2,1)} %get-tuple-element.249.grad_ref.mine_ref, bf16[1024,1664]{1,0:T(8,128)(2,1)} %get-tuple-element.234.grad_ref.other_ref, bf16[1024,2176]{1,0:T(8,128)(2,1)} %bitcast.10.wq_ref.wk_ref.wv_ref.wg_ref.wab_ref.wo_ref.w0_ref, ...), custom_call_target="tpu_custom_call" | custom-call | flops 3489660928 | bytes 17000000 | tf_op jit(solution)/shard_map/back_rows/pallas_call | solution.py:561
  400.6 8.5 %collective-permute-done.47 = bf16[128,2304]{1,0:T(8,128)(2,1)S(1)} collective-permute-done((bf16[128,2304]{1,0:T(8,128)(2,1)S(1)}, bf16[128,2304]{1,0:T(8,128)(2,1)S(1)}, u32[]{:S(2)}, u32[]{:S(2)}) %collective-permute-start.47) | collective-permute-done | bytes 589856 | tf_op jit(solution)/shard_map/ppermute | solution.py:709
  423.8 21.3 %collective-permute-done.39 = f32[9,256]{1,0:T(8,128)S(1)} collective-permute-done((f32[9,256]{1,0:T(8,128)S(1)}, f32[9,256]{1,0:T(8,128)S(1)}, u32[]{:S(2)}, u32[]{:S(2)}) %collective-permute-start.39) | collective-permute-done | bytes 9248 | tf_op jit(solution)/shard_map/ppermute | solution.py:729
  451.2 12.8 %collective-permute-done.31 = bf16[128,2176]{1,0:T(8,128)(2,1)S(1)} collective-permute-done((bf16[128,2176]{1,0:T(8,128)(2,1)S(1)}, bf16[128,2176]{1,0:T(8,128)(2,1)S(1)}, u32[]{:S(2)}, u32[]{:S(2)}) %collective-permute-start.31) | collective-permute-done | bytes 557088 | tf_op jit(solution)/shard_map/ppermute | solution.py:709
  468.3 10.3 %collective-permute-done.33 = bf16[128,2176]{1,0:T(8,128)(2,1)S(1)} collective-permute-done((bf16[128,2176]{1,0:T(8,128)(2,1)S(1)}, bf16[128,2176]{1,0:T(8,128)(2,1)S(1)}, u32[]{:S(2)}, u32[]{:S(2)}) %collective-permute-start.33) | collective-permute-done | bytes 557088 | tf_op jit(solution)/shard_map/ppermute | solution.py:709
  481.1 10.8 %collective-permute-done.40 = bf16[128,2176]{1,0:T(8,128)(2,1)S(1)} collective-permute-done((bf16[128,2176]{1,0:T(8,128)(2,1)S(1)}, bf16[128,2176]{1,0:T(8,128)(2,1)S(1)}, u32[]{:S(2)}, u32[]{:S(2)}) %collective-permute-start.40) | collective-permute-done | bytes 557088 | tf_op jit(solution)/shard_map/ppermute | solution.py:715
  (272 shorter events, 144.7 us)
Async XLA Ops:
  7.5 15.8 %collective-permute-start.2 = (bf16[128,2176]{1,0:T(8,128)(2,1)S(1)}, bf16[128,2176]{1,0:T(8,128)(2,1)S(1)}, u32[]{:S(2)}, u32[]{:S(2)}) collective-permute-start(bf16[128,2176]{1,0:T(8,128)(2,1)S(1)} %pad_maximum_fusion.1), channel_id=1, source_target_pairs={{0,8},{8,16},{16,24},{24,28},{28,20},{20,12},{12,4},{4,0},{1,9},{9... | collective-permute-start | bytes 1671176 | tf_op jit(solution)/shard_map/ppermute | solution.py:642
  10.5 14.4 %collective-permute-start.3 = (bf16[128,2176]{1,0:T(8,128)(2,1)S(1)}, bf16[128,2176]{1,0:T(8,128)(2,1)S(1)}, u32[]{:S(2)}, u32[]{:S(2)}) collective-permute-start(bf16[128,2176]{1,0:T(8,128)(2,1)S(1)} %pad_maximum_fusion.1), channel_id=1, source_target_pairs={{8,0},{16,8},{24,16},{28,24},{20,28},{12,20},{4,12},{0,4},{9,1},{1... | collective-permute-start | bytes 1671176 | tf_op jit(solution)/shard_map/ppermute | solution.py:642
  10.6 52.5 %collective-permute-start.12 = (bf16[64,2304]{1,0:T(8,128)(2,1)S(1)}, bf16[64,2304]{1,0:T(8,128)(2,1)}, u32[]{:S(2)}, u32[]{:S(2)}) collective-permute-start(bf16[64,2304]{1,0:T(8,128)(2,1)S(1)} %broadcast_select_fusion.4), channel_id=1, source_target_pairs={{0,2},{2,0},{1,3},{3,1},{4,6},{6,4},{5,7},{7,5},{8,10},{10,8},{9,1... | collective-permute-start | bytes 884744 | tf_op jit(solution)/shard_map/ppermute | solution.py:593
  63.1 79.5 %collective-permute-start.10 = (bf16[1024,2176]{1,0:T(8,128)(2,1)}, bf16[1024,2176]{1,0:T(8,128)(2,1)}, u32[]{:S(2)}, u32[]{:S(2)}) collective-permute-start(bf16[1024,2176]{1,0:T(8,128)(2,1)} %bitcast.10.wq_ref.wk_ref.wv_ref.wg_ref.wab_ref.wo_ref.w0_ref), channel_id=1, source_target_pairs={{0,2},{2,0},{1,3},{3,1},{4,6},{6,4},{5,7},{7,5},{8,10},{10,8},{9,1... | collective-permute-start | bytes 13369352 | tf_op jit(solution)/shard_map/ppermute | solution.py:593
  64.3 15.8 %collective-permute-start.13 = (bf16[128,2304]{1,0:T(8,128)(2,1)S(1)}, bf16[128,2304]{1,0:T(8,128)(2,1)S(1)}, u32[]{:S(2)}, u32[]{:S(2)}) collective-permute-start(bf16[128,2304]{1,0:T(8,128)(2,1)S(1)} %pad_maximum_fusion.refs_0_), channel_id=1, source_target_pairs={{0,8},{8,16},{16,24},{24,28},{28,20},{20,12},{12,4},{4,0},{1,9},{9... | collective-permute-start | bytes 1769480 | tf_op jit(solution)/shard_map/ppermute | solution.py:642
  65.0 15.5 %collective-permute-start.14 = (bf16[128,2304]{1,0:T(8,128)(2,1)S(1)}, bf16[128,2304]{1,0:T(8,128)(2,1)S(1)}, u32[]{:S(2)}, u32[]{:S(2)}) collective-permute-start(bf16[128,2304]{1,0:T(8,128)(2,1)S(1)} %pad_maximum_fusion.refs_0_), channel_id=1, source_target_pairs={{8,0},{16,8},{24,16},{28,24},{20,28},{12,20},{4,12},{0,4},{9,1},{1... | collective-permute-start | bytes 1769480 | tf_op jit(solution)/shard_map/ppermute | solution.py:642
  66.3 33.6 %collective-permute-start = (bf16[512,1024]{1,0:T(8,128)(2,1)S(1)}, bf16[512,1024]{1,0:T(8,128)(2,1)S(1)}, u32[]{:S(2)}, u32[]{:S(2)}) collective-permute-start(bf16[512,1024]{1,0:T(8,128)(2,1)S(1)} %copy-done.1), channel_id=1, source_target_pairs={{0,1},{1,0},{2,3},{3,2},{4,5},{5,4},{6,7},{7,6},{8,9},{9,8},{10,11... | collective-permute-start | bytes 3145736 | tf_op jit(solution)/shard_map/ppermute | solution.py:593
  80.5 14.7 %collective-permute-start.15 = (bf16[128,2304]{1,0:T(8,128)(2,1)S(1)}, bf16[128,2304]{1,0:T(8,128)(2,1)}, u32[]{:S(2)}, u32[]{:S(2)}) collective-permute-start(bf16[128,2304]{1,0:T(8,128)(2,1)S(1)} %collective-permute-done.13.refs_1_), channel_id=1, source_target_pairs={{0,8},{8,16},{16,24},{24,28},{28,20},{20,12},{12,4},{4,0},{1,9},{9... | collective-permute-start | bytes 1769480 | tf_op jit(solution)/shard_map/ppermute | solution.py:642
  81.0 14.5 %collective-permute-start.16 = (bf16[128,2304]{1,0:T(8,128)(2,1)S(1)}, bf16[128,2304]{1,0:T(8,128)(2,1)}, u32[]{:S(2)}, u32[]{:S(2)}) collective-permute-start(bf16[128,2304]{1,0:T(8,128)(2,1)S(1)} %collective-permute-done.14.refs_2_), channel_id=1, source_target_pairs={{8,0},{16,8},{24,16},{28,24},{20,28},{12,20},{4,12},{0,4},{9,1},{1... | collective-permute-start | bytes 1769480 | tf_op jit(solution)/shard_map/ppermute | solution.py:642
  82.5 129.9 %collective-permute-start.23 = (bf16[512,1024]{1,0:T(8,128)(2,1)}, bf16[512,1024]{1,0:T(8,128)(2,1)}, u32[]{:S(2)}, u32[]{:S(2)}) collective-permute-start(bf16[512,1024]{1,0:T(8,128)(2,1)} %refs_2_.3), channel_id=1, source_target_pairs={{0,1},{1,0},{2,3},{3,2},{4,5},{5,4},{6,7},{7,6},{8,9},{9,8},{10,11... | collective-permute-start | bytes 3145736 | tf_op jit(solution)/shard_map/ppermute | solution.py:593
  123.6 71.2 %collective-permute-start.21 = (bf16[1024,2304]{1,0:T(8,128)(2,1)}, bf16[1024,2304]{1,0:T(8,128)(2,1)}, u32[]{:S(2)}, u32[]{:S(2)}) collective-permute-start(bf16[1024,2304]{1,0:T(8,128)(2,1)} %lay_out.1.mine_ref), channel_id=1, source_target_pairs={{0,2},{2,0},{1,3},{3,1},{4,6},{6,4},{5,7},{7,5},{8,10},{10,8},{9,1... | collective-permute-start | bytes 14155784 | tf_op jit(solution)/shard_map/ppermute | solution.py:593
  158.8 31.4 %collective-permute-start.11 = (bf16[512,1024]{1,0:T(8,128)(2,1)}, bf16[512,1024]{1,0:T(8,128)(2,1)S(1)}, u32[]{:S(2)}, u32[]{:S(2)}) collective-permute-start(bf16[512,1024]{1,0:T(8,128)(2,1)} %add_convert_fusion.1), channel_id=1, source_target_pairs={{0,1},{1,0},{2,3},{3,2},{4,5},{5,4},{6,7},{7,6},{8,9},{9,8},{10,11... | collective-permute-start | bytes 3145736 | tf_op jit(solution)/shard_map/ppermute | solution.py:593
  194.2 25.4 %collective-permute-start.22 = (bf16[512,1024]{1,0:T(8,128)(2,1)S(1)}, bf16[512,1024]{1,0:T(8,128)(2,1)}, u32[]{:S(2)}, u32[]{:S(2)}) collective-permute-start(bf16[512,1024]{1,0:T(8,128)(2,1)S(1)} %multiply_convert_fusion.1.x_ref.refs_0_), channel_id=1, source_target_pairs={{0,1},{1,0},{2,3},{3,2},{4,5},{5,4},{6,7},{7,6},{8,9},{9,8},{10,11... | collective-permute-start | bytes 3145736 | tf_op jit(solution)/shard_map/ppermute | solution.py:593
  236.7 24.7 %collective-permute-start.24 = (bf16[512,1024]{1,0:T(8,128)(2,1)}, bf16[512,1024]{1,0:T(8,128)(2,1)S(1)}, u32[]{:S(2)}, u32[]{:S(2)}) collective-permute-start(bf16[512,1024]{1,0:T(8,128)(2,1)} %get-tuple-element.182), channel_id=1, source_target_pairs={{0,1},{1,0},{2,3},{3,2},{4,5},{5,4},{6,7},{7,6},{8,9},{9,8},{10,11... | collective-permute-start | bytes 3145736 | tf_op jit(solution)/shard_map/ppermute | solution.py:593
  248.2 71.8 %collective-permute-start.42 = (bf16[1024,2304]{1,0:T(8,128)(2,1)}, bf16[1024,2304]{1,0:T(8,128)(2,1)}, u32[]{:S(2)}, u32[]{:S(2)}) collective-permute-start(bf16[1024,2304]{1,0:T(8,128)(2,1)} %late_grads.2), channel_id=1, source_target_pairs={{0,2},{2,0},{1,3},{3,1},{4,6},{6,4},{5,7},{7,5},{8,10},{10,8},{9,1... | collective-permute-start | bytes 14155784 | tf_op jit(solution)/shard_map/ppermute | solution.py:593
  267.8 28.5 %collective-permute-start.25 = (bf16[512,1024]{1,0:T(8,128)(2,1)S(1)}, bf16[512,1024]{1,0:T(8,128)(2,1)}, u32[]{:S(2)}, u32[]{:S(2)}) collective-permute-start(bf16[512,1024]{1,0:T(8,128)(2,1)S(1)} %get-tuple-element.207.resid_ref.resid_s), channel_id=1, source_target_pairs={{0,1},{1,0},{2,3},{3,2},{4,5},{5,4},{6,7},{7,6},{8,9},{9,8},{10,11... | collective-permute-start | bytes 3145736 | tf_op jit(solution)/shard_map/ppermute | solution.py:593
  320.0 39.7 %collective-permute-start.27 = (bf16[1024,2176]{1,0:T(8,128)(2,1)}, bf16[1024,2176]{1,0:T(8,128)(2,1)}, u32[]{:S(2)}, u32[]{:S(2)}) collective-permute-start(bf16[1024,2176]{1,0:T(8,128)(2,1)} %mix_grads.2), channel_id=1, source_target_pairs={{0,2},{2,0},{1,3},{3,1},{4,6},{6,4},{5,7},{7,5},{8,10},{10,8},{9,1... | collective-permute-start | bytes 13369352 | tf_op jit(solution)/shard_map/ppermute | solution.py:593
  322.9 16.0 %collective-permute-start.43 = (bf16[128,2304]{1,0:T(8,128)(2,1)}, bf16[128,2304]{1,0:T(8,128)(2,1)}, u32[]{:S(2)}, u32[]{:S(2)}) collective-permute-start(bf16[128,2304]{1,0:T(8,128)(2,1)} %get-tuple-element.369), channel_id=1, source_target_pairs={{0,8},{8,16},{16,24},{24,28},{28,20},{20,12},{12,4},{4,0},{1,9},{9... | collective-permute-start | bytes 1769480 | tf_op jit(solution)/shard_map/ppermute | solution.py:709
  323.7 15.8 %collective-permute-start.44 = (bf16[128,2304]{1,0:T(8,128)(2,1)}, bf16[128,2304]{1,0:T(8,128)(2,1)}, u32[]{:S(2)}, u32[]{:S(2)}) collective-permute-start(bf16[128,2304]{1,0:T(8,128)(2,1)} %get-tuple-element.368), channel_id=1, source_target_pairs={{8,0},{16,8},{24,16},{28,24},{20,28},{12,20},{4,12},{0,4},{9,1},{1... | collective-permute-start | bytes 1769480 | tf_op jit(solution)/shard_map/ppermute | solution.py:709
  328.1 70.9 %collective-permute-start.26 = (bf16[512,1024]{1,0:T(8,128)(2,1)}, bf16[512,1024]{1,0:T(8,128)(2,1)S(1)}, u32[]{:S(2)}, u32[]{:S(2)}) collective-permute-start(bf16[512,1024]{1,0:T(8,128)(2,1)} %get-tuple-element.192), channel_id=1, source_target_pairs={{0,1},{1,0},{2,3},{3,2},{4,5},{5,4},{6,7},{7,6},{8,9},{9,8},{10,11... | collective-permute-start | bytes 3145736 | tf_op jit(solution)/shard_map/ppermute | solution.py:593
  342.9 16.8 %collective-permute-start.45 = (bf16[128,2304]{1,0:T(8,128)(2,1)}, bf16[128,2304]{1,0:T(8,128)(2,1)}, u32[]{:S(2)}, u32[]{:S(2)}) collective-permute-start(bf16[128,2304]{1,0:T(8,128)(2,1)} %get-tuple-element.367), channel_id=1, source_target_pairs={{0,8},{8,16},{16,24},{24,28},{28,20},{20,12},{12,4},{4,0},{1,9},{9... | collective-permute-start | bytes 1769480 | tf_op jit(solution)/shard_map/ppermute | solution.py:709
  344.5 15.2 %collective-permute-start.46 = (bf16[128,2304]{1,0:T(8,128)(2,1)}, bf16[128,2304]{1,0:T(8,128)(2,1)}, u32[]{:S(2)}, u32[]{:S(2)}) collective-permute-start(bf16[128,2304]{1,0:T(8,128)(2,1)} %get-tuple-element.366), channel_id=1, source_target_pairs={{8,0},{16,8},{24,16},{28,24},{20,28},{12,20},{4,12},{0,4},{9,1},{1... | collective-permute-start | bytes 1769480 | tf_op jit(solution)/shard_map/ppermute | solution.py:709
  396.9 14.4 %collective-permute-start.48 = (bf16[128,2304]{1,0:T(8,128)(2,1)S(1)}, bf16[128,2304]{1,0:T(8,128)(2,1)S(1)}, u32[]{:S(2)}, u32[]{:S(2)}) collective-permute-start(bf16[128,2304]{1,0:T(8,128)(2,1)S(1)} %get-tuple-element.364), channel_id=1, source_target_pairs={{8,0},{16,8},{24,16},{28,24},{20,28},{12,20},{4,12},{0,4},{9,1},{1... | collective-permute-start | bytes 1769480 | tf_op jit(solution)/shard_map/ppermute | solution.py:709
  397.4 14.7 %collective-permute-start.36 = (f32[73,256]{1,0:T(8,128)S(1)}, f32[73,256]{1,0:T(8,128)S(1)}, u32[]{:S(2)}, u32[]{:S(2)}) collective-permute-start(f32[73,256]{1,0:T(8,128)S(1)} %fusion.33), channel_id=1, source_target_pairs={{0,8},{4,12},{8,0},{12,4},{16,24},{20,28},{24,16},{28,20},{1,9},{5... | collective-permute-start | bytes 224264 | tf_op jit(solution)/shard_map/ppermute | solution.py:729
  413.8 33.1 %collective-permute-start.49 = (bf16[128,2304]{1,0:T(8,128)(2,1)S(1)}, bf16[128,2304]{1,0:T(8,128)(2,1)S(1)}, u32[]{:S(2)}, u32[]{:S(2)}) collective-permute-start(bf16[128,2304]{1,0:T(8,128)(2,1)S(1)} %fusion.1), channel_id=1, source_target_pairs={{0,8},{8,16},{16,24},{24,28},{28,20},{20,12},{12,4},{4,0},{1,9},{9... | collective-permute-start | bytes 1769480 | tf_op jit(solution)/shard_map/ppermute | solution.py:715
  417.8 30.9 %collective-permute-start.29 = (bf16[128,2176]{1,0:T(8,128)(2,1)S(1)}, bf16[128,2176]{1,0:T(8,128)(2,1)S(1)}, u32[]{:S(2)}, u32[]{:S(2)}) collective-permute-start(bf16[128,2176]{1,0:T(8,128)(2,1)S(1)} %get-tuple-element.375), channel_id=1, source_target_pairs={{0,8},{8,16},{16,24},{24,28},{28,20},{20,12},{12,4},{4,0},{1,9},{9... | collective-permute-start | bytes 1671176 | tf_op jit(solution)/shard_map/ppermute | solution.py:709
  417.8 30.9 %collective-permute-start.30 = (bf16[128,2176]{1,0:T(8,128)(2,1)S(1)}, bf16[128,2176]{1,0:T(8,128)(2,1)S(1)}, u32[]{:S(2)}, u32[]{:S(2)}) collective-permute-start(bf16[128,2176]{1,0:T(8,128)(2,1)S(1)} %get-tuple-element.374), channel_id=1, source_target_pairs={{8,0},{16,8},{24,16},{28,24},{20,28},{12,20},{4,12},{0,4},{9,1},{1... | collective-permute-start | bytes 1671176 | tf_op jit(solution)/shard_map/ppermute | solution.py:709
  419.9 60.8 %collective-permute-start.28 = (bf16[512,1024]{1,0:T(8,128)(2,1)S(1)}, bf16[512,1024]{1,0:T(8,128)(2,1)S(1)}, u32[]{:S(2)}, u32[]{:S(2)}) collective-permute-start(bf16[512,1024]{1,0:T(8,128)(2,1)S(1)} %copy-done.30), channel_id=1, source_target_pairs={{0,1},{1,0},{2,3},{3,2},{4,5},{5,4},{6,7},{7,6},{8,9},{9,8},{10,11... | collective-permute-start | bytes 3145736 | tf_op jit(solution)/shard_map/ppermute | solution.py:593
  421.6 23.6 %collective-permute-start.39 = (f32[9,256]{1,0:T(8,128)S(1)}, f32[9,256]{1,0:T(8,128)S(1)}, u32[]{:S(2)}, u32[]{:S(2)}) collective-permute-start(f32[9,256]{1,0:T(8,128)S(1)} %slice.315), channel_id=1, source_target_pairs={{0,1},{1,0},{2,3},{3,2},{4,5},{5,4},{6,7},{7,6},{8,9},{9,8},{10,11... | collective-permute-start | bytes 27656 | tf_op jit(solution)/shard_map/ppermute | solution.py:729
  449.0 15.1 %collective-permute-start.31 = (bf16[128,2176]{1,0:T(8,128)(2,1)S(1)}, bf16[128,2176]{1,0:T(8,128)(2,1)S(1)}, u32[]{:S(2)}, u32[]{:S(2)}) collective-permute-start(bf16[128,2176]{1,0:T(8,128)(2,1)S(1)} %get-tuple-element.373), channel_id=1, source_target_pairs={{0,8},{8,16},{16,24},{24,28},{28,20},{20,12},{12,4},{4,0},{1,9},{9... | collective-permute-start | bytes 1671176 | tf_op jit(solution)/shard_map/ppermute | solution.py:709
  449.4 14.7 %collective-permute-start.32 = (bf16[128,2176]{1,0:T(8,128)(2,1)S(1)}, bf16[128,2176]{1,0:T(8,128)(2,1)S(1)}, u32[]{:S(2)}, u32[]{:S(2)}) collective-permute-start(bf16[128,2176]{1,0:T(8,128)(2,1)S(1)} %get-tuple-element.372), channel_id=1, source_target_pairs={{8,0},{16,8},{24,16},{28,24},{20,28},{12,20},{4,12},{0,4},{9,1},{1... | collective-permute-start | bytes 1671176 | tf_op jit(solution)/shard_map/ppermute | solution.py:709
  464.4 14.1 %collective-permute-start.33 = (bf16[128,2176]{1,0:T(8,128)(2,1)S(1)}, bf16[128,2176]{1,0:T(8,128)(2,1)S(1)}, u32[]{:S(2)}, u32[]{:S(2)}) collective-permute-start(bf16[128,2176]{1,0:T(8,128)(2,1)S(1)} %get-tuple-element.371), channel_id=1, source_target_pairs={{0,8},{8,16},{16,24},{24,28},{28,20},{20,12},{12,4},{4,0},{1,9},{9... | collective-permute-start | bytes 1671176 | tf_op jit(solution)/shard_map/ppermute | solution.py:709
  (52 other events, 610.0 us)

commit v3 on v2

--- a/solution.py
+++ b/solution.py
@@ -479,42 +479,101 @@
     )(x, cot, mine, other, *held)
 
 
-def late_kernel(plan, held, *refs):
-    lefts, rights = refs[: plan[0]], refs[plan[0] : plan[0] + len(plan[1])]
-    out_ref, turned = refs[-2], refs[-1]
-    step = pl.program_id(0)
-    for at, (right, (source, fresh)) in enumerate(zip(rights, plan[1])):
-
-        @pl.when(step == at)
-        def _(right=right, source=source, fresh=fresh):
-            if fresh:
-                turned[:, :LEN] = lefts[2 * source][...].T
-                turned[:, LEN:] = lefts[2 * source + 1][...].T
-            total = dot_nn(turned[...], right[...])
-            if held:
-                total = total + refs[plan[0] + len(plan[1])][...].astype(F32)
-            out_ref[...] = total.astype(BF16)
-
-
-def late_grads(normed, cot, units, came=None):
+def late_kernel(normed_s, normed_o, cot_s, cot_o, gate_ref, up_ref, hidden_ref, out_ref):
+    size = hidden_ref.shape[1]
+    normed = jnp.concatenate([normed_s[...].T, normed_o[...].T], axis=1)
+    cot = jnp.concatenate([cot_s[...].T, cot_o[...].T], axis=1)
+    for at, (left, right) in enumerate(((normed, gate_ref), (normed, up_ref), (cot, hidden_ref))):
+        out_ref[:, at * size : (at + 1) * size] = dot_nn(left, right[...]).astype(BF16)
+
+
+def late_grads(normed, cot, units):
     hidden, grad_gate, grad_up = units
-    rows, tile = hidden.shape
-    width = cot[0].shape[1]
-    lefts, rights = [*normed, *cot], [grad_gate, grad_up, hidden]
-    plan = (4, ((0, True), (0, False), (1, True)))
-    across = pl.BlockSpec((width, tile), lambda i: (0, i))
-    held = [came] if came is not None else []
+    (rows, size), width, tile = hidden.shape, cot[0].shape[1], 256
     return pl.pallas_call(
-        functools.partial(late_kernel, plan, len(held)),
-        grid=(3,),
-        in_specs=[pl.BlockSpec((LEN, width), lambda i: (0, 0))] * 4 + [pl.BlockSpec((rows, tile), lambda i: (0, 0))] * 3
-        + [across] * len(held),
-        out_specs=across,
-        out_shape=jax.ShapeDtypeStruct((width, 3 * tile), BF16),
-        scratch_shapes=[pltpu.VMEM((width, rows), BF16)],
-        cost_estimate=pl.CostEstimate(flops=6 * rows * width * tile, bytes_accessed=16 * 10**6, transcendentals=0),
+        late_kernel,
+        grid=(width // tile,),
+        in_specs=[pl.BlockSpec((LEN, tile), lambda i: (0, i))] * 4 + [pl.BlockSpec((rows, size), lambda i: (0, 0))] * 3,
+        out_specs=pl.BlockSpec((tile, 3 * size), lambda i: (i, 0)),
+        out_shape=jax.ShapeDtypeStruct((width, 3 * size), BF16),
+        cost_estimate=pl.CostEstimate(flops=6 * rows * width * size, bytes_accessed=16 * 10**6, transcendentals=0),
         name="late_grads",
-    )(*lefts, *rights, *held)
+    )(*normed, *cot, grad_gate, grad_up, hidden)
+
+
+def out_kernel(gated0_ref, gated1_ref, w0_ref, w1_ref, out_ref):
+    out_ref[...] = (dot_nt(gated0_ref[...], w0_ref[...]) + dot_nt(gated1_ref[...], w1_ref[...])).astype(BF16)
+
+
+def out_rows(gated, weights, width):
+    (rows, size), tile = gated[0].shape, 256
+    return pl.pallas_call(
+        out_kernel,
+        grid=(rows // tile,),
+        in_specs=[pl.BlockSpec((tile, size), lambda i: (i, 0))] * 2 + [pl.BlockSpec((width, size), lambda i: (0, 0))] * 2,
+        out_specs=pl.BlockSpec((tile, width), lambda i: (i, 0)),
+        out_shape=jax.ShapeDtypeStruct((rows, width), BF16),
+        cost_estimate=pl.CostEstimate(flops=4 * rows * width * size, bytes_accessed=4 * 10**6, transcendentals=0),
+        name="out_rows",
+    )(*gated, *weights)
+
+
+def resid_kernel(gated0_ref, gated1_ref, w0_ref, w1_ref, tokens_ref, came_ref, gain_ref, resid_ref, normed_ref):
+    resid = dot_nt(gated0_ref[...], w0_ref[...]) + dot_nt(gated1_ref[...], w1_ref[...])
+    resid = tokens_ref[...].astype(F32) + (resid + came_ref[...].astype(F32))
+    factor = lax.rsqrt(jnp.mean(resid * resid, axis=1, keepdims=True) + 1e-05)
+    resid_ref[...] = resid
+    normed_ref[...] = (resid * factor * gain_ref[...]).astype(BF16)
+
+
+def resid_rows_of(gated, weights, tokens, came, gain):
+    (rows, width), (_, size), tile = tokens.shape, gated[0].shape, 256
+    wide = pl.BlockSpec((tile, width), lambda i: (i, 0))
+    return pl.pallas_call(
+        resid_kernel,
+        grid=(rows // tile,),
+        in_specs=[pl.BlockSpec((tile, size), lambda i: (i, 0))] * 2 + [pl.BlockSpec((width, size), lambda i: (0, 0))] * 2
+        + [wide, wide, pl.BlockSpec((1, width), lambda i: (0, 0))],
+        out_specs=[wide, wide],
+        out_shape=[jax.ShapeDtypeStruct((rows, width), F32), jax.ShapeDtypeStruct((rows, width), BF16)],
+        cost_estimate=pl.CostEstimate(flops=4 * rows * width * size, bytes_accessed=8 * 10**6, transcendentals=rows),
+        name="resid_rows",
+    )(*gated, *weights, tokens, came, gain)
+
+
+def resid_back_kernel(resid_ref, back_ref, came_ref, cot_ref, gain_ref, grad_ref, low_ref, sum_ref):
+    resid = resid_ref[...]
+    factor = lax.rsqrt(jnp.mean(resid * resid, axis=1, keepdims=True) + 1e-05)
+    unit = resid * factor
+    rows = back_ref[...] + came_ref[...].astype(F32)
+    inner = rows * gain_ref[...]
+    grad = cot_ref[...].astype(F32) + factor * (inner - unit * jnp.mean(inner * unit, axis=1, keepdims=True))
+    grad_ref[...] = grad
+    low_ref[...] = grad.astype(BF16)
+    part = jnp.sum(rows * unit, axis=0, keepdims=True)
+
+    @pl.when(pl.program_id(0) == 0)
+    def _():
+        sum_ref[...] = part
+
+    @pl.when(pl.program_id(0) > 0)
+    def _():
+        sum_ref[...] = sum_ref[...] + part
+
+
+def resid_back(resid, back, came, cot, gain):
+    (rows, width), tile = resid.shape, 128
+    wide, flat = pl.BlockSpec((tile, width), lambda i: (i, 0)), pl.BlockSpec((1, width), lambda i: (0, 0))
+    return pl.pallas_call(
+        resid_back_kernel,
+        grid=(rows // tile,),
+        in_specs=[wide] * 4 + [flat],
+        out_specs=[wide, wide, flat],
+        out_shape=[jax.ShapeDtypeStruct((rows, width), F32), jax.ShapeDtypeStruct((rows, width), BF16),
+                   jax.ShapeDtypeStruct((1, width), F32)],
+        cost_estimate=pl.CostEstimate(flops=20 * rows * width, bytes_accessed=9 * 10**6, transcendentals=rows),
+        name="resid_back",
+    )(resid, back, came, cot, gain)
 
 
 def mix_kernel(held, resid_s, resid_o, normed_ref, gated_s, gated_o, grad_ref, *refs):
@@ -573,8 +632,54 @@
     )(*grads, *weights, unit)
 
 
-def against_rows(left, right):
-    return lax.dot_general(left, right, (((1,), (1,)), ((), ())), preferred_element_type=F32)
+def pack_kernel(cuts, core_ref, *refs):
+    sources, outs = refs[: len(cuts)], refs[len(cuts) :]
+    for out_ref, side in zip(outs, (core_ref[0], 1 - core_ref[0])):
+        for source, (start, size) in zip(sources, cuts):
+            out_ref[:, start : start + size] = source[:, pl.ds(pl.multiple_of(side * size, 128), size)]
+
+
+def pack(core, values):
+    cuts, at = [], 0
+    for value in values:
+        cuts.append((at, value.shape[1] // 2))
+        at += value.shape[1] // 2
+    rows = values[0].shape[0]
+    return pl.pallas_call(
+        functools.partial(pack_kernel, cuts),
+        grid_spec=pltpu.PrefetchScalarGridSpec(
+            num_scalar_prefetch=1,
+            grid=(1,),
+            in_specs=[pl.BlockSpec(value.shape, lambda i, core_ref: (0, 0)) for value in values],
+            out_specs=[pl.BlockSpec((rows, at), lambda i, core_ref: (0, 0))] * 2,
+        ),
+        out_shape=[jax.ShapeDtypeStruct((rows, at), values[0].dtype)] * 2,
+        cost_estimate=pl.CostEstimate(flops=0, bytes_accessed=8 * rows * at, transcendentals=0),
+        name="pack",
+    )(core, *values)
+
+
+def unpack_kernel(cuts, core_ref, mine_ref, came_ref, *outs):
+    for ref, side in ((mine_ref, core_ref[0]), (came_ref, 1 - core_ref[0])):
+        for out_ref, (start, size) in zip(outs, cuts):
+            out_ref[:, pl.ds(pl.multiple_of(side * size, 128), size)] = ref[:, start : start + size]
+
+
+def unpack(core, mine, came, sizes):
+    rows, cols = mine.shape
+    cuts = [(sum(sizes[:at]), size) for at, size in enumerate(sizes)]
+    return pl.pallas_call(
+        functools.partial(unpack_kernel, cuts),
+        grid_spec=pltpu.PrefetchScalarGridSpec(
+            num_scalar_prefetch=1,
+            grid=(1,),
+            in_specs=[pl.BlockSpec((rows, cols), lambda i, core_ref: (0, 0))] * 2,
+            out_specs=[pl.BlockSpec((rows, 2 * size), lambda i, core_ref: (0, 0)) for size in sizes],
+        ),
+        out_shape=[jax.ShapeDtypeStruct((rows, 2 * size), mine.dtype) for size in sizes],
+        cost_estimate=pl.CostEstimate(flops=0, bytes_accessed=16 * rows * cols, transcendentals=0),
+        name="unpack",
+    )(core, mine, came)
 
 
 def row_factor(values):
@@ -612,7 +717,10 @@
 
 
 def chip_rows(parts):
-    mine, other = own_half(parts)
+    return joined_rows(*own_half(parts))
+
+
+def joined_rows(mine, other):
     return jnp.concatenate(by_core(mine, swap(other, "core")), axis=0)
 
 
@@ -633,7 +741,7 @@
         place = (self.place + offset + self.chips) % self.chips
         return jnp.where(place < self.chips // 2, 2 * place, 2 * (self.chips - 1 - place) + 1)
 
-    def gather(self, piece, joined):
+    def gather(self, piece, joined, first=None, halved=True):
         rows = piece.shape[0]
         pieces, offsets = [piece], [0]
         up = down = piece
@@ -643,7 +751,12 @@
             up, down = lax.optimization_barrier((up, down))
             pieces += [up, down]
             offsets += [-step, step]
+            if step == 1 and first is not None:
+                first(up)
         far = self.chips // 2
+        if not halved:
+            pieces.append(lax.ppermute(up, "chip", self.ahead))
+            return joined(pieces, [self.chip_at(offset) for offset in offsets + [far]])
         top = lax.ppermute(up[: rows // 2], "chip", self.ahead)
         bottom = lax.ppermute(down[rows // 2 :], "chip", self.back)
         pieces += lax.optimization_barrier((top, bottom))
@@ -663,15 +776,12 @@
 
         def kernel(places_ref, *refs):
             out_ref, held, into, out = refs[count:]
-            firsts = [at * rows for at in range(count - 1)] + [(count - 2) * rows + rows // 2]
             stages, results = [], []
             for at, ref in enumerate(refs[:count]):
-                start = pl.multiple_of(places_ref[min(at, count - 2)] * rows, rows)
-                if at == count - 1:
-                    start = pl.multiple_of(start + rows // 2, rows // 2)
-                slot = held.at[pl.ds(firsts[at], ref.shape[0]), :]
+                start = pl.multiple_of(places_ref[at] * rows, rows)
+                slot = held.at[pl.ds(at * rows, rows), :]
                 stages.append(pltpu.make_async_copy(ref, slot, into.at[at]))
-                results.append(pltpu.make_async_copy(slot, out_ref.at[pl.ds(start, ref.shape[0]), :], out.at[at]))
+                results.append(pltpu.make_async_copy(slot, out_ref.at[pl.ds(start, rows), :], out.at[at]))
                 stages[-1].start()
             for stage, result in zip(stages, results):
                 stage.wait()
@@ -745,17 +855,23 @@
     cot_o = swap(cotangent, "tensor")
 
     pad = jnp.zeros((w_query.shape[0], 128 - 2 * heads_n), BF16)
-    mix_parts = [
-        jnp.concatenate(list(parts) + [pad], axis=1)
-        for parts in zip(*map(halves, (w_out.T, w_query, w_key, w_value, w_gate, w_decay, w_write)))
-    ]
-    ffn_rows = chip_rows([
-        jnp.concatenate(parts, axis=1)
-        for parts in zip(*(wide_halves(value, FF_HALF) for value in (w_ffgate, w_ffup, w_ffdown.T)))
-    ])
-    w_mix = [ring.gather(chip_rows(mix_parts), ring.by_slices)]
+    core = lax.axis_index("core").astype(jnp.int32).reshape(1)
+    rates = jnp.concatenate(
+        [part for pair in zip(*map(halves, (w_decay, w_write))) for part in (*pair, pad)], axis=1
+    )
+    mix_parts = pack(core, [w_out.T, w_query, w_key, w_value, w_gate, rates])
+    ffn_rows = []
+
+    def pack_ffn(ready):
+        values = lax.optimization_barrier((w_ffgate, w_ffup, w_ffdown.T, ready))[:3]
+        parts = [
+            jnp.concatenate(parts, axis=1) for parts in zip(*(wide_halves(value, FF_HALF) for value in values))
+        ]
+        ffn_rows.append(chip_rows(parts))
+
+    w_mix = [ring.gather(joined_rows(*mix_parts), ring.by_slices, pack_ffn)]
     w_mix.append(swap(w_mix[0], "core"))
-    w_ffn = [ring.gather(after(ffn_rows, w_mix[0]), ring.by_copies)]
+    w_ffn = [ring.gather(after(ffn_rows[0], w_mix[0]), ring.by_copies, halved=False)]
     w_ffn.append(swap(w_ffn[0], "core"))
     val_w = heads_n * DV
 
@@ -775,30 +891,25 @@
     def mix(normed, seq, side):
         mixed[seq, side] = mix_forward(normed, w_mix[side], seq, params[side])
 
-    def out_part(seq):
-        return against_rows(mixed[seq, 0][0], w_mix[0][:, :val_w]) + against_rows(mixed[seq, 1][0], w_mix[1][:, :val_w])
-
     mix(normed1, 1, 0)
     mix(after(normed1, mixed[1, 0][0]), 1, 1)
-    part_o = out_part(1).astype(BF16)
+    part_o = out_rows((mixed[1, 0][0], mixed[1, 1][0]), w_mix, tokens.shape[1])
     came_s = swap(part_o, "tensor")
     mix(after(normed1, part_o), 0, 0)
     mix(after(normed1, mixed[0, 0][0]), 0, 1)
-    resid1 = tokens32[:LEN] + out_part(0) + came_s.astype(F32)
-    factor2 = row_factor(resid1)
-    unit2 = resid1 * factor2
-    normed2_s = (unit2 * norm_gain2).astype(BF16)
+    gain2 = norm_gain2.reshape(1, -1)
+    resid1, normed2_s = resid_rows_of((mixed[0, 0][0], mixed[0, 1][0]), w_mix, tokens, came_s, gain2)
     normed2_o = swap(normed2_s, "tensor")
 
     *units, part_s, back_s = ffn_both(normed2_s, cotangent, w_ffn[0], w_ffn[1], 0, 2 * LEN, F32)
     *units, part_low, back_low = ffn_both(normed2_o, cot_o, w_ffn[0], w_ffn[1], 1, 2 * LEN, BF16, units)
-    grad_rows2 = back_s + swap(back_low, "tensor").astype(F32)
+    came_rows2 = swap(back_low, "tensor")
     normed2, cot = (normed2_s, after(normed2_o, back_low)), (cotangent, cot_o)
     late_sent = late_grads(normed2, cot, units[3:])
     late_came = swap(late_sent, "core")
     late_own = late_grads((normed2_s, after(normed2_o, late_sent)), cot, units[:3])
-    grad_resid = cotangent.astype(F32) + norm_backward(unit2, factor2, norm_gain2, grad_rows2)
-    resid_s = after(grad_resid.astype(BF16), late_own)
+    grad_resid, resid_s, grad_gain2 = resid_back(resid1, back_s, came_rows2, cotangent, gain2)
+    resid_s = after(resid_s, late_own)
     resid_o = swap(resid_s, "tensor")
     resid_rows = (resid_s, resid_o)
     result = resid1 + part_s + swap(after(part_low, resid_o), "tensor").astype(F32)
@@ -823,7 +934,10 @@
     grad_proj[0] = after(grad_proj[0], mix_own)
 
     _, back_sent, gain_o = back_rows(grad_proj, w_mix, unit1, 1)
-    mix_sum = owner_rows(mix_last(back_sent))
+    mix_rows = mix_last(back_sent)
+    mine_rows, other_rows = own_half((mix_rows[: mix_rows.shape[0] // 2], mix_rows[mix_rows.shape[0] // 2 :]))
+    key_w = heads_n * DK
+    mix_sum = unpack(core, mine_rows, swap(other_rows, "core"), (val_w, key_w, key_w, val_w, val_w, 128))
     back_s, _, gain_s = back_rows(grad_proj, w_mix, unit1, 0)
     grad_gain1 = gain_o[0] + gain_s[0]
     came_back = swap(back_sent, "tensor")
@@ -832,7 +946,6 @@
     grad_rows1 = back_s + came_back.astype(F32)
     grad_tokens = grad_resid + norm_backward(unit_s, factor_s, norm_gain1, grad_rows1)
 
-    grad_gain2 = jnp.sum(grad_rows2 * unit2, axis=0)
     head_rows = jnp.concatenate(by_core(small[0][0], small[1][0]), axis=0)
     out_gain_row = jnp.sum(head_rows[:, 8], axis=0, keepdims=True)
     wide = jnp.concatenate(
@@ -849,25 +962,23 @@
     def columns(parts, start, size):
         return jnp.concatenate([part[:, start : start + size] for part in parts], axis=1)
 
-    key_w = heads_n * DK
-    at = [0, val_w, val_w + key_w, val_w + 2 * key_w, 2 * val_w + 2 * key_w, 3 * val_w + 2 * key_w]
     return (
         result.astype(BF16),
         grad_tokens,
         gains[:count].reshape(-1),
-        columns(mix_sum, at[1], key_w),
-        columns(mix_sum, at[2], key_w),
-        columns(mix_sum, at[3], val_w),
-        columns(mix_sum, at[4], val_w),
-        columns(mix_sum, at[5], heads_n),
-        columns(mix_sum, at[5] + heads_n, heads_n),
+        mix_sum[1],
+        mix_sum[2],
+        mix_sum[3],
+        mix_sum[4],
+        jnp.concatenate([mix_sum[5][:, start : start + heads_n] for start in (0, 128)], axis=1),
+        jnp.concatenate([mix_sum[5][:, start : start + heads_n] for start in (heads_n, 128 + heads_n)], axis=1),
         taps(head_rows[:, 4:8, :DK]),
         taps(head_rows[:, 4:8, DK:]),
         taps(head_rows[:, :4]),
         head_rows[:, 9, 0],
         head_rows[:, 9, 1],
         gains[2 * count],
-        columns(mix_sum, at[0], val_w).T,
+        mix_sum[0].T,
         gains[count : 2 * count].reshape(-1),
         columns(late_sum, 0, ff),
         columns(late_sum, FF_HALF, ff),

time: 506 us -> 527 us (1.042)
  waiting for transfers between devices: 162 us -> 194 us
  Pallas kernels: 208 us -> 226 us
  matrix products: 12.4 us -> 0 us
  other arithmetic: 43.4 us -> 32.4 us
    ppermute x16, waiting for transfers between devices: 10.9 us -> 32.2 us  [swap(): return lax.ppermute(value, axis, SWAP)]
    pallas_call x2 -> x7, Pallas kernels: 21.3 us -> 38.3 us  [the longest x2 19.7 us: late_grads(): pl.pallas_call(late_kernel, grid=(width // tile,), in_specs=[pl.BlockSpec...]
    dot_general x4 -> x0, matrix products: 12.4 us -> none  [against_rows(): lax.dot_general(left, right, (((1,), (1,)), ((), ())), preferred_element_...]
    ppermute x0 -> x1, waiting for transfers between devices: none -> 9.01 us  [gather(): pieces.append(lax.ppermute(up, 'chip', self.ahead))]
    convert_element_type x3 -> x0, other arithmetic: 6.41 us -> none  [the longest x1 3.67 us: layer(): resid_s = after(grad_resid.astype(BF16), late_own)]
  transfers between devices with their start and end apart: 51 -> 50, of which waited for: 31 -> 31; matrix products, arithmetic and copies ran while one was open for 14% -> 8% of each run, Pallas kernels for 38% -> 39%
where the time goes in v3:
time: 527 us; the launch traced here: 522 us
  Pallas kernels  226 us (43%)
  waiting for transfers between devices  194 us (37%)
  starting transfers between devices  41.7 us (8%)
  other arithmetic  32.4 us (6%)
  local copies, waits for them, and re-layouts  26.5 us (5%)
    ppermute x6, waiting for transfers between devices, gather(): lax.ppermute(up, 'chip', self.ahead)  60.6 us
    pallas_call x4, Pallas kernels, mix_backward(): pl.pallas_call(functools.partial(backward_kernel, heads_n), grid=(heads_n...  55.5 us
    pallas_call x4, Pallas kernels, mix_forward(): pl.pallas_call(functools.partial(forward_kernel, heads_n), grid=(heads_n,...  53 us
    ppermute x6, waiting for transfers between devices, scatter_sum(): lax.ppermute(up, 'chip', self.ahead)  41.4 us
    pallas_call x2, Pallas kernels, ffn_both(): pl.pallas_call(functools.partial(ffn_kernel, len(held)), grid=(1,), in_sp...  34.4 us
    ppermute x16, waiting for transfers between devices, swap(): return lax.ppermute(value, axis, SWAP)  32.2 us
    ppermute x5, waiting for transfers between devices, all_sum(): came = lax.ppermute(value, axis, [(at, at ^ step) for at in range(size)])  25.6 us
    pallas_call x2, Pallas kernels, mix_grads(): pl.pallas_call(functools.partial(mix_kernel, len(held)), grid=(width // t...  20.2 us
  transfers between devices with their start and end apart: 50, of which 31 were waited for; matrix products, arithmetic and copies ran while one was open for 8% of the time, Pallas kernels for 39%

profile of v3, /device:TPU:0, one launch (start us, length us, event | category | flops | bytes accessed | tf_op | source)
XLA Modules:
  0.0 521.5 jit_solution(18061328987395990787)
XLA Ops:
  14.7 9.4 %collective-permute-done.2 = bf16[128,2176]{1,0:T(8,128)(2,1)S(1)} collective-permute-done((bf16[128,2176]{1,0:T(8,128)(2,1)S(1)}, bf16[128,2176]{1,0:T(8,128)(2,1)S(1)}, u32[]{:S(2)}, u32[]{:S(2)}) %collective-permute-start.2) | collective-permute-done | bytes 557088 | tf_op jit(solution)/shard_map/ppermute | solution.py:750
  30.2 9.0 %collective-permute-done.4 = bf16[128,2176]{1,0:T(8,128)(2,1)S(1)} collective-permute-done((bf16[128,2176]{1,0:T(8,128)(2,1)S(1)}, bf16[128,2176]{1,0:T(8,128)(2,1)S(1)}, u32[]{:S(2)}, u32[]{:S(2)}) %collective-permute-start.4) | collective-permute-done | bytes 557088 | tf_op jit(solution)/shard_map/ppermute | solution.py:750
  46.5 10.4 %collective-permute-done.6 = bf16[128,2176]{1,0:T(8,128)(2,1)S(1)} collective-permute-done((bf16[128,2176]{1,0:T(8,128)(2,1)S(1)}, bf16[128,2176]{1,0:T(8,128)(2,1)S(1)}, u32[]{:S(2)}, u32[]{:S(2)}) %collective-permute-start.6) | collective-permute-done | bytes 557088 | tf_op jit(solution)/shard_map/ppermute | solution.py:750
  70.1 11.2 %collective-permute-done.13.refs_1_ = bf16[128,2304]{1,0:T(8,128)(2,1)S(1)} collective-permute-done((bf16[128,2304]{1,0:T(8,128)(2,1)S(1)}, bf16[128,2304]{1,0:T(8,128)(2,1)S(1)}, u32[]{:S(2)}, u32[]{:S(2)}) %collective-permute-start.13) | collective-permute-done | bytes 589856 | tf_op jit(solution)/shard_map/ppermute | solution.py:750
  83.8 10.6 %collective-permute-done.15.refs_3_ = bf16[128,2304]{1,0:T(8,128)(2,1)S(1)} collective-permute-done((bf16[128,2304]{1,0:T(8,128)(2,1)S(1)}, bf16[128,2304]{1,0:T(8,128)(2,1)S(1)}, u32[]{:S(2)}, u32[]{:S(2)}) %collective-permute-start.15) | collective-permute-done | bytes 589856 | tf_op jit(solution)/shard_map/ppermute | solution.py:750
  97.3 10.0 %collective-permute-done.17.refs_5_ = bf16[128,2304]{1,0:T(8,128)(2,1)} collective-permute-done((bf16[128,2304]{1,0:T(8,128)(2,1)S(1)}, bf16[128,2304]{1,0:T(8,128)(2,1)}, u32[]{:S(2)}, u32[]{:S(2)}) %collective-permute-start.17) | collective-permute-done | bytes 589856 | tf_op jit(solution)/shard_map/ppermute | solution.py:750
  109.6 9.0 %collective-permute-done.19.refs_7_ = bf16[128,2304]{1,0:T(8,128)(2,1)} collective-permute-done((bf16[128,2304]{1,0:T(8,128)(2,1)}, bf16[128,2304]{1,0:T(8,128)(2,1)}, u32[]{:S(2)}, u32[]{:S(2)}) %collective-permute-start.19) | collective-permute-done | bytes 589856 | tf_op jit(solution)/shard_map/ppermute | solution.py:758
  128.1 21.5 %collective-permute-done = bf16[512,1024]{1,0:T(8,128)(2,1)S(1)} collective-permute-done((bf16[512,1024]{1,0:T(8,128)(2,1)S(1)}, bf16[512,1024]{1,0:T(8,128)(2,1)S(1)}, u32[]{:S(2)}, u32[]{:S(2)}) %collective-permute-start) | collective-permute-done | bytes 1048608 | tf_op jit(solution)/shard_map/ppermute | solution.py:698
  153.4 13.5 %mix_forward.4 = (bf16[512,512]{1,0:T(8,128)(2,1)}, bf16[512,512]{1,0:T(8,128)(2,1)}, bf16[512,512]{1,0:T(8,128)(2,1)}, bf16[1,2,4,128,128]{4,3,2,1,0:T(8,128)(2...) custom-call(bf16[1024,1024]{1,0:T(8,128)(2,1)} %get-tuple-element.17, ...), custom_call_target="tpu_custom_call" | custom-call | flops 6000000000 | bytes 10000000 | tf_op jit(solution)/shard_map/mix_forward/pallas_call | solution.py:377
  166.9 13.1 %mix_forward.5 = (bf16[512,512]{1,0:T(8,128)(2,1)}, bf16[512,512]{1,0:T(8,128)(2,1)}, bf16[512,512]{1,0:T(8,128)(2,1)}, bf16[1,2,4,128,128]{4,3,2,1,0:T(8,128)(2...) custom-call(bf16[1024,1024]{1,0:T(8,128)(2,1)} %get-tuple-element.17, ...), custom_call_target="tpu_custom_call" | custom-call | flops 6000000000 | bytes 10000000 | tf_op jit(solution)/shard_map/mix_forward/pallas_call | solution.py:377
  185.6 13.1 %mix_forward.6 = (bf16[512,512]{1,0:T(8,128)(2,1)}, bf16[512,512]{1,0:T(8,128)(2,1)}, bf16[512,512]{1,0:T(8,128)(2,1)}, bf16[1,2,4,128,128]{4,3,2,1,0:T(8,128)(2...) custom-call(bf16[1024,1024]{1,0:T(8,128)(2,1)} %get-tuple-element.17, ...), custom_call_target="tpu_custom_call" | custom-call | flops 6000000000 | bytes 10000000 | tf_op jit(solution)/shard_map/mix_forward/pallas_call | solution.py:377
  198.7 13.3 %mix_forward.7 = (bf16[512,512]{1,0:T(8,128)(2,1)}, bf16[512,512]{1,0:T(8,128)(2,1)}, bf16[512,512]{1,0:T(8,128)(2,1)}, bf16[1,2,4,128,128]{4,3,2,1,0:T(8,128)(2...) custom-call(bf16[1024,1024]{1,0:T(8,128)(2,1)} %get-tuple-element.17, ...), custom_call_target="tpu_custom_call" | custom-call | flops 6000000000 | bytes 10000000 | tf_op jit(solution)/shard_map/mix_forward/pallas_call | solution.py:377
  218.4 17.3 %ffn_both.2 = (bf16[1024,768]{1,0:T(8,128)(2,1)}, bf16[1024,768]{1,0:T(8,128)(2,1)}, bf16[1024,768]{1,0:T(8,128)(2,1)}, bf16[1024,768]{1,0:T(8,128)(2,1)}, bf16[...) custom-call(bf16[512,1024]{1,0:T(8,128)(2,1)} %get-tuple-element.181.x_ref.normed_s, ...), custom_call_target="tpu_custom_call" | custom-call | flops 9663676416 | bytes 25000000 | tf_op jit(solution)/shard_map/ffn_both/pallas_call | solution.py:468
  235.7 6.2 %collective-permute-done.21.x_ref.normed_o = bf16[512,1024]{1,0:T(8,128)(2,1)S(1)} collective-permute-done((bf16[512,1024]{1,0:T(8,128)(2,1)}, bf16[512,1024]{1,0:T(8,128)(2,1)S(1)}, u32[]{:S(2)}, u32[]{:S(2)}) %collective-permute-start.21) | collective-permute-done | bytes 1048608 | tf_op jit(solution)/shard_map/ppermute | solution.py:698
  242.9 17.1 %ffn_both.3 = (bf16[1024,768]{1,0:T(8,128)(2,1)}, bf16[1024,768]{1,0:T(8,128)(2,1)}, bf16[1024,768]{1,0:T(8,128)(2,1)}, bf16[1024,768]{1,0:T(8,128)(2,1)}, bf16[...) custom-call(bf16[512,1024]{1,0:T(8,128)(2,1)} %copy-done.34, ...), custom_call_target="tpu_custom_call", output_to_operand_aliasing={{0}: (4, {}), {1}: (5, {}), {2}: (6, {}), {3}: (7, {}), {4}... | custom-call | flops 9663676416 | bytes 25000000 | tf_op jit(solution)/shard_map/ffn_both/pallas_call | solution.py:468
  260.6 9.8 %late_grads.2 = bf16[1024,2304]{1,0:T(8,128)(2,1)} custom-call(bf16[512,1024]{1,0:T(8,128)(2,1)} %get-tuple-element.181.x_ref.normed_s, bf16[512,1024]{1,0:T(8,128)(2,1)} %copy-done.34, bf16[512,1024]{1,0:T(8,128)(2,1)} %cot_s.3, bf16[512,1024]{1,0:T(8,128)(2,1)} %copy-done.33, bf16[1024,768]{1,0:T(8,128)(2,1)} %get-tuple-element.204.gate_ref, ...), custom_call_target="tpu_custom_call" | custom-call | flops 4831838208 | bytes 16000000 | tf_op jit(solution)/shard_map/late_grads/pallas_call | solution.py:493
  270.4 9.8 %late_grads.3 = bf16[1024,2304]{1,0:T(8,128)(2,1)} custom-call(bf16[512,1024]{1,0:T(8,128)(2,1)} %get-tuple-element.181.x_ref.normed_s, bf16[512,1024]{1,0:T(8,128)(2,1)} %copy-done.34, bf16[512,1024]{1,0:T(8,128)(2,1)} %cot_s.3, bf16[512,1024]{1,0:T(8,128)(2,1)} %copy-done.33, bf16[1024,768]{1,0:T(8,128)(2,1)} %get-tuple-element.208.gate_ref, ...), custom_call_target="tpu_custom_call" | custom-call | flops 4831838208 | bytes 16000000 | tf_op jit(solution)/shard_map/late_grads/pallas_call | solution.py:493
  284.2 5.5 %resid_back.1 = (f32[512,1024]{1,0:T(8,128)}, bf16[512,1024]{1,0:T(8,128)(2,1)}, f32[1,1024]{1,0:T(1,128)}) custom-call(f32[512,1024]{1,0:T(8,128)} %get-tuple-element.180.resid_ref, f32[512,1024]{1,0:T(8,128)} %get-tuple-element.200.back_ref, bf16[512,1024]{1,0:T(8,128)(2,1)} %copy-done.8, bf16[512,1024]{1,0:T(8,128)(2,1)} %cot_s.3, f32[1,1024]{1,0:T(1,128)} %bitcast.153), custom_call_target="tpu_custom_call" | custom-call | flops 10485760 | bytes 9000000 | tf_op jit(solution)/shard_map/resid_back/pallas_call | solution.py:567
  290.2 14.1 %mix_backward.4 = (bf16[1024,1664]{1,0:T(8,128)(2,1)}, f32[1,2,16,256]{3,2,1,0:T(8,128)}) custom-call(bf16[512,1024]{1,0:T(8,128)(2,1)} %get-tuple-element.228.resid_ref.resid_s, bf16[1024,2176]{1,0:T(8,128)(2,1)} %collective-permute-done.10.wq_ref.wk_ref.wv_ref.wg_ref.wab_ref.w1_ref.wo_ref, f32[4,256]{1,0:T(4,128)} %get-tuple-element.424.cq_ref, ...), custom_call_target="tpu_custom_call" | custom-call | flops 10000000000 | bytes 12000000 | tf_op jit(solution)/shard_map/mix_backward/pallas_call | solution.py:405
  304.3 13.7 %mix_backward.5 = (bf16[1024,1664]{1,0:T(8,128)(2,1)}, f32[1,2,16,256]{3,2,1,0:T(8,128)}) custom-call(bf16[512,1024]{1,0:T(8,128)(2,1)} %get-tuple-element.228.resid_ref.resid_s, bf16[1024,2176]{1,0:T(8,128)(2,1)} %bitcast.11.wq_ref.wk_ref.wv_ref.wg_ref.wab_ref.w0_ref.wo_ref, f32[4,256]{1,0:T(4,128)} %get-tuple-element.423.cq_ref, ...), custom_call_target="tpu_custom_call" | custom-call | flops 10000000000 | bytes 12000000 | tf_op jit(solution)/shard_map/mix_backward/pallas_call | solution.py:405
  319.0 13.9 %mix_backward.6 = (bf16[1024,1664]{1,0:T(8,128)(2,1)}, f32[1,2,16,256]{3,2,1,0:T(8,128)}) custom-call(bf16[512,1024]{1,0:T(8,128)(2,1)} %copy-done.6, bf16[1024,2176]{1,0:T(8,128)(2,1)} %collective-permute-done.10.wq_ref.wk_ref.wv_ref.wg_ref.wab_ref.w1_ref.wo_ref, f32[4,256]{1,0:T(4,128)} %get-tuple-element.424.cq_ref, ...), custom_call_target="tpu_custom_call", output_to_operand_aliasing={{0}: (19, {})} | custom-call | flops 10000000000 | bytes 12000000 | tf_op jit(solution)/shard_map/mix_backward/pallas_call | solution.py:405
  332.8 9.7 %mix_grads.2 = bf16[1024,2176]{1,0:T(8,128)(2,1)} custom-call(bf16[512,1024]{1,0:T(8,128)(2,1)} %get-tuple-element.228.resid_ref.resid_s, bf16[512,1024]{1,0:T(8,128)(2,1)} %copy-done.6, bf16[1024,1024]{1,0:T(8,128)(2,1)} %get-tuple-element.178.x_ref.normed_ref, bf16[512,512]{1,0:T(8,128)(2,1)} %get-tuple-element.179.gated1_ref.gated_s, ...), custom_call_target="tpu_custom_call" | custom-call | flops 4563402752 | bytes 14000000 | tf_op jit(solution)/shard_map/mix_grads/pallas_call | solution.py:596
  352.0 9.5 %collective-permute-done.42 = bf16[128,2304]{1,0:T(8,128)(2,1)} collective-permute-done((bf16[128,2304]{1,0:T(8,128)(2,1)}, bf16[128,2304]{1,0:T(8,128)(2,1)}, u32[]{:S(2)}, u32[]{:S(2)}) %collective-permute-start.42) | collective-permute-done | bytes 589856 | tf_op jit(solution)/shard_map/ppermute | solution.py:819
  367.3 13.8 %mix_backward.7 = (bf16[1024,1664]{1,0:T(8,128)(2,1)}, f32[1,2,16,256]{3,2,1,0:T(8,128)}) custom-call(bf16[512,1024]{1,0:T(8,128)(2,1)} %copy-done.6, bf16[1024,2176]{1,0:T(8,128)(2,1)} %bitcast.11.wq_ref.wk_ref.wv_ref.wg_ref.wab_ref.w0_ref.wo_ref, f32[4,256]{1,0:T(4,128)} %get-tuple-element.423.cq_ref, ...), custom_call_target="tpu_custom_call", output_to_operand_aliasing={{0}: (19, {})} | custom-call | flops 10000000000 | bytes 12000000 | tf_op jit(solution)/shard_map/mix_backward/pallas_call | solution.py:405
  382.0 10.5 %mix_grads.3 = bf16[1024,2176]{1,0:T(8,128)(2,1)} custom-call(bf16[512,1024]{1,0:T(8,128)(2,1)} %get-tuple-element.228.resid_ref.resid_s, bf16[512,1024]{1,0:T(8,128)(2,1)} %copy-done.6, bf16[1024,1024]{1,0:T(8,128)(2,1)} %get-tuple-element.178.x_ref.normed_ref, bf16[512,512]{1,0:T(8,128)(2,1)} %get-tuple-element.177.gated0_ref.gated_s, ...), custom_call_target="tpu_custom_call" | custom-call | flops 4563402752 | bytes 14000000 | tf_op jit(solution)/shard_map/mix_grads/pallas_call | solution.py:596
  392.5 9.7 %back_rows.2 = (f32[512,1024]{1,0:T(8,128)}, bf16[512,1024]{1,0:T(8,128)(2,1)}, f32[1,1024]{1,0:T(1,128)}) custom-call(bf16[1024,1664]{1,0:T(8,128)(2,1)} %get-tuple-element.270.grad_ref.mine_ref, bf16[1024,1664]{1,0:T(8,128)(2,1)} %get-tuple-element.255.grad_ref.other_ref, bf16[1024,2176]{1,0:T(8,128)(2,1)} %bitcast.11.wq_ref.wk_ref.wv_ref.wg_ref.wab_ref.w0_ref.wo_ref, ...), custom_call_target="tpu_custom_call" | custom-call | flops 3489660928 | bytes 17000000 | tf_op jit(solution)/shard_map/back_rows/pallas_call | solution.py:620
  402.2 9.7 %back_rows.3 = (f32[512,1024]{1,0:T(8,128)}, bf16[512,1024]{1,0:T(8,128)(2,1)}, f32[1,1024]{1,0:T(1,128)}) custom-call(bf16[1024,1664]{1,0:T(8,128)(2,1)} %get-tuple-element.270.grad_ref.mine_ref, bf16[1024,1664]{1,0:T(8,128)(2,1)} %get-tuple-element.255.grad_ref.other_ref, bf16[1024,2176]{1,0:T(8,128)(2,1)} %bitcast.11.wq_ref.wk_ref.wv_ref.wg_ref.wab_ref.w0_ref.wo_ref, ...), custom_call_target="tpu_custom_call" | custom-call | flops 3489660928 | bytes 17000000 | tf_op jit(solution)/shard_map/back_rows/pallas_call | solution.py:620
  420.8 8.8 %collective-permute-done.46 = bf16[128,2304]{1,0:T(8,128)(2,1)S(1)} collective-permute-done((bf16[128,2304]{1,0:T(8,128)(2,1)S(1)}, bf16[128,2304]{1,0:T(8,128)(2,1)S(1)}, u32[]{:S(2)}, u32[]{:S(2)}) %collective-permute-start.46) | collective-permute-done | bytes 589856 | tf_op jit(solution)/shard_map/ppermute | solution.py:819
  444.6 21.3 %collective-permute-done.38 = f32[9,256]{1,0:T(8,128)S(1)} collective-permute-done((f32[9,256]{1,0:T(8,128)S(1)}, f32[9,256]{1,0:T(8,128)S(1)}, u32[]{:S(2)}, u32[]{:S(2)}) %collective-permute-start.38) | collective-permute-done | bytes 9248 | tf_op jit(solution)/shard_map/ppermute | solution.py:839
  472.0 12.8 %collective-permute-done.30 = bf16[128,2176]{1,0:T(8,128)(2,1)S(1)} collective-permute-done((bf16[128,2176]{1,0:T(8,128)(2,1)S(1)}, bf16[128,2176]{1,0:T(8,128)(2,1)S(1)}, u32[]{:S(2)}, u32[]{:S(2)}) %collective-permute-start.30) | collective-permute-done | bytes 557088 | tf_op jit(solution)/shard_map/ppermute | solution.py:819
  489.0 10.3 %collective-permute-done.32 = bf16[128,2176]{1,0:T(8,128)(2,1)S(1)} collective-permute-done((bf16[128,2176]{1,0:T(8,128)(2,1)S(1)}, bf16[128,2176]{1,0:T(8,128)(2,1)S(1)}, u32[]{:S(2)}, u32[]{:S(2)}) %collective-permute-start.32) | collective-permute-done | bytes 557088 | tf_op jit(solution)/shard_map/ppermute | solution.py:819
  502.6 10.2 %collective-permute-done.39 = bf16[128,2176]{1,0:T(8,128)(2,1)S(1)} collective-permute-done((bf16[128,2176]{1,0:T(8,128)(2,1)S(1)}, bf16[128,2176]{1,0:T(8,128)(2,1)S(1)}, u32[]{:S(2)}, u32[]{:S(2)}) %collective-permute-start.39) | collective-permute-done | bytes 557088 | tf_op jit(solution)/shard_map/ppermute | solution.py:825
  (258 shorter events, 142.0 us)
Async XLA Ops:
  8.3 15.8 %collective-permute-start.2 = (bf16[128,2176]{1,0:T(8,128)(2,1)S(1)}, bf16[128,2176]{1,0:T(8,128)(2,1)S(1)}, u32[]{:S(2)}, u32[]{:S(2)}) collective-permute-start(bf16[128,2176]{1,0:T(8,128)(2,1)S(1)} %pad_maximum_fusion.2), channel_id=1, source_target_pairs={{0,8},{8,16},{16,24},{24,28},{28,20},{20,12},{12,4},{4,0},{1,9},{9... | collective-permute-start | bytes 1671176 | tf_op jit(solution)/shard_map/ppermute | solution.py:750
  11.2 14.4 %collective-permute-start.3 = (bf16[128,2176]{1,0:T(8,128)(2,1)S(1)}, bf16[128,2176]{1,0:T(8,128)(2,1)S(1)}, u32[]{:S(2)}, u32[]{:S(2)}) collective-permute-start(bf16[128,2176]{1,0:T(8,128)(2,1)S(1)} %pad_maximum_fusion.2), channel_id=1, source_target_pairs={{8,0},{16,8},{24,16},{28,24},{20,28},{12,20},{4,12},{0,4},{9,1},{1... | collective-permute-start | bytes 1671176 | tf_op jit(solution)/shard_map/ppermute | solution.py:750
  27.7 15.0 %collective-permute-start.5 = (bf16[128,2176]{1,0:T(8,128)(2,1)S(1)}, bf16[128,2176]{1,0:T(8,128)(2,1)S(1)}, u32[]{:S(2)}, u32[]{:S(2)}) collective-permute-start(bf16[128,2176]{1,0:T(8,128)(2,1)S(1)} %collective-permute-done.3), channel_id=1, source_target_pairs={{8,0},{16,8},{24,16},{28,24},{20,28},{12,20},{4,12},{0,4},{9,1},{1... | collective-permute-start | bytes 1671176 | tf_op jit(solution)/shard_map/ppermute | solution.py:750
  42.8 14.1 %collective-permute-start.6 = (bf16[128,2176]{1,0:T(8,128)(2,1)S(1)}, bf16[128,2176]{1,0:T(8,128)(2,1)S(1)}, u32[]{:S(2)}, u32[]{:S(2)}) collective-permute-start(bf16[128,2176]{1,0:T(8,128)(2,1)S(1)} %collective-permute-done.4), channel_id=1, source_target_pairs={{0,8},{8,16},{16,24},{24,28},{28,20},{20,12},{12,4},{4,0},{1,9},{9... | collective-permute-start | bytes 1671176 | tf_op jit(solution)/shard_map/ppermute | solution.py:750
  44.4 13.8 %collective-permute-start.7 = (bf16[128,2176]{1,0:T(8,128)(2,1)S(1)}, bf16[128,2176]{1,0:T(8,128)(2,1)S(1)}, u32[]{:S(2)}, u32[]{:S(2)}) collective-permute-start(bf16[128,2176]{1,0:T(8,128)(2,1)S(1)} %collective-permute-done.5), channel_id=1, source_target_pairs={{8,0},{16,8},{24,16},{28,24},{20,28},{12,20},{4,12},{0,4},{9,1},{1... | collective-permute-start | bytes 1671176 | tf_op jit(solution)/shard_map/ppermute | solution.py:750
  83.8 83.1 %collective-permute-start.10 = (bf16[1024,2176]{1,0:T(8,128)(2,1)}, bf16[1024,2176]{1,0:T(8,128)(2,1)}, u32[]{:S(2)}, u32[]{:S(2)}) collective-permute-start(bf16[1024,2176]{1,0:T(8,128)(2,1)} %bitcast.11.wq_ref.wk_ref.wv_ref.wg_ref.wab_ref.w0_ref.wo_ref), channel_id=1, source_target_pairs={{0,2},{2,0},{1,3},{3,1},{4,6},{6,4},{5,7},{7,5},{8,10},{10,8},{9,1... | collective-permute-start | bytes 13369352 | tf_op jit(solution)/shard_map/ppermute | solution.py:698
  123.4 95.0 %collective-permute-start.20 = (bf16[1024,2304]{1,0:T(8,128)(2,1)}, bf16[1024,2304]{1,0:T(8,128)(2,1)}, u32[]{:S(2)}, u32[]{:S(2)}) collective-permute-start(bf16[1024,2304]{1,0:T(8,128)(2,1)} %lay_out.1.mine_ref), channel_id=1, source_target_pairs={{0,2},{2,0},{1,3},{3,1},{4,6},{6,4},{5,7},{7,5},{8,10},{10,8},{9,1... | collective-permute-start | bytes 14155784 | tf_op jit(solution)/shard_map/ppermute | solution.py:698
  123.5 26.1 %collective-permute-start = (bf16[512,1024]{1,0:T(8,128)(2,1)S(1)}, bf16[512,1024]{1,0:T(8,128)(2,1)S(1)}, u32[]{:S(2)}, u32[]{:S(2)}) collective-permute-start(bf16[512,1024]{1,0:T(8,128)(2,1)S(1)} %copy-done), channel_id=1, source_target_pairs={{0,1},{1,0},{2,3},{3,2},{4,5},{5,4},{6,7},{7,6},{8,9},{9,8},{10,11... | collective-permute-start | bytes 3145736 | tf_op jit(solution)/shard_map/ppermute | solution.py:698
  125.1 110.5 %collective-permute-start.22 = (bf16[512,1024]{1,0:T(8,128)(2,1)S(1)}, bf16[512,1024]{1,0:T(8,128)(2,1)S(1)}, u32[]{:S(2)}, u32[]{:S(2)}) collective-permute-start(bf16[512,1024]{1,0:T(8,128)(2,1)S(1)} %copy-done.7), channel_id=1, source_target_pairs={{0,1},{1,0},{2,3},{3,2},{4,5},{5,4},{6,7},{7,6},{8,9},{9,8},{10,11... | collective-permute-start | bytes 3145736 | tf_op jit(solution)/shard_map/ppermute | solution.py:698
  184.1 27.8 %collective-permute-start.11 = (bf16[512,1024]{1,0:T(8,128)(2,1)}, bf16[512,1024]{1,0:T(8,128)(2,1)S(1)}, u32[]{:S(2)}, u32[]{:S(2)}) collective-permute-start(bf16[512,1024]{1,0:T(8,128)(2,1)} %out_rows.1), channel_id=1, source_target_pairs={{0,1},{1,0},{2,3},{3,2},{4,5},{5,4},{6,7},{7,6},{8,9},{9,8},{10,11... | collective-permute-start | bytes 3145736 | tf_op jit(solution)/shard_map/ppermute | solution.py:698
  217.9 24.0 %collective-permute-start.21 = (bf16[512,1024]{1,0:T(8,128)(2,1)}, bf16[512,1024]{1,0:T(8,128)(2,1)S(1)}, u32[]{:S(2)}, u32[]{:S(2)}) collective-permute-start(bf16[512,1024]{1,0:T(8,128)(2,1)} %get-tuple-element.181.x_ref.normed_s), channel_id=1, source_target_pairs={{0,1},{1,0},{2,3},{3,2},{4,5},{5,4},{6,7},{7,6},{8,9},{9,8},{10,11... | collective-permute-start | bytes 3145736 | tf_op jit(solution)/shard_map/ppermute | solution.py:698
  260.0 23.2 %collective-permute-start.23 = (bf16[512,1024]{1,0:T(8,128)(2,1)}, bf16[512,1024]{1,0:T(8,128)(2,1)S(1)}, u32[]{:S(2)}, u32[]{:S(2)}) collective-permute-start(bf16[512,1024]{1,0:T(8,128)(2,1)} %get-tuple-element.201), channel_id=1, source_target_pairs={{0,1},{1,0},{2,3},{3,2},{4,5},{5,4},{6,7},{7,6},{8,9},{9,8},{10,11... | collective-permute-start | bytes 3145736 | tf_op jit(solution)/shard_map/ppermute | solution.py:698
  270.4 72.1 %collective-permute-start.41 = (bf16[1024,2304]{1,0:T(8,128)(2,1)}, bf16[1024,2304]{1,0:T(8,128)(2,1)}, u32[]{:S(2)}, u32[]{:S(2)}) collective-permute-start(bf16[1024,2304]{1,0:T(8,128)(2,1)} %late_grads.2), channel_id=1, source_target_pairs={{0,2},{2,0},{1,3},{3,1},{4,6},{6,4},{5,7},{7,5},{8,10},{10,8},{9,1... | collective-permute-start | bytes 14155784 | tf_op jit(solution)/shard_map/ppermute | solution.py:698
  289.7 28.3 %collective-permute-start.24 = (bf16[512,1024]{1,0:T(8,128)(2,1)}, bf16[512,1024]{1,0:T(8,128)(2,1)S(1)}, u32[]{:S(2)}, u32[]{:S(2)}) collective-permute-start(bf16[512,1024]{1,0:T(8,128)(2,1)} %get-tuple-element.228.resid_ref.resid_s), channel_id=1, source_target_pairs={{0,1},{1,0},{2,3},{3,2},{4,5},{5,4},{6,7},{7,6},{8,9},{9,8},{10,11... | collective-permute-start | bytes 3145736 | tf_op jit(solution)/shard_map/ppermute | solution.py:698
  342.5 39.4 %collective-permute-start.26 = (bf16[1024,2176]{1,0:T(8,128)(2,1)}, bf16[1024,2176]{1,0:T(8,128)(2,1)}, u32[]{:S(2)}, u32[]{:S(2)}) collective-permute-start(bf16[1024,2176]{1,0:T(8,128)(2,1)} %mix_grads.2), channel_id=1, source_target_pairs={{0,2},{2,0},{1,3},{3,1},{4,6},{6,4},{5,7},{7,5},{8,10},{10,8},{9,1... | collective-permute-start | bytes 13369352 | tf_op jit(solution)/shard_map/ppermute | solution.py:698
  345.4 16.0 %collective-permute-start.42 = (bf16[128,2304]{1,0:T(8,128)(2,1)}, bf16[128,2304]{1,0:T(8,128)(2,1)}, u32[]{:S(2)}, u32[]{:S(2)}) collective-permute-start(bf16[128,2304]{1,0:T(8,128)(2,1)} %get-tuple-element.373), channel_id=1, source_target_pairs={{0,8},{8,16},{16,24},{24,28},{28,20},{20,12},{12,4},{4,0},{1,9},{9... | collective-permute-start | bytes 1769480 | tf_op jit(solution)/shard_map/ppermute | solution.py:819
  346.1 15.8 %collective-permute-start.43 = (bf16[128,2304]{1,0:T(8,128)(2,1)}, bf16[128,2304]{1,0:T(8,128)(2,1)}, u32[]{:S(2)}, u32[]{:S(2)}) collective-permute-start(bf16[128,2304]{1,0:T(8,128)(2,1)} %get-tuple-element.372), channel_id=1, source_target_pairs={{8,0},{16,8},{24,16},{28,24},{20,28},{12,20},{4,12},{0,4},{9,1},{1... | collective-permute-start | bytes 1769480 | tf_op jit(solution)/shard_map/ppermute | solution.py:819
  350.4 68.7 %collective-permute-start.25 = (bf16[512,1024]{1,0:T(8,128)(2,1)}, bf16[512,1024]{1,0:T(8,128)(2,1)S(1)}, u32[]{:S(2)}, u32[]{:S(2)}) collective-permute-start(bf16[512,1024]{1,0:T(8,128)(2,1)} %get-tuple-element.212), channel_id=1, source_target_pairs={{0,1},{1,0},{2,3},{3,2},{4,5},{5,4},{6,7},{7,6},{8,9},{9,8},{10,11... | collective-permute-start | bytes 3145736 | tf_op jit(solution)/shard_map/ppermute | solution.py:698
  365.2 16.7 %collective-permute-start.44 = (bf16[128,2304]{1,0:T(8,128)(2,1)}, bf16[128,2304]{1,0:T(8,128)(2,1)}, u32[]{:S(2)}, u32[]{:S(2)}) collective-permute-start(bf16[128,2304]{1,0:T(8,128)(2,1)} %get-tuple-element.371), channel_id=1, source_target_pairs={{0,8},{8,16},{16,24},{24,28},{28,20},{20,12},{12,4},{4,0},{1,9},{9... | collective-permute-start | bytes 1769480 | tf_op jit(solution)/shard_map/ppermute | solution.py:819
  365.7 16.3 %collective-permute-start.45 = (bf16[128,2304]{1,0:T(8,128)(2,1)}, bf16[128,2304]{1,0:T(8,128)(2,1)}, u32[]{:S(2)}, u32[]{:S(2)}) collective-permute-start(bf16[128,2304]{1,0:T(8,128)(2,1)} %get-tuple-element.370), channel_id=1, source_target_pairs={{8,0},{16,8},{24,16},{28,24},{20,28},{12,20},{4,12},{0,4},{9,1},{1... | collective-permute-start | bytes 1769480 | tf_op jit(solution)/shard_map/ppermute | solution.py:819
  415.7 13.8 %collective-permute-start.46 = (bf16[128,2304]{1,0:T(8,128)(2,1)S(1)}, bf16[128,2304]{1,0:T(8,128)(2,1)S(1)}, u32[]{:S(2)}, u32[]{:S(2)}) collective-permute-start(bf16[128,2304]{1,0:T(8,128)(2,1)S(1)} %get-tuple-element.369), channel_id=1, source_target_pairs={{0,8},{8,16},{16,24},{24,28},{28,20},{20,12},{12,4},{4,0},{1,9},{9... | collective-permute-start | bytes 1769480 | tf_op jit(solution)/shard_map/ppermute | solution.py:819
  416.3 15.8 %collective-permute-start.47 = (bf16[128,2304]{1,0:T(8,128)(2,1)S(1)}, bf16[128,2304]{1,0:T(8,128)(2,1)S(1)}, u32[]{:S(2)}, u32[]{:S(2)}) collective-permute-start(bf16[128,2304]{1,0:T(8,128)(2,1)S(1)} %get-tuple-element.368), channel_id=1, source_target_pairs={{8,0},{16,8},{24,16},{28,24},{20,28},{12,20},{4,12},{0,4},{9,1},{1... | collective-permute-start | bytes 1769480 | tf_op jit(solution)/shard_map/ppermute | solution.py:819
  419.0 14.0 %collective-permute-start.35 = (f32[73,256]{1,0:T(8,128)S(1)}, f32[73,256]{1,0:T(8,128)S(1)}, u32[]{:S(2)}, u32[]{:S(2)}) collective-permute-start(f32[73,256]{1,0:T(8,128)S(1)} %fusion.27), channel_id=1, source_target_pairs={{0,8},{4,12},{8,0},{12,4},{16,24},{20,28},{24,16},{28,20},{1,9},{5... | collective-permute-start | bytes 224264 | tf_op jit(solution)/shard_map/ppermute | solution.py:839
  435.2 32.6 %collective-permute-start.48 = (bf16[128,2304]{1,0:T(8,128)(2,1)S(1)}, bf16[128,2304]{1,0:T(8,128)(2,1)S(1)}, u32[]{:S(2)}, u32[]{:S(2)}) collective-permute-start(bf16[128,2304]{1,0:T(8,128)(2,1)S(1)} %fusion.1), channel_id=1, source_target_pairs={{0,8},{8,16},{16,24},{24,28},{28,20},{20,12},{12,4},{4,0},{1,9},{9... | collective-permute-start | bytes 1769480 | tf_op jit(solution)/shard_map/ppermute | solution.py:825
  438.6 30.9 %collective-permute-start.28 = (bf16[128,2176]{1,0:T(8,128)(2,1)S(1)}, bf16[128,2176]{1,0:T(8,128)(2,1)S(1)}, u32[]{:S(2)}, u32[]{:S(2)}) collective-permute-start(bf16[128,2176]{1,0:T(8,128)(2,1)S(1)} %get-tuple-element.379), channel_id=1, source_target_pairs={{0,8},{8,16},{16,24},{24,28},{28,20},{20,12},{12,4},{4,0},{1,9},{9... | collective-permute-start | bytes 1671176 | tf_op jit(solution)/shard_map/ppermute | solution.py:819
  438.6 30.8 %collective-permute-start.29 = (bf16[128,2176]{1,0:T(8,128)(2,1)S(1)}, bf16[128,2176]{1,0:T(8,128)(2,1)S(1)}, u32[]{:S(2)}, u32[]{:S(2)}) collective-permute-start(bf16[128,2176]{1,0:T(8,128)(2,1)S(1)} %get-tuple-element.378), channel_id=1, source_target_pairs={{8,0},{16,8},{24,16},{28,24},{20,28},{12,20},{4,12},{0,4},{9,1},{1... | collective-permute-start | bytes 1671176 | tf_op jit(solution)/shard_map/ppermute | solution.py:819
  440.7 61.4 %collective-permute-start.27 = (bf16[512,1024]{1,0:T(8,128)(2,1)S(1)}, bf16[512,1024]{1,0:T(8,128)(2,1)S(1)}, u32[]{:S(2)}, u32[]{:S(2)}) collective-permute-start(bf16[512,1024]{1,0:T(8,128)(2,1)S(1)} %copy-done.32), channel_id=1, source_target_pairs={{0,1},{1,0},{2,3},{3,2},{4,5},{5,4},{6,7},{7,6},{8,9},{9,8},{10,11... | collective-permute-start | bytes 3145736 | tf_op jit(solution)/shard_map/ppermute | solution.py:698
  442.8 23.2 %collective-permute-start.38 = (f32[9,256]{1,0:T(8,128)S(1)}, f32[9,256]{1,0:T(8,128)S(1)}, u32[]{:S(2)}, u32[]{:S(2)}) collective-permute-start(f32[9,256]{1,0:T(8,128)S(1)} %slice.206), channel_id=1, source_target_pairs={{0,1},{1,0},{2,3},{3,2},{4,5},{5,4},{6,7},{7,6},{8,9},{9,8},{10,11... | collective-permute-start | bytes 27656 | tf_op jit(solution)/shard_map/ppermute | solution.py:839
  469.8 15.1 %collective-permute-start.30 = (bf16[128,2176]{1,0:T(8,128)(2,1)S(1)}, bf16[128,2176]{1,0:T(8,128)(2,1)S(1)}, u32[]{:S(2)}, u32[]{:S(2)}) collective-permute-start(bf16[128,2176]{1,0:T(8,128)(2,1)S(1)} %get-tuple-element.377), channel_id=1, source_target_pairs={{0,8},{8,16},{16,24},{24,28},{28,20},{20,12},{12,4},{4,0},{1,9},{9... | collective-permute-start | bytes 1671176 | tf_op jit(solution)/shard_map/ppermute | solution.py:819
  470.2 14.7 %collective-permute-start.31 = (bf16[128,2176]{1,0:T(8,128)(2,1)S(1)}, bf16[128,2176]{1,0:T(8,128)(2,1)S(1)}, u32[]{:S(2)}, u32[]{:S(2)}) collective-permute-start(bf16[128,2176]{1,0:T(8,128)(2,1)S(1)} %get-tuple-element.376), channel_id=1, source_target_pairs={{8,0},{16,8},{24,16},{28,24},{20,28},{12,20},{4,12},{0,4},{9,1},{1... | collective-permute-start | bytes 1671176 | tf_op jit(solution)/shard_map/ppermute | solution.py:819
  485.2 14.1 %collective-permute-start.32 = (bf16[128,2176]{1,0:T(8,128)(2,1)S(1)}, bf16[128,2176]{1,0:T(8,128)(2,1)S(1)}, u32[]{:S(2)}, u32[]{:S(2)}) collective-permute-start(bf16[128,2176]{1,0:T(8,128)(2,1)S(1)} %get-tuple-element.375), channel_id=1, source_target_pairs={{0,8},{8,16},{16,24},{24,28},{28,20},{20,12},{12,4},{4,0},{1,9},{9... | collective-permute-start | bytes 1671176 | tf_op jit(solution)/shard_map/ppermute | solution.py:819
  485.7 13.8 %collective-permute-start.33 = (bf16[128,2176]{1,0:T(8,128)(2,1)S(1)}, bf16[128,2176]{1,0:T(8,128)(2,1)S(1)}, u32[]{:S(2)}, u32[]{:S(2)}) collective-permute-start(bf16[128,2176]{1,0:T(8,128)(2,1)S(1)} %get-tuple-element.374), channel_id=1, source_target_pairs={{8,0},{16,8},{24,16},{28,24},{20,28},{12,20},{4,12},{0,4},{9,1},{1... | collective-permute-start | bytes 1671176 | tf_op jit(solution)/shard_map/ppermute | solution.py:819
  (56 other events, 841.1 us)
